TPU v7x, 128 devices: a whole 4x4x4 slice. The times are simulated.
128 devices in a mesh: segment: 8 (over x, z_lo), ctx: 16 (over z_hi, y, core).
Axes of the slice: x: 4, y: 4, z: 4 (z_hi: 2, z_lo: 2; z = z_hi * 2 + z_lo), core: 2. Of those that a mesh axis runs over, the one named last changes fastest.
Arguments:
- queries: bfloat16 [8, 8, 4096, 2048], P('segment', None, 'ctx'), may hold values from -3 to 3
- keys: bfloat16 [8, 8, 4096, 512], P('segment', None, 'ctx'), may hold values from -3 to 3
- values: bfloat16 [8, 8, 4096, 512], P('segment', None, 'ctx'), may hold values from -6 to 6
- grad_slab: bfloat16 [8, 4096, 2048], P('segment', 'ctx'), may hold values from -6 to 6
- plan: int32 [8], P('segment'), may hold values from 0 to 7
- random_blocks: int32 [32, 3], replicated, may hold values from 1 to 31, as said below
Outputs:
- query_grad: bfloat16 [8, 4096, 2048], P('segment', 'ctx')
- key_grad: bfloat16 [8, 4096, 512], P('segment', 'ctx')
- value_grad: bfloat16 [8, 4096, 512], P('segment', 'ctx')
Inputs may be any that keep to these rules, and one draw needn't show every extreme that they name: `random_blocks`: each row b holds 3 different block numbers, none equal to b - 1, b, b + 1 (mod 32) or to 0.
All inputs are finite; a program needn't handle non-finite values.
Results may differ from a plain program's by a relative error of at most 0.012.
Values may be sent and summed in bfloat16 or wider, within the bound.
No kernel may reach another device: no remote copies, remote signals or barrier semaphores. Data moves between devices by JAX's collectives and lax.ppermute only.
A program may use at most 192 MiB of HBM per device.

v0:
```python
import jax
import jax.numpy as jnp
from jax import lax
from jax.sharding import PartitionSpec as P

HD = 128
BLK = 128


def from_behind(block, axis, distance):
    devices = range(lax.axis_size(axis))
    route = [((i - distance) % len(devices), i) for i in devices]
    return lax.ppermute(block, axis, route)


def unchanged(partial_sum):
    return partial_sum


def global_rows(query_rows, grad_rows, key_set, value_set, score_scale, total_fn, delta_fn):
    scores = (
        jnp.einsum("htgd,hsd->hgts", query_rows, key_set, preferred_element_type=jnp.float32)
        * score_scale
    )
    exp_scores = jnp.exp(scores)
    totals = total_fn(jnp.sum(exp_scores, axis=3))
    weights = exp_scores / totals[..., None]
    weights_low = weights.astype(jnp.bfloat16)
    dprobs = jnp.einsum("htgd,hsd->hgts", grad_rows, value_set, preferred_element_type=jnp.float32)
    deltas = delta_fn(jnp.sum(weights_low.astype(jnp.float32) * dprobs, axis=3))
    dscore = (weights * (dprobs - deltas[..., None])).astype(jnp.bfloat16)
    dquery = score_scale * jnp.einsum(
        "hgts,hsd->htgd", dscore, key_set, preferred_element_type=jnp.float32
    )
    key_term = score_scale * jnp.einsum(
        "hgts,htgd->hsd", dscore, query_rows, preferred_element_type=jnp.float32
    )
    value_term = jnp.einsum(
        "hgts,htgd->hsd", weights_low, grad_rows, preferred_element_type=jnp.float32
    )
    return (dquery, key_term, value_term)


def per_device(queries, keys, values, grad_slab, plan, random_blocks):
    upstream = from_behind(grad_slab, "segment", -1)[0]
    chosen_mb = plan[0]
    query_now = lax.dynamic_index_in_dim(queries[0], chosen_mb, 0, keepdims=False)
    key_now = lax.dynamic_index_in_dim(keys[0], chosen_mb, 0, keepdims=False)
    value_now = lax.dynamic_index_in_dim(values[0], chosen_mb, 0, keepdims=False)
    tok_rows = query_now.shape[0]
    q_width = query_now.shape[1]
    kv_width = key_now.shape[1]
    kv_heads = kv_width // HD
    group_size = q_width // HD // kv_heads
    n_local = tok_rows // BLK
    n_blocks = n_local * lax.axis_size("ctx")
    score_scale = HD ** (-0.5)
    key_all, value_all = (
        lax.all_gather(key_now, "ctx", axis=0, tiled=True),
        lax.all_gather(value_now, "ctx", axis=0, tiled=True),
    )
    first_block = lax.axis_index("ctx") * n_local
    my_blocks = first_block + jnp.arange(n_local, dtype=jnp.int32)
    global_id = jnp.int32(0)
    rand_rows = lax.dynamic_slice_in_dim(random_blocks, first_block, n_local, 0)
    window_ids = jnp.stack(
        [(my_blocks - 1) % n_blocks, my_blocks, (my_blocks + 1) % n_blocks], axis=1
    )
    in_window = jnp.any(window_ids == global_id, axis=1)
    slot_ids = jnp.concatenate([window_ids, jnp.zeros((n_local, 1), jnp.int32), rand_rows], axis=1)
    n_slots = slot_ids.shape[1]
    valid_slots = jnp.concatenate(
        [
            jnp.ones((n_local, 3), jnp.float32),
            (1.0 - in_window.astype(jnp.float32))[:, None],
            jnp.ones((n_local, n_slots - 4), jnp.float32),
        ],
        axis=1,
    )
    plain_row = (my_blocks != global_id).astype(jnp.float32).reshape(n_local, 1, 1, 1, 1, 1)
    query_five = query_now.reshape(n_local, BLK, kv_heads, group_size, HD)
    grad_five = upstream.reshape(n_local, BLK, kv_heads, group_size, HD)
    key_blocks = key_all.reshape(n_blocks, BLK, kv_heads, HD)[slot_ids]
    value_blocks = value_all.reshape(n_blocks, BLK, kv_heads, HD)[slot_ids]
    scores = (
        jnp.einsum(
            "ntkgd,neskd->nkgtes", query_five, key_blocks, preferred_element_type=jnp.float32
        )
        * score_scale
    )
    exp_scores = jnp.exp(scores) * valid_slots.reshape(n_local, 1, 1, 1, n_slots, 1)
    totals = jnp.sum(exp_scores, axis=(4, 5))
    weights = exp_scores / totals[..., None, None]
    weights_low = weights.astype(jnp.bfloat16)
    dprobs = jnp.einsum(
        "ntkgd,neskd->nkgtes", grad_five, value_blocks, preferred_element_type=jnp.float32
    )
    deltas = jnp.sum(weights_low.astype(jnp.float32) * dprobs, axis=(4, 5))
    dscore = (weights * (dprobs - deltas[..., None, None]) * plain_row).astype(jnp.bfloat16)
    weights_row = weights_low * plain_row.astype(jnp.bfloat16)
    dquery = score_scale * jnp.einsum(
        "nkgtes,neskd->ntkgd", dscore, key_blocks, preferred_element_type=jnp.float32
    )
    key_term = score_scale * jnp.einsum(
        "nkgtes,ntkgd->neskd", dscore, query_five, preferred_element_type=jnp.float32
    )
    value_term = jnp.einsum(
        "nkgtes,ntkgd->neskd", weights_row, grad_five, preferred_element_type=jnp.float32
    )
    slot_terms = jnp.concatenate(
        [
            key_term.reshape(n_local * n_slots, BLK, kv_width),
            value_term.reshape(n_local * n_slots, BLK, kv_width),
        ],
        axis=2,
    )
    grad_buffer = (
        jnp.zeros((n_blocks, BLK, 2 * kv_width), jnp.float32)
        .at[slot_ids.reshape(-1)]
        .add(slot_terms)
    )
    local_index = global_id - first_block
    owns_row = (local_index >= 0) & (local_index < n_local)
    clipped = jnp.clip(local_index, 0, n_local - 1)
    row_query = lax.dynamic_slice_in_dim(query_now, clipped * BLK, BLK, 0)
    row_grad = lax.dynamic_slice_in_dim(upstream, clipped * BLK, BLK, 0)

    def whole_row(operands):
        head_query = operands[0].reshape(BLK, kv_heads, group_size, HD).transpose(1, 0, 2, 3)
        head_grad = operands[1].reshape(BLK, kv_heads, group_size, HD).transpose(1, 0, 2, 3)
        keys_heads = key_all.reshape(n_blocks * BLK, kv_heads, HD).transpose(1, 0, 2)
        values_heads = value_all.reshape(n_blocks * BLK, kv_heads, HD).transpose(1, 0, 2)

        def per_head(items):
            outputs = global_rows(
                items[0][None],
                items[1][None],
                items[2][None],
                items[3][None],
                score_scale,
                unchanged,
                unchanged,
            )
            return (outputs[0][0], outputs[1][0], outputs[2][0])

        row_dq, row_dk, row_dv = lax.map(
            per_head, (head_query, head_grad, keys_heads, values_heads)
        )
        row_dq = row_dq.transpose(1, 0, 2, 3).reshape(BLK, q_width)
        row_kv = jnp.concatenate(
            [
                row_dk.transpose(1, 0, 2).reshape(n_blocks * BLK, kv_width),
                row_dv.transpose(1, 0, 2).reshape(n_blocks * BLK, kv_width),
            ],
            axis=1,
        )
        return (row_dq, row_kv)

    def no_row(operands):
        return (
            jnp.zeros((BLK, q_width), jnp.float32),
            jnp.zeros((n_blocks * BLK, 2 * kv_width), jnp.float32),
        )

    row_dq, row_kv = lax.cond(owns_row, whole_row, no_row, (row_query, row_grad))
    grad_buffer = grad_buffer + row_kv.reshape(n_blocks, BLK, 2 * kv_width)
    query_flat = dquery.reshape(tok_rows, q_width)
    current_rows = lax.dynamic_slice_in_dim(query_flat, clipped * BLK, BLK, 0)
    query_flat = lax.dynamic_update_slice_in_dim(
        query_flat, current_rows + row_dq * owns_row.astype(jnp.float32), clipped * BLK, 0
    )
    flat_buffer = grad_buffer.reshape(n_blocks * BLK, 2 * kv_width)
    kv_summed = lax.psum_scatter(flat_buffer, "ctx", scatter_dimension=0, tiled=True)
    query_out = query_flat.astype(jnp.bfloat16)[None]
    key_out = kv_summed[:, :kv_width].astype(jnp.bfloat16)[None]
    value_out = kv_summed[:, kv_width:].astype(jnp.bfloat16)[None]
    return (query_out, key_out, value_out)


def solution(mesh):
    return jax.shard_map(
        per_device,
        mesh=mesh,
        in_specs=(
            P("segment", None, "ctx", None),
            P("segment", None, "ctx", None),
            P("segment", None, "ctx", None),
            P("segment", "ctx", None),
            P("segment"),
            P(),
        ),
        out_specs=(P("segment", "ctx", None), P("segment", "ctx", None), P("segment", "ctx", None)),
        check_vma=False,
    )
```

profile of v0, /device:TPU:0, one launch (start us, length us, event | category | flops | bytes accessed | tf_op | source)
XLA Modules:
  0.0 531.3 jit_solution(9461408023295520977)
XLA Ops:
  9.7 1.0 constant_dynamic-slice_fusion.5
  11.6 2.3 copy.112
  13.9 4.2 collective-permute-start
  19.8 1.3 constant_dynamic-slice_fusion.3
  21.9 1.0 copy.138
  23.6 18.5 %collective-permute-done = bf16[1,256,2048]{1,2,0:T(8,128)(2,1)S(1)} collective-permute-done((bf16[1,256,2048]{1,2,0:T(8,128)(2,1)}, bf16[1,256,2048]{1,2,0:T(8,128)(2,1)S(1)}, u32[]{:S(2)}, u32[]{:S(2)}) %collective-permute-start) | collective-permute-done | bytes 1048608 | tf_op jit(solution)/shard_map/ppermute | solution.py:13
  42.3 43.7 %all-gather.7.cloned.1.call-done = bf16[1,1,4096,512]{2,3,1,0:T(8,128)(2,1)} async-done(((bf16[1,1,256,512]{2,3,1,0:T(8,128)(2,1)}), bf16[1,1,4096,512]{2,3,1,0:T(8,128)(2,1)}) %all-gather.7.cloned.1.call-update) | async-done | bytes 4194320 | tf_op jit(solution)/shard_map/all_gather | solution.py:60
  86.0 5.4 %copy.172 = bf16[64,8,32,128]{3,2,1,0:T(8,128)(2,1)} copy(bf16[64,8,32,128]{3,1,2,0:T(8,128)(2,1)} %bitcast.267) | data formatting | bytes 8388608
  91.5 7.5 %copy.111 = bf16[32,128,4,128]{3,1,2,0:T(8,128)(2,1)} copy(bf16[32,128,4,128]{1,0,3,2:T(8,128)(2,1)} %bitcast.258) | data formatting | bytes 8388608 | tf_op jit(solution)/shard_map/reshape | solution.py:84
  99.0 47.6 %all-gather.5.cloned.1.call-done = bf16[1,1,4096,512]{2,3,1,0:T(8,128)(2,1)} async-done(((bf16[1,1,256,512]{2,3,1,0:T(8,128)(2,1)}), bf16[1,1,4096,512]{2,3,1,0:T(8,128)(2,1)}) %all-gather.5.cloned.1.call-update) | async-done | bytes 4194320 | tf_op jit(solution)/shard_map/all_gather | solution.py:59
  146.6 5.4 %copy.171 = bf16[64,8,32,128]{3,2,1,0:T(8,128)(2,1)} copy(bf16[64,8,32,128]{3,1,2,0:T(8,128)(2,1)} %bitcast.255) | data formatting | bytes 8388608
  152.0 7.6 %copy.106 = bf16[32,128,4,128]{3,1,2,0:T(8,128)(2,1)} copy(bf16[32,128,4,128]{1,0,3,2:T(8,128)(2,1)} %bitcast.259) | data formatting | bytes 8388608 | tf_op jit(solution)/shard_map/reshape | solution.py:83
  159.6 4.3 gather_fusion.1
  163.8 4.2 gather_fusion
  168.0 8.1 %bitcast_reduce_fusion.1 = (f32[2,4,4,128]{3,2,1,0:T(4,128)S(1)}, f32[2,4,7,128,128,4]{4,3,5,2,1,0:T(8,128)}) fusion(f32[2,7]{1,0:T(2,128)S(1)} %pad_maximum_fusion.2, bf16[2,128,4,4,128,1]{1,4,3,5,2,0:T(8,128)(2,1)S(1)} %copy.138, bf16[2,7,128,4,128,1]{4,2,3,1,0,5:T(8,128)(2,1)} %bitcast.262), kind=kOutput, calls=%fused_computation.55 | convolution fusion | flops 950530048 | bytes 17580088 | tf_op jit(solution)/shard_map/ntkgd,neskd->nkgtes/dot_general | solution.py:86
  176.1 9.0 %fusion.47 = f32[2,7,128,4,128]{2,4,1,3,0:T(8,128)} fusion(bf16[2]{0:T(256)(128)(2,1)S(1)} %fusion.65, bf16[2,128,4,4,128,1]{1,0,4,3,2,5:T(2,128)(2,1)S(1)} %bitcast.272, f32[2,4,7,128,128,4]{4,3,5,2,1,0:T(8,128)} %get-tuple-element.178, f32[2,4,4,128]{3,2,1,0:T(4,128)S(1)} %get-tuple-element.177, f32[2,7]{1,0:T(2,128)S(1)} %pad_maximum_fusion.2), kind=kOutput, calls=%fused_computation.68 | convolution fusion | flops 957874176 | bytes 19415100 | tf_op jit(solution)/shard_map/nkgtes,ntkgd->neskd/dot_general | solution.py:107
  185.1 2.3 copy.127
  187.4 12.9 %fusion.35 = (f32[2,4,4,128]{3,2,1,0:T(4,128)S(1)}, f32[2,4,7,128,128,4]{4,3,5,2,1,0:T(8,128)}) fusion(f32[2,4,4,128]{3,2,1,0:T(4,128)S(1)} %get-tuple-element.177, f32[2,7]{1,0:T(2,128)S(1)} %pad_maximum_fusion.2, f32[2,4,7,128,128,4]{4,3,5,2,1,0:T(8,128)} %get-tuple-element.178, bf16[2,128,4,4,128,1]{1,0,4,3,2,5:T(2,128)(2,1)S(1)} %bitcast.273, ...), kind=kOutput, calls=%fused_computation.50 | convolution fusion | flops 965210112 | bytes 32276536 | tf_op jit(solution)/shard_map/ntkgd,neskd->nkgtes/dot_general | solution.py:95
  200.3 1.6 slice-done.2
  202.5 10.5 %fusion.38 = bf16[2,4,4,128,7,128]{3,5,2,4,1,0:T(8,128)(2,1)} fusion(f32[2,4,7,128,128,4]{4,3,5,2,1,0:T(8,128)} %get-tuple-element.180, f32[2]{0:T(128)S(1)} %compare_convert_fusion, f32[2,4,4,128]{3,2,1,0:T(4,128)S(1)} %get-tuple-element.179, f32[2,4,4,128]{3,2,1,0:T(4,128)S(1)} %get-tuple-element.177, f32[2,7]{1,0:T(2,128)S(1)} %pad_maximum_fusion.2, ...), kind=kLoop, calls=%fused_computation.53 | loop fusion | flops 25690112 | bytes 36732992 | tf_op jit(solution)/shard_map/convert_element_type | solution.py:99
  212.9 5.5 %fusion.43 = f32[2,7,128,4,128]{2,4,1,3,0:T(8,128)S(1)} fusion(bf16[2,128,4,4,128,1]{1,4,3,5,2,0:T(8,128)(2,1)S(1)} %copy.138, bf16[2,4,4,128,7,128]{3,5,2,4,1,0:T(8,128)(2,1)} %fusion.38), kind=kOutput, calls=%fused_computation.63 | convolution fusion | flops 940441600 | bytes 12058624 | tf_op jit(solution)/shard_map/nkgtes,ntkgd->neskd/dot_general | solution.py:104
  218.8 3.5 pad_maximum_fusion.1
  222.3 8.4 %copy.128 = f32[14,128,1024]{2,1,0:T(8,128)} copy(f32[14,128,1024]{1,2,0:T(8,128)} %pad_maximum_fusion.1) | data formatting | bytes 14680064 | tf_op jit(solution)/shard_map/concatenate | solution.py:110
  230.7 131.0 %conditional.1 = (f32[32,128,1024]{2,1,0:T(8,128)}, f32[128,2048]{1,0:T(8,128)S(1)}) conditional(s32[]{:T(128)} %convert_element_type.63, () %tuple.25, (s32[]{:T(128)}, s32[]{:T(128)}, bf16[1,8,256,2048]{3,2,1,0:T(8,128)(2,1)}, bf16[1,256,2048]{1,2,0:T(8,128)(2,1)S(1)}, bf16[4096,512]{0,1:T(8,128)(2,1)}, /*index=5*/bf16[4096,512]{0,1:T(8,128)(2,1)}) %tuple.69), branch_computations={%region_3.4_spmd, %region_4.9_spmd} | conditional | flops 2722692096 | bytes 192693488 | solution.py:165
  230.9 11.7 %copy.119 = bf16[1,8,256,2048]{2,3,1,0:T(8,128)(2,1)} copy(bf16[1,8,256,2048]{3,2,1,0:T(8,128)(2,1)} %get-tuple-element.150) | data formatting | bytes 16777216 | tf_op jit(solution)/shard_map
  242.6 1.4 constant_dynamic-slice_fusion.1
  244.0 61.1 %while.18 = (s32[]{:T(128)}, f32[4,128,4,128]{1,3,2,0:T(8,128)S(1)}, f32[4,4096,128]{2,1,0:T(8,128)}, f32[4,4096,128]{2,1,0:T(8,128)}, bf16[4,4096,128]{1,2,0:T(...) while((s32[]{:T(128)}, ...), condition=%wide.region_8.8_spmd, body=%wide.region_5.7_spmd.sunk | while | flops 2718497792 | bytes 71058528 | solution.py:146
  244.0 2.6 bitcast_reduce_fusion.3
  246.7 2.8 fusion.95
  249.5 3.3 fusion.91
  252.8 2.0 fusion.92
  254.8 2.0 fusion.93
  256.8 2.6 fusion.94
  259.4 2.6 bitcast_reduce_fusion.3
  262.0 2.8 fusion.95
  264.8 3.3 fusion.91
  268.1 2.0 fusion.92
  270.1 2.0 fusion.93
  272.1 2.6 fusion.94
  274.6 2.6 bitcast_reduce_fusion.3
  277.3 2.8 fusion.95
  280.1 3.3 fusion.91
  283.3 2.0 fusion.92
  285.3 2.0 fusion.93
  287.3 2.6 fusion.94
  289.9 2.6 bitcast_reduce_fusion.3
  292.5 2.8 fusion.95
  295.3 3.3 fusion.91
  298.6 2.0 fusion.92
  300.6 2.0 fusion.93
  302.6 2.6 fusion.94
  305.2 11.8 %copy.100 = f32[4096,4,128]{2,1,0:T(4,128)} copy(f32[4096,4,128]{2,0,1:T(8,128)} %bitcast.264) | data formatting | bytes 16777216 | tf_op jit(solution)/shard_map/cond/branch_1_fun/transpose | solution.py:153
  317.0 10.3 %concatenate.39 = f32[32,128,512]{2,1,0:T(8,128)} reshape(f32[4096,4,128]{2,1,0:T(4,128)} %copy.100) | data formatting | bytes 16777216 | tf_op jit(solution)/shard_map/cond/branch_1_fun/concatenate | solution.py:150
  327.6 12.1 %copy.99 = f32[4096,4,128]{2,1,0:T(4,128)} copy(f32[4096,4,128]{2,0,1:T(8,128)} %bitcast.265) | data formatting | bytes 16777216 | tf_op jit(solution)/shard_map/cond/branch_1_fun/transpose | solution.py:152
  339.6 10.3 %concatenate.38 = f32[32,128,512]{2,1,0:T(8,128)} reshape(f32[4096,4,128]{2,1,0:T(4,128)} %copy.99) | data formatting | bytes 16777216 | tf_op jit(solution)/shard_map/cond/branch_1_fun/concatenate | solution.py:150
  349.9 11.7 %pad_maximum_fusion = f32[32,128,1024]{2,1,0:T(8,128)} fusion(f32[32,128,512]{2,1,0:T(8,128)} %concatenate.39, f32[32,128,512]{2,1,0:T(8,128)} %concatenate.38), kind=kLoop, calls=%fused_computation.45 | loop fusion | flops 4194304 | bytes 33554432 | tf_op jit(solution)/shard_map/cond/branch_1_fun/concatenate | solution.py:150
  361.7 17.4 %scatter_fusion = f32[32,128,1024]{2,1,0:T(8,128)} fusion(f32[32,128,1024]{2,1,0:T(8,128)} %get-tuple-element.111, s32[14]{0:T(128)S(1)} %copy-done.4, f32[14,128,1024]{2,1,0:T(8,128)} %copy.128), kind=kCustom, calls=%fused_computation.2 | custom fusion | flops 1835008 | bytes 22020152 | tf_op jit(solution)/shard_map/scatter-add | solution.py:120
  379.1 6.5 %fusion.46 = f32[2,128,4,4,128]{1,4,3,2,0:T(8,128)} fusion(bf16[2,4,4,128,7,128]{3,5,2,4,1,0:T(8,128)(2,1)} %fusion.38, bf16[2,7,128,4,128,1]{4,2,3,1,0,5:T(8,128)(2,1)} %bitcast.263), kind=kOutput, calls=%fused_computation.67 | convolution fusion | flops 940048384 | bytes 11272192 | tf_op jit(solution)/shard_map/nkgtes,neskd->ntkgd/dot_general | solution.py:101
  385.6 3.4 copy.118
  389.1 3.4 reshape.396
  392.4 2.5 add_dynamic-update-slice_fusion
  395.0 3.1 convert_bitcast_fusion
  398.0 124.6 %reduce-scatter.2.cloned.1.call-done = f32[256,1024]{1,0:T(8,128)} async-done(((f32[4096,1024]{1,0:T(8,128)}), f32[256,1024]{1,0:T(8,128)}) %reduce-scatter.2.cloned.1.call-update) | async-done | bytes 1048592 | tf_op jit(solution)/shard_map/reduce_scatter | solution.py:173
  522.6 1.3 convert.4
  (62 shorter events, 8.5 us)
Async XLA Ops:
  7.2 1.6 copy-start
  7.2 78.9 %all-gather.7.cloned.1.call-start = ((), (), s32[]{:S(2)}) async-start(), calls=%async_computation.3 | async-start | bytes 4456448 | tf_op jit(solution)/shard_map/all_gather | solution.py:60
  9.7 136.9 %all-gather.5.cloned.1.call-start = ((), (), s32[]{:S(2)}) async-start(), calls=%async_computation.2 | async-start | bytes 4456448 | tf_op jit(solution)/shard_map/all_gather | solution.py:59
  11.6 511.0 %reduce-scatter.2.cloned.1.call-start = ((), (), s32[]{:S(2)}) async-start(), calls=%async_computation.1 | async-start | bytes 17825792 | tf_op jit(solution)/shard_map/reduce_scatter | solution.py:173
  13.9 28.2 %collective-permute-start = (bf16[1,256,2048]{1,2,0:T(8,128)(2,1)}, bf16[1,256,2048]{1,2,0:T(8,128)(2,1)S(1)}, u32[]{:S(2)}, u32[]{:S(2)}) collective-permute-start(bf16[1,256,2048]{1,2,0:T(8,128)(2,1)} %copy.112), channel_id=1, source_target_pairs={{16,0},{32,16},{48,32},{64,48},{80,64},{96,80},{112,96},{0,112},{1... | collective-permute-start | bytes 3145736 | tf_op jit(solution)/shard_map/ppermute | solution.py:13
  187.4 12.9 %slice-start = ((s8[14680064]{0:T(1024)(128)(4,1)}), s8[4194304]{0:T(1024)(128)(4,1)S(1)}, s32[]{:S(2)}) async-start(s8[14680064]{0:T(1024)(128)(4,1)} %bitcast.253), calls=%async_computation.4 | async-start | bytes 8388608
  187.4 12.9 %slice-start.1 = ((s8[14680064]{0:T(1024)(128)(4,1)}), s8[4194304]{0:T(1024)(128)(4,1)S(1)}, s32[]{:S(2)}) async-start(s8[14680064]{0:T(1024)(128)(4,1)} %bitcast.253), calls=%async_computation.5 | async-start | bytes 8388608
  187.4 14.5 %slice-start.2 = ((s8[14680064]{0:T(1024)(128)(4,1)}), s8[4194304]{0:T(1024)(128)(4,1)S(1)}, s32[]{:S(2)}) async-start(s8[14680064]{0:T(1024)(128)(4,1)} %bitcast.253), calls=%async_computation.6 | async-start | bytes 8388608
  187.4 15.1 %slice-start.3 = ((s8[14680064]{0:T(1024)(128)(4,1)}), s8[2097152]{0:T(1024)(128)(4,1)S(1)}, s32[]{:S(2)}) async-start(s8[14680064]{0:T(1024)(128)(4,1)} %bitcast.253), calls=%async_computation.7 | async-start | bytes 4194304
  230.7 131.0 %copy-start.4 = (s32[14]{0:T(128)S(1)}, s32[14]{0:T(128)}, u32[]{:S(2)}) copy-start(s32[14]{0:T(128)} %fusion.64) | copy-start | bytes 172
  361.7 17.4 %copy-start.2 = (f32[128,2048]{1,0:T(8,128)}, f32[128,2048]{1,0:T(8,128)S(1)}, u32[]{:S(2)}) copy-start(f32[128,2048]{1,0:T(8,128)S(1)} %get-tuple-element.154) | copy-start | bytes 3145732
  379.1 13.3 %copy-start.3 = (f32[128,2048]{1,0:T(8,128)S(1)}, f32[128,2048]{1,0:T(8,128)}, u32[]{:S(2)}) copy-start(f32[128,2048]{1,0:T(8,128)} %copy-done.2) | copy-start | bytes 3145732
  379.1 145.6 %copy-start.1 = (bf16[1,8,256,512]{3,2,1,0:T(8,128)(2,1)S(1)}, bf16[1,8,256,512]{3,2,1,0:T(8,128)(2,1)}, u32[]{:S(2)}) copy-start(bf16[1,8,256,512]{3,2,1,0:T(8,128)(2,1)} %param.12) | copy-start | bytes 6291460
Sparse Core Ops, SparseCore 0:
  10.9 75.1 all-gather.6
  88.9 57.6 all-gather.4
  379.2 143.3 reduce-scatter.1
where the time goes:
time: 534 us; the launch traced here: 531 us
  waiting for transfers between devices  234 us (44%)
  local copies, waits for them, and re-layouts  124 us (23%)
  matrix products  95 us (18%)
  other arithmetic  58.6 us (11%)
  between operations  14.7 us (3%)
    reduce_scatter x1, waiting for transfers between devices, per_device(): lax.psum_scatter(flat_buffer, 'ctx', scatter_dimension=0, tiled=True)  125 us
    all_gather x1, waiting for transfers between devices, per_device(): lax.all_gather(key_now, 'ctx', axis=0, tiled=True)  47.6 us
    all_gather x1, waiting for transfers between devices, per_device(): lax.all_gather(value_now, 'ctx', axis=0, tiled=True)  43.7 us
    concatenate x2, local copies, waits for them, and re-layouts, whole_row(): jnp.concatenate([row_dk.transpose(1, 0, 2).reshape(n_blocks * BLK, kv_wid...  20.6 us
    ppermute x1, waiting for transfers between devices, from_behind(): return lax.ppermute(block, axis, route)  18.5 us
    unnamed x23, local copies, waits for them, and re-layouts  17.8 us
    scatter-add x1, other arithmetic, per_device(): grad_buffer = jnp.zeros((n_blocks, BLK, 2 * kv_width), jnp.float32).at[sl...  17.4 us
    dot_general x4, matrix products, global_rows(): jnp.einsum('htgd,hsd->hgts', grad_rows, value_set, preferred_element_type...  13.1 us
  transfers between devices with their start and end apart: 4, of which 4 were waited for; matrix products, arithmetic and copies ran while one was open for 8% of the time, Pallas kernels for 0%

commit v1 on v0

v1 whole, which is shorter than its diff:
```python
import functools
import math

import jax
import jax.numpy as jnp
from jax import lax
from jax.experimental import pallas as pl
from jax.experimental.pallas import tpu as pltpu
from jax.sharding import PartitionSpec as P

HD = 128
BLK = 128
NH = 4
SCALE = HD**-0.5
EXP2_SCALE = SCALE * math.log2(math.e)
F32 = jnp.float32
BF16 = jnp.bfloat16
NT = (((1,), (1,)), ((), ()))
TN = (((0,), (0,)), ((), ()))
MIB = 2**20


def dot(a, b, dims=(((1,), (0,)), ((), ()))):
    return lax.dot_general(a, b, dims, preferred_element_type=F32)


def params(mib=8):
    return pltpu.CompilerParams(vmem_limit_bytes=mib * MIB)


def on_chip(kernel, name, out_shape, *operands, scratch=(), mib=8):
    vmem = pl.BlockSpec(memory_space=pltpu.VMEM)
    return pl.pallas_call(
        kernel,
        in_specs=[pl.BlockSpec(memory_space=pltpu.SMEM)] + [vmem] * (len(operands) - 1),
        out_specs=[vmem] * len(out_shape),
        out_shape=out_shape,
        scratch_shapes=list(scratch),
        compiler_params=params(mib),
        name=name,
    )(*operands)


def shape(dims, dtype):
    return jax.ShapeDtypeStruct(dims, dtype)


def stored(dims, dtype):
    return pltpu.HBM(dims, dtype)


def after(x, *others):
    return lax.optimization_barrier((x, *others))[0]


def pack_kernel(
    info_ref, k_ref, v_ref, q_ref, g_ref,
    kv_ref, send_ref, edge_ref, q0_ref, q1_ref, g0_ref, g1_ref,
):
    edge = pl.ds(pl.multiple_of(info_ref[1] % 2 * BLK, BLK), BLK)
    for i, ref in enumerate((k_ref, v_ref)):
        kv_ref[i] = ref[0]
        edge_ref[i] = ref[0, edge, :]
        for b in range(2):
            for j in range(8):
                piece = ref[0, b * BLK + j * 16 : b * BLK + (j + 1) * 16, :]
                send_ref[j, i, b] = piece
                send_ref[j + 8, i, b] = piece
    half = q0_ref.shape[1]
    q0_ref[...] = q_ref[0, :, :half]
    q1_ref[...] = q_ref[0, :, half:]
    g0_ref[...] = g_ref[:, :half]
    g1_ref[...] = g_ref[:, half:]


def pack(info, keys, values, queries, grad):
    width, q_width = keys.shape[2], queries.shape[2]
    spec = pl.BlockSpec((1, 2 * BLK, width), lambda i, info: (info[0], 0, 0))
    half = pl.BlockSpec((BLK, q_width // 2), lambda i, info: (0, 0))
    inputs = [pltpu.with_memory_space_constraint(a, pltpu.HBM) for a in (keys, values, queries, grad)]
    return pl.pallas_call(
        pack_kernel,
        grid_spec=pltpu.PrefetchScalarGridSpec(
            num_scalar_prefetch=1,
            grid=(1,),
            in_specs=[
                spec,
                spec,
                pl.BlockSpec((1, BLK, q_width), lambda i, info: (info[0], 0, 0)),
                pl.BlockSpec((BLK, q_width), lambda i, info: (0, 0)),
            ],
            out_specs=[
                pl.BlockSpec((2, 2 * BLK, width), lambda i, info: (0, 0, 0)),
                pl.BlockSpec((16, 2, 2, 16, width), lambda i, info: (0, 0, 0, 0, 0)),
                pl.BlockSpec((2, BLK, width), lambda i, info: (0, 0, 0)),
                *[half] * 4,
            ],
        ),
        out_shape=[
            stored((2, 2 * BLK, width), BF16),
            stored((16, 2, 2, 16, width), BF16),
            stored((2, BLK, width), BF16),
            *[stored((BLK, q_width // 2), BF16)] * 4,
        ],
        compiler_params=params(16),
        name="pack",
    )(info, *inputs)


def select_kernel(table_ref, got_ref, send_ref):
    for d in range(8):
        for s in range(7):
            block = table_ref[d * 7 + s]
            owner, which = block // 2, block % 2
            for i in range(2):
                send_ref[d, i, s] = got_ref[owner, i, which]


def combine_kernel(table_ref, got_ref, row_ref, send_ref, acc_ref):
    acc_ref[...] = jnp.zeros_like(acc_ref)
    acc_ref[:, :, :, :, columns(table_ref[56], 2 * HD)] = row_ref[...]
    for d in range(8):
        for s in range(7):
            block = table_ref[d * 7 + s]
            owner, which = block // 2, block % 2
            for i in range(2):
                acc_ref[owner, i, which] += got_ref[d, i, s].astype(F32)
    send_ref[...] = acc_ref[...].astype(BF16)


def heads_to_rows(cols):
    return jnp.concatenate([cols[:, h * HD : (h + 1) * HD] for h in range(NH)], axis=0)


def columns(g, width):
    return pl.ds(pl.multiple_of(g * width, width), width)


def attend_kernel(
    info_ref, q_ref, do_ref, own_ref, part_ref, nb_ref, rv_ref,
    dq_ref, down_ref, winp_ref, winn_ref, send_ref, wk_ref, zero_ref,
):
    rank = info_ref[1]
    even = rank % 2 == 0

    @pl.when(even)
    def _():
        wk_ref[0] = nb_ref[...]
        wk_ref[1] = part_ref[:, :BLK, :]

    @pl.when(jnp.logical_not(even))
    def _():
        wk_ref[0] = part_ref[:, BLK:, :]
        wk_ref[1] = nb_ref[...]

    def attend(n):
        rows = slice(n * BLK, (n + 1) * BLK)
        q, do = heads_to_rows(q_ref[0, rows, :]), heads_to_rows(do_ref[rows, :])

        def blocks(i):
            parts = [own_ref[i], wk_ref[n, i], rv_ref[:, i, 0].reshape(BLK, HD)]
            parts += [rv_ref[:, i, 1 + 3 * n + j].reshape(BLK, HD) for j in range(3)]
            return jnp.concatenate(parts, axis=0)

        k, v = blocks(0), blocks(1)
        e = jnp.exp2(dot(k, q, NT) * EXP2_SCALE)
        if n == 1:
            twice = jnp.logical_or(rank == 0, rank == 15)
            keep = jnp.where(twice, 0.0, 1.0).astype(F32)
            e = jnp.concatenate([e[: 3 * BLK], e[3 * BLK : 4 * BLK] * keep, e[4 * BLK :]], axis=0)
        p = e * (1.0 / jnp.sum(e, axis=0, keepdims=True))
        pb = p.astype(BF16)
        dp = dot(v, do, NT)
        delta = jnp.sum(p * dp, axis=0, keepdims=True)
        ds = (p * (dp - delta)).astype(BF16)
        dqt = dot(k, ds, TN) * SCALE
        dq_ref[rows, :] = jnp.concatenate(
            [dqt[:, h * HD : (h + 1) * HD].T for h in range(NH)], axis=1
        ).astype(BF16)
        return dot(ds, q) * SCALE, dot(pb, do)

    def emit(n, grads):
        for i, grad in enumerate(grads):
            if n == 0:
                down_ref[i] = grad[: 2 * BLK]
                zero_ref[i] = grad[3 * BLK : 4 * BLK]
            else:
                down_ref[i] += grad[: 2 * BLK]
                total = zero_ref[i] + grad[3 * BLK : 4 * BLK]
                send_ref[:, i, 0] = total.astype(BF16).reshape(8, 16, HD)
            wk_ref[n, i] = grad[2 * BLK : 3 * BLK].astype(BF16)
            for j in range(3):
                got = grad[(4 + j) * BLK : (5 + j) * BLK].astype(BF16)
                send_ref[:, i, 1 + 3 * n + j] = got.reshape(8, 16, HD)

    @pl.when(rank != 0)
    def _():
        emit(0, attend(0))

    @pl.when(rank == 0)
    def _():
        dq_ref[:BLK, :] = jnp.zeros((BLK, NH * HD), BF16)
        emit(0, [jnp.zeros((7 * BLK, HD), F32)] * 2)

    emit(1, attend(1))

    @pl.when(even)
    def _():
        winn_ref[...] = wk_ref[0]
        winp_ref[...] = wk_ref[1]

    @pl.when(jnp.logical_not(even))
    def _():
        winp_ref[...] = wk_ref[0]
        winn_ref[...] = wk_ref[1]


def attend(info, queries, upstream, own, partner, neighbour, got):
    q_width, width = queries.shape[2], own.shape[2]
    kv_spec = pl.BlockSpec((2, 2 * BLK, HD), lambda g, info: (0, 0, g))
    win_spec = pl.BlockSpec((2, BLK, HD), lambda g, info: (0, 0, g))
    piece_spec = pl.BlockSpec((8, 2, 7, 16, HD), lambda g, info: (0, 0, 0, 0, g))
    row_spec = pl.BlockSpec((2 * BLK, NH * HD), lambda g, info: (0, g))
    return pl.pallas_call(
        attend_kernel,
        grid_spec=pltpu.PrefetchScalarGridSpec(
            num_scalar_prefetch=1,
            grid=(width // HD,),
            in_specs=[
                pl.BlockSpec((1, 2 * BLK, NH * HD), lambda g, info: (info[0], 0, g)),
                row_spec, kv_spec, kv_spec, win_spec, piece_spec,
            ],
            out_specs=[row_spec, kv_spec, win_spec, win_spec, piece_spec],
            scratch_shapes=[pltpu.VMEM((2, 2, BLK, HD), BF16), pltpu.VMEM((2, BLK, HD), F32)],
        ),
        out_shape=[
            stored((2 * BLK, q_width), BF16),
            stored((2, 2 * BLK, width), F32),
            stored((2, BLK, width), BF16),
            stored((2, BLK, width), BF16),
            stored((8, 2, 7, 16, width), BF16),
        ],
        compiler_params=params(28),
        cost_estimate=pl.CostEstimate(
            flops=10 * q_width * 14 * BLK * BLK, transcendentals=q_width * 14 * BLK, bytes_accessed=10 * MIB
        ),
        name="attend",
    )(
        info,
        *(
            pltpu.with_memory_space_constraint(a, pltpu.HBM)
            for a in (queries, upstream, own, partner, neighbour)
        ),
        got,
    )


def row_parts(info_ref, x_ref, got_ref, g):
    kc = columns(2 * (info_ref[1] // 8) + g, HD)
    qc = slice(g * NH * HD, (g + 1) * NH * HD)
    n_keys = got_ref.shape[0] * 2 * 16
    q, do = heads_to_rows(x_ref[0, :, qc]), heads_to_rows(x_ref[1, :, qc])
    return (q, do, *(got_ref[:, i, :, :, kc].reshape(n_keys, HD) for i in range(2)))


def stats_kernel(info_ref, x_ref, got_ref, out_ref):
    for g in range(2):
        q, do, k, v = row_parts(info_ref, x_ref, got_ref, g)
        e = jnp.exp2(dot(k, q, NT) * EXP2_SCALE)
        total = jnp.sum(e, axis=0, keepdims=True)
        inverse = jnp.where(total > 0, 1.0 / total, 0.0)
        delta = jnp.sum(e * inverse * dot(v, do, NT), axis=0, keepdims=True)
        rows = [a[:, h * BLK : (h + 1) * BLK] for a in (total, delta) for h in range(NH)]
        out_ref[g] = jnp.concatenate(rows, axis=0)


def row_kernel(info_ref, x_ref, got_ref, st_ref, dq_ref, down_ref):
    def lanes(a):
        return jnp.concatenate([a[h : h + 1] for h in range(NH)], axis=1)

    for g in range(2):
        q, do, k, v = row_parts(info_ref, x_ref, got_ref, g)
        inverse, mixed = 1.0 / st_ref[g, :NH, :], st_ref[g, NH:, :]
        p = jnp.exp2(dot(k, q, NT) * EXP2_SCALE) * lanes(inverse)
        pb = p.astype(BF16)
        ds = (p * (dot(v, do, NT) - lanes(mixed))).astype(BF16)
        dqt = dot(k, ds, TN) * SCALE
        dq_ref[:, g * NH * HD : (g + 1) * NH * HD] = jnp.concatenate(
            [dqt[:, h * HD : (h + 1) * HD].T for h in range(NH)], axis=1
        ).astype(BF16)
        kc = slice(g * HD, (g + 1) * HD)
        for i, grad in enumerate((dot(ds, q) * SCALE, dot(pb, do))):
            down_ref[:, i, :, :, kc] = grad.reshape(16, 2, 16, HD)


def place_kernel(info_ref, *refs):
    *part_refs, dq_ref, out_ref = refs
    width = part_refs[0].shape[1]

    @pl.when(info_ref[1] == 0)
    def _():
        for h in range(2):
            out_ref[:, h * width : (h + 1) * width] = part_refs[h][...]

    @pl.when(info_ref[1] != 0)
    def _():
        out_ref[...] = dq_ref[...]


def place(info, parts, dq):
    top = pl.BlockSpec((BLK, dq.shape[1]), lambda i, info: (0, 0))
    piece = pl.BlockSpec(parts[0].shape, lambda i, info: (0, 0))
    return pl.pallas_call(
        place_kernel,
        grid_spec=pltpu.PrefetchScalarGridSpec(
            num_scalar_prefetch=1, grid=(1,), in_specs=[piece] * 2 + [top], out_specs=top
        ),
        out_shape=stored(dq.shape, BF16),
        input_output_aliases={3: 0},
        compiler_params=params(12),
        name="place",
    )(info, *parts, dq)


def finish_kernel(info_ref, own_ref, winp_ref, winn_ref, got_ref, dk_ref, dv_ref):
    even = info_ref[1] % 2 == 0

    def total(first_ref, second_ref):
        for i, out_ref in enumerate((dk_ref, dv_ref)):
            for b, win_ref in enumerate((first_ref, second_ref)):
                for j in range(8):
                    rows = slice(b * BLK + j * 16, b * BLK + (j + 1) * 16)
                    pieces = got_ref[j, i, b].astype(F32) + got_ref[j + 8, i, b].astype(F32)
                    window = win_ref[i, j * 16 : (j + 1) * 16].astype(F32)
                    out_ref[rows, :] = (own_ref[i, rows, :] + pieces + window).astype(BF16)

    @pl.when(even)
    def _():
        total(winn_ref, winp_ref)

    @pl.when(jnp.logical_not(even))
    def _():
        total(winp_ref, winn_ref)


def send(block, pairs):
    return lax.ppermute(block, "ctx", pairs)


def add(a, *others):
    total = a.astype(F32)
    for o in others:
        total = total + o.astype(F32)
    return total.astype(BF16)


def merge_stats(mine, other):
    sums, deltas = zip(*((a[:, :NH], a[:, NH:]) for a in (mine, other)))
    total = sums[0] + sums[1]
    inverse = jnp.where(total > 0, 1.0 / total, 0.0)
    delta = (sums[0] * inverse) * deltas[0] + (sums[1] * inverse) * deltas[1]
    return jnp.concatenate([total, delta], axis=1)


def per_device(queries, keys, values, grad_slab, plan, random_blocks):
    n_seg, n_ctx = lax.axis_size("segment"), lax.axis_size("ctx")
    rank = lax.axis_index("ctx").astype(jnp.int32)
    queries, keys, values, grad = queries[0], keys[0], values[0], grad_slab[0]
    width, q_width = keys.shape[2], queries.shape[2]
    half = q_width // 2
    info = jnp.concatenate([plan, rank[None]])
    halves = [list(range(8)), list(range(8, 16))]
    slots = jnp.concatenate(
        [jnp.zeros((n_ctx, 1), jnp.int32), random_blocks.reshape(n_ctx, 6)], axis=1
    )
    side = rank // 8
    table = lax.dynamic_slice_in_dim(slots, side * 8, 8, 0).reshape(56)
    table = jnp.concatenate([table, side[None]])

    def exchange(x):
        return lax.all_to_all(x, "ctx", 0, 0, tiled=True)

    def exchange_half(x):
        return lax.all_to_all(x, "ctx", 0, 0, tiled=True, axis_index_groups=halves)

    both = ("segment", "ctx")

    def flat(s, r):
        return (s % n_seg) * n_ctx + r

    own, send1, edge, q0, q1, g0, g1 = pack(info, keys, values, queries, grad)
    q1 = send(q1, [(0, 8)])
    g0 = lax.ppermute(g0, both, [(flat(s + 1, 0), flat(s, 0)) for s in range(n_seg)])
    g1 = lax.ppermute(g1, both, [(flat(s + 1, 0), flat(s, 8)) for s in range(n_seg)])
    got1 = exchange(send1)
    x = jnp.stack([jnp.where(rank == 0, q0, jnp.zeros((), BF16)) + q1, g0 + g1])
    swap = [(r, r ^ 1) for r in range(n_ctx)]
    ring = [(r, (r - 1 if r % 2 == 0 else r + 1) % n_ctx) for r in range(n_ctx)]
    partner, neighbour = send(own, swap), send(edge, ring)
    x = x + sum(send(x, [(r, r + 2 * y) for r in (0, 8)]) for y in (1, 2, 3))
    x, got1, grad, partner, neighbour = lax.optimization_barrier(
        (x, got1, grad, partner, neighbour)
    )
    upstream = lax.ppermute(grad, "segment", [((s + 1) % n_seg, s) for s in range(n_seg)])
    (send2,) = on_chip(select_kernel, "select", [stored((8, 2, 7, 16, width), BF16)], table, got1)
    got2 = exchange_half(send2)
    x = x + send(x, [(r, r + 1) for r in range(0, n_ctx, 2)])
    (stats,) = on_chip(stats_kernel, "row_stats", [stored((2, 8, BLK), F32)], info, x, got1)
    stats = merge_stats(stats, send(stats, swap))
    others = [
        send(stats, [(r, (r // 8) * 8 + (r + 2 * y) % 8) for r in range(n_ctx)]) for y in (1, 2, 3)
    ]
    got2, stats, *others = lax.optimization_barrier((got2, stats, *others))
    dq, down, winp, winn, send3 = attend(
        info, queries, upstream, own, partner, neighbour, got2
    )
    got3 = exchange_half(send3)
    stats, *others = lax.optimization_barrier((stats, *others, send3))[:4]
    stats = merge_stats(merge_stats(stats, others[1]), merge_stats(others[0], others[2]))
    part, row = on_chip(
        row_kernel,
        "row_grads",
        [stored((BLK, half), BF16), stored((16, 2, 2, 16, 2 * HD), F32)],
        info, x, got1, stats,
    )
    winp, winn = send(winp, swap), send(winn, ring)
    part = add(part, send(part, [(r + 1, r) for r in range(0, n_ctx, 2)]))
    near = [send(part, [(r + 2 * y, r) for r in (0, 8)]) for y in (1, 2, 3)]
    got3, winp, part, *near = lax.optimization_barrier((got3, winp, part, *near))

    (send4,) = on_chip(
        combine_kernel,
        "combine",
        [stored((16, 2, 2, 16, width), BF16)],
        table, got3, row,
        scratch=[pltpu.VMEM((16, 2, 2, 16, width), F32)],
    )
    got4 = exchange(send4)
    part = after(add(part, *near), send4)
    dq = place(info, [part, send(part, [(8, 0)])], dq)
    got4, dq = lax.optimization_barrier((got4, dq))
    dk, dv = on_chip(
        finish_kernel,
        "finish",
        [shape((2 * BLK, width), BF16)] * 2,
        info, down, winp, winn, got4,
    )
    return dq[None], dk[None], dv[None]


def solution(mesh):
    return jax.shard_map(
        per_device,
        mesh=mesh,
        in_specs=(
            P("segment", None, "ctx", None),
            P("segment", None, "ctx", None),
            P("segment", None, "ctx", None),
            P("segment", "ctx", None),
            P("segment"),
            P(),
        ),
        out_specs=(P("segment", "ctx", None), P("segment", "ctx", None), P("segment", "ctx", None)),
        check_vma=False,
    )
```

time: 534 us -> 162 us (0.30)
  waiting for transfers between devices: 234 us -> 64.3 us
  local copies, waits for them, and re-layouts: 124 us -> 1.75 us
  matrix products: 95 us -> 0 us
  starting transfers between devices: 4.32 us -> 60.8 us
  other arithmetic: 58.6 us -> 6.34 us
  Pallas kernels: 0 us -> 26.7 us
  between operations: 14.7 us -> 1.56 us
    reduce_scatter x1 -> x0, waiting for transfers between devices: 125 us -> none  [per_device(): lax.psum_scatter(flat_buffer, 'ctx', scatter_dimension=0, tiled=True)]
    dot_general x25 -> x0, matrix products: 95 us -> none  [the longest x4 13.1 us: global_rows(): jnp.einsum('htgd,hsd->hgts', grad_rows, value_set, preferred_element_type...]
    all_gather x2 -> x0, waiting for transfers between devices: 91.3 us -> none  [the longest x1 47.6 us: per_device(): lax.all_gather(key_now, 'ctx', axis=0, tiled=True)]
    ppermute x1 -> x21, waiting for transfers between devices: 18.5 us -> 64.3 us  [the longest x18 63 us: send(): return lax.ppermute(block, 'ctx', pairs)]
    ppermute x1 -> x21, starting transfers between devices: 4.2 us -> 38.8 us  [the longest x18 28.8 us: send(): return lax.ppermute(block, 'ctx', pairs)]
    concatenate x10 -> x0, local copies, waits for them, and re-layouts: 29.5 us -> none  [the longest x2 20.6 us: whole_row(): jnp.concatenate([row_dk.transpose(1, 0, 2).reshape(n_blocks * BLK, kv_wid...]
    pallas_call x0 -> x8, Pallas kernels: none -> 26.7 us  [the longest x5 11.2 us: on_chip(): pl.pallas_call(kernel, in_specs=[pl.BlockSpec(memory_space=pltpu.SMEM)] +...]
    transpose x3 -> x0, local copies, waits for them, and re-layouts: 26.1 us -> none  [the longest x1 12.1 us: whole_row(): row_dk.transpose(1, 0, 2).reshape(n_blocks * BLK, kv_width)]
  transfers between devices with their start and end apart: 4 -> 25, of which waited for: 4 -> 12; matrix products, arithmetic and copies ran while one was open for 8% -> 4% of each run, Pallas kernels for 0% -> 5%
where the time goes in v1:
time: 162 us; the launch traced here: 161 us
  waiting for transfers between devices  64.3 us (40%)
  starting transfers between devices  60.8 us (38%)
  Pallas kernels  26.7 us (16%)
  other arithmetic  6.34 us (4%)
  local copies, waits for them, and re-layouts  1.75 us (1%)
    ppermute x18, waiting for transfers between devices, send(): return lax.ppermute(block, 'ctx', pairs)  63 us
    ppermute x18, starting transfers between devices, send(): return lax.ppermute(block, 'ctx', pairs)  28.8 us
    all_to_all x2, starting transfers between devices, exchange_half(): return lax.all_to_all(x, 'ctx', 0, 0, tiled=True, axis_index_groups=halves)  13.9 us
    pallas_call x5, Pallas kernels, on_chip(): pl.pallas_call(kernel, in_specs=[pl.BlockSpec(memory_space=pltpu.SMEM)] +...  11.2 us
    pallas_call x1, Pallas kernels, attend(): pl.pallas_call(attend_kernel, grid_spec=pltpu.PrefetchScalarGridSpec(num_...  9.54 us
    all_to_all x2, starting transfers between devices, exchange(): return lax.all_to_all(x, 'ctx', 0, 0, tiled=True)  8.15 us
    ppermute x1, starting transfers between devices, per_device(): lax.ppermute(g0, both, [(flat(s + 1, 0), flat(s, 0)) for s in range(n_seg)])  6.22 us
    pallas_call x1, Pallas kernels, pack(): pl.pallas_call(pack_kernel, grid_spec=pltpu.PrefetchScalarGridSpec(num_sc...  3.54 us
  transfers between devices with their start and end apart: 25, of which 12 were waited for; matrix products, arithmetic and copies ran while one was open for 4% of the time, Pallas kernels for 5%

profile of v1, /device:TPU:0, one launch (start us, length us, event | category | flops | bytes accessed | tf_op | source)
XLA Modules:
  0.0 161.4 jit_solution(8687270917988862108)
XLA Ops:
  1.3 0.1 pad_add_fusion.1.info_ref
  1.4 3.5 %pack.1 = (bf16[2,256,512]{2,1,0:T(8,128)(2,1)}, bf16[16,2,2,16,512]{4,3,2,1,0:T(8,128)(2,1)}, bf16[2,128,512]{2,1,0:T(8,128)(2,1)}, bf16[128,1024]{1,0:T(8,128)...) custom-call(s32[2]{0:T(128)S(1)} %pad_add_fusion.1.info_ref, ...), custom_call_target="tpu_custom_call" | custom-call | tf_op jit(solution)/shard_map/pack/pallas_call | solution.py:81
  4.9 6.2 %collective-permute-start.1 = (bf16[128,1024]{1,0:T(8,128)(2,1)}, bf16[128,1024]{1,0:T(8,128)(2,1)S(1)}, u32[]{:S(2)}, u32[]{:S(2)}) collective-permute-start(bf16[128,1024]{1,0:T(8,128)(2,1)} %get-tuple-element.44), channel_id=1, source_target_pairs={{16,0},{32,16},{48,32},{64,48},{80,64},{96,80},{112,96},{0,112}} | collective-permute-start | bytes 786440 | tf_op jit(solution)/shard_map/ppermute | solution.py:393
  11.1 2.8 %collective-permute-start.2 = (bf16[128,1024]{1,0:T(8,128)(2,1)}, bf16[128,1024]{1,0:T(8,128)(2,1)S(1)}, u32[]{:S(2)}, u32[]{:S(2)}) collective-permute-start(bf16[128,1024]{1,0:T(8,128)(2,1)} %get-tuple-element.45), channel_id=1, source_target_pairs={{16,8},{32,24},{48,40},{64,56},{80,72},{96,88},{112,104},{0,120}} | collective-permute-start | bytes 786440 | tf_op jit(solution)/shard_map/ppermute | solution.py:394
  13.9 1.3 collective-permute-start
  15.3 3.7 %all-to-all-start = ((bf16[16,2,2,16,512]{4,3,2,1,0:T(8,128)(2,1)}), bf16[16,2,2,16,512]{4,3,2,1,0:T(8,128)(2,1)S(1)}, u32[]{:S(2)}, u32[]{:S(2)}) async-start(bf16[16,2,2,16,512]{4,3,2,1,0:T(8,128)(2,1)} %get-tuple-element.46), calls=%async_computation | async-start | bytes 2097152 | tf_op jit(solution)/shard_map/all_to_all | solution.py:381
  18.9 0.0 copy-start.6
  19.0 0.0 collective-permute-done.1
  19.0 0.4 collective-permute-done
  19.5 0.8 pad_maximum_fusion
  20.3 4.6 %collective-permute-start.5 = (bf16[2,128,1024]{2,1,0:T(8,128)(2,1)}, bf16[2,128,1024]{2,1,0:T(8,128)(2,1)S(1)}, u32[]{:S(2)}, u32[]{:S(2)}) collective-permute-start(bf16[2,128,1024]{2,1,0:T(8,128)(2,1)} %pad_maximum_fusion), channel_id=1, source_target_pairs={{0,6},{8,14},{16,22},{24,30},{32,38},{40,46},{48,54},{56,62},{64,7... | collective-permute-start | bytes 1572872 | tf_op jit(solution)/shard_map/ppermute | solution.py:347
  24.9 1.3 collective-permute-start.4
  26.2 1.3 collective-permute-start.3
  27.5 0.1 collective-permute-start.6
  27.6 0.7 collective-permute-start.7
  28.3 0.1 copy.11
  28.4 0.1 reshape.12
  28.5 0.1 pad_dynamic-slice_fusion
  28.5 0.1 reshape.13
  28.6 0.1 pad_add_fusion.table_ref
  28.7 8.3 %collective-permute-done.5 = bf16[2,128,1024]{2,1,0:T(8,128)(2,1)S(1)} collective-permute-done((bf16[2,128,1024]{2,1,0:T(8,128)(2,1)}, bf16[2,128,1024]{2,1,0:T(8,128)(2,1)S(1)}, u32[]{:S(2)}, u32[]{:S(2)}) %collective-permute-start.5) | collective-permute-done | bytes 524320 | tf_op jit(solution)/shard_map/ppermute | solution.py:347
  37.0 2.9 %collective-permute-done.4 = bf16[2,128,1024]{2,1,0:T(8,128)(2,1)S(1)} collective-permute-done((bf16[2,128,1024]{2,1,0:T(8,128)(2,1)}, bf16[2,128,1024]{2,1,0:T(8,128)(2,1)S(1)}, u32[]{:S(2)}, u32[]{:S(2)}) %collective-permute-start.4) | collective-permute-done | bytes 524320 | tf_op jit(solution)/shard_map/ppermute | solution.py:347
  39.9 5.6 %collective-permute-done.3 = bf16[2,128,1024]{2,1,0:T(8,128)(2,1)S(1)} collective-permute-done((bf16[2,128,1024]{2,1,0:T(8,128)(2,1)}, bf16[2,128,1024]{2,1,0:T(8,128)(2,1)S(1)}, u32[]{:S(2)}, u32[]{:S(2)}) %collective-permute-start.3) | collective-permute-done | bytes 524320 | tf_op jit(solution)/shard_map/ppermute | solution.py:347
  45.5 0.9 add_add_fusion
  46.4 0.0 all-to-all-done.got_ref
  46.4 2.2 %select.6 = bf16[8,2,7,16,512]{4,3,2,1,0:T(8,128)(2,1)} custom-call(s32[57]{0:T(128)S(1)} %pad_add_fusion.table_ref, bf16[16,2,2,16,512]{4,3,2,1,0:T(8,128)(2,1)S(1)} %all-to-all-done.got_ref), custom_call_target="tpu_custom_call" | custom-call | tf_op jit(solution)/shard_map/select/pallas_call | solution.py:33
  48.6 3.8 %all-to-all-start.1 = ((bf16[8,2,7,16,512]{4,3,2,1,0:T(8,128)(2,1)}), bf16[8,2,7,16,512]{4,3,2,1,0:T(8,128)(2,1)S(1)}, u32[]{:S(2)}, u32[]{:S(2)}) async-start(bf16[8,2,7,16,512]{4,3,2,1,0:T(8,128)(2,1)} %select.6), calls=%async_computation.1 | async-start | bytes 3670016 | tf_op jit(solution)/shard_map/all_to_all | solution.py:384
  52.4 0.9 collective-permute-start.8
  53.3 2.1 %collective-permute-start.9 = (bf16[2,128,1024]{2,1,0:T(8,128)(2,1)S(1)}, bf16[2,128,1024]{2,1,0:T(8,128)(2,1)S(1)}, u32[]{:S(2)}, u32[]{:S(2)}) collective-permute-start(bf16[2,128,1024]{2,1,0:T(8,128)(2,1)S(1)} %copy-done.2), channel_id=1, source_target_pairs={{0,1},{2,3},{4,5},{6,7},{8,9},{10,11},{12,13},{14,15},{16,17},{18,... | collective-permute-start | bytes 1572872 | tf_op jit(solution)/shard_map/ppermute | solution.py:347
  55.4 1.5 collective-permute-done.9
  56.9 1.2 add.66.x_ref
  58.1 1.9 %row_stats.1 = f32[2,8,128]{2,1,0:T(8,128)} custom-call(s32[2]{0:T(128)S(1)} %pad_add_fusion.1.info_ref, bf16[2,128,1024]{2,1,0:T(8,128)(2,1)S(1)} %add.66.x_ref, bf16[16,2,2,16,512]{4,3,2,1,0:T(8,128)(2,1)S(1)} %all-to-all-done.got_ref), custom_call_target="tpu_custom_call" | custom-call | tf_op jit(solution)/shard_map/row_stats/pallas_call | solution.py:33
  60.0 0.4 collective-permute-start.10
  60.4 1.0 collective-permute-done.10
  61.4 0.8 fusion
  62.2 2.9 %collective-permute-start.13 = (f32[2,8,128]{2,1,0:T(8,128)S(1)}, f32[2,8,128]{2,1,0:T(8,128)S(1)}, u32[]{:S(2)}, u32[]{:S(2)}) collective-permute-start(f32[2,8,128]{2,1,0:T(8,128)S(1)} %pad_maximum_fusion.1), channel_id=1, source_target_pairs={{0,6},{1,7},{2,0},{3,1},{4,2},{5,3},{6,4},{7,5},{8,14},{9,15},{10,... | collective-permute-start | bytes 24584 | tf_op jit(solution)/shard_map/ppermute | solution.py:347
  65.2 0.9 collective-permute-start.12
  66.0 0.9 collective-permute-start.11
  66.9 8.7 %collective-permute-done.13 = f32[2,8,128]{2,1,0:T(8,128)S(1)} collective-permute-done((f32[2,8,128]{2,1,0:T(8,128)S(1)}, f32[2,8,128]{2,1,0:T(8,128)S(1)}, u32[]{:S(2)}, u32[]{:S(2)}) %collective-permute-start.13) | collective-permute-done | bytes 8224 | tf_op jit(solution)/shard_map/ppermute | solution.py:347
  75.5 1.5 collective-permute-done.12
  77.0 1.2 collective-permute-done.8.do_ref
  78.3 9.5 %attend.1 = (bf16[256,2048]{1,0:T(8,128)(2,1)}, f32[2,256,512]{2,1,0:T(8,128)}, bf16[2,128,512]{2,1,0:T(8,128)(2,1)}, bf16[2,128,512]{2,1,0:T(8,128)(2,1)}, bf16[8,2,7,16,512]{4,3,2,1,0:T(8,128)(2,1)}) custom-call(s32[2]{0:T(128)S(1)} %pad_add_fusion.1.info_ref, bf16[8,256,2048]{2,1,0:T(8,128)(2,1)} %bitcast.14, ...), custom_call_target="tpu_custom_call" | custom-call | flops 4697620480 | bytes 10485760 | tf_op jit(solution)/shard_map/attend/pallas_call | solution.py:224
  87.8 10.1 %all-to-all-start.2 = ((bf16[8,2,7,16,512]{4,3,2,1,0:T(8,128)(2,1)}), bf16[8,2,7,16,512]{4,3,2,1,0:T(8,128)(2,1)S(1)}, u32[]{:S(2)}, u32[]{:S(2)}) async-start(bf16[8,2,7,16,512]{4,3,2,1,0:T(8,128)(2,1)} %get-tuple-element.55), calls=%async_computation.2 | async-start | bytes 3670016 | tf_op jit(solution)/shard_map/all_to_all | solution.py:384
  98.0 3.2 %row_grads.1 = (bf16[128,1024]{1,0:T(8,128)(2,1)}, f32[16,2,2,16,256]{4,3,2,1,0:T(8,128)}) custom-call(s32[2]{0:T(128)S(1)} %pad_add_fusion.1.info_ref, bf16[2,128,1024]{2,1,0:T(8,128)(2,1)S(1)} %add.66.x_ref, bf16[16,2,2,16,512]{4,3,2,1,0:T(8,128)(2,1)S(1)} %all-to-all-done.got_ref, f32[2,8,128]{2,1,0:T(8,128)S(1)} %pad_maximum_fusion.2.st_ref), custom_call_target="tpu_custom_call" | custom-call | tf_op jit(solution)/shard_map/row_grads/pallas_call | solution.py:33
  101.2 1.3 collective-permute-start.15
  102.5 1.2 collective-permute-start.14
  103.7 1.1 collective-permute-done.15
  104.8 1.0 add_convert_fusion.1
  105.9 1.3 collective-permute-start.18
  107.2 1.3 collective-permute-start.17
  108.5 1.3 collective-permute-start.16
  109.8 0.0 collective-permute-done.14.winp_ref
  109.8 17.9 %collective-permute-done.18 = bf16[128,1024]{1,0:T(8,128)(2,1)S(1)} collective-permute-done((bf16[128,1024]{1,0:T(8,128)(2,1)S(1)}, bf16[128,1024]{1,0:T(8,128)(2,1)S(1)}, u32[]{:S(2)}, u32[]{:S(2)}) %collective-permute-start.18) | collective-permute-done | bytes 262176 | tf_op jit(solution)/shard_map/ppermute | solution.py:347
  127.7 0.0 collective-permute-done.16
  127.7 0.0 copy-start.4
  127.7 1.4 copy-done.1
  129.1 2.3 %combine.1 = bf16[16,2,2,16,512]{4,3,2,1,0:T(8,128)(2,1)} custom-call(s32[57]{0:T(128)S(1)} %pad_add_fusion.table_ref, bf16[8,2,7,16,512]{4,3,2,1,0:T(8,128)(2,1)S(1)} %all-to-all-done.2.got_ref, f32[16,2,2,16,256]{4,3,2,1,0:T(8,128)S(1)} %copy-done.1), custom_call_target="tpu_custom_call" | custom-call | tf_op jit(solution)/shard_map/combine/pallas_call | solution.py:33
  131.4 4.5 %all-to-all-start.3 = ((bf16[16,2,2,16,512]{4,3,2,1,0:T(8,128)(2,1)}), bf16[16,2,2,16,512]{4,3,2,1,0:T(8,128)(2,1)S(1)}, u32[]{:S(2)}, u32[]{:S(2)}) async-start(bf16[16,2,2,16,512]{4,3,2,1,0:T(8,128)(2,1)} %combine.1), calls=%async_computation.3 | async-start | bytes 2097152 | tf_op jit(solution)/shard_map/all_to_all | solution.py:381
  135.9 1.3 add_convert_fusion.refs_0_
  137.2 1.3 collective-permute-start.19
  138.5 4.8 %collective-permute-start.20 = (bf16[2,128,512]{2,1,0:T(8,128)(2,1)S(1)}, bf16[2,128,512]{2,1,0:T(8,128)(2,1)S(1)}, u32[]{:S(2)}, u32[]{:S(2)}) collective-permute-start(bf16[2,128,512]{2,1,0:T(8,128)(2,1)S(1)} %copy-done.8), channel_id=1, source_target_pairs={{0,15},{1,2},{2,1},{3,4},{4,3},{5,6},{6,5},{7,8},{8,7},{9,10},{10,... | collective-permute-start | bytes 786440 | tf_op jit(solution)/shard_map/ppermute | solution.py:347
  143.3 14.1 %collective-permute-done.19.refs_1_ = bf16[128,1024]{1,0:T(8,128)(2,1)S(1)} collective-permute-done((bf16[128,1024]{1,0:T(8,128)(2,1)S(1)}, bf16[128,1024]{1,0:T(8,128)(2,1)S(1)}, u32[]{:S(2)}, u32[]{:S(2)}) %collective-permute-start.19) | collective-permute-done | bytes 262176 | tf_op jit(solution)/shard_map/ppermute | solution.py:347
  157.4 2.4 %place.1 = bf16[256,2048]{1,0:T(8,128)(2,1)} custom-call(s32[2]{0:T(128)S(1)} %pad_add_fusion.1.info_ref, bf16[128,1024]{1,0:T(8,128)(2,1)S(1)} %add_convert_fusion.refs_0_, bf16[128,1024]{1,0:T(8,128)(2,1)S(1)} %collective-permute-done.19.refs_1_, bf16[256,2048]{1,0:T(8,128)(2,1)} %get-tuple-element.73.refs_2_), custom_call_target="tpu_custom_call", output_to_operand_aliasing={{}: (3, {})} | custom-call | tf_op jit(solution)/shard_map/place/pallas_call | solution.py:313
  159.8 1.6 finish.1
  (29 shorter events, 0.1 us)
Async XLA Ops:
  4.9 14.5 %copy-start.5 = (bf16[128,1024]{1,0:T(8,128)(2,1)S(1)}, bf16[128,1024]{1,0:T(8,128)(2,1)}, u32[]{:S(2)}) copy-start(bf16[128,1024]{1,0:T(8,128)(2,1)} %get-tuple-element.42) | copy-start | bytes 786436
  4.9 14.1 %collective-permute-start.1 = (bf16[128,1024]{1,0:T(8,128)(2,1)}, bf16[128,1024]{1,0:T(8,128)(2,1)S(1)}, u32[]{:S(2)}, u32[]{:S(2)}) collective-permute-start(bf16[128,1024]{1,0:T(8,128)(2,1)} %get-tuple-element.44), channel_id=1, source_target_pairs={{16,0},{32,16},{48,32},{64,48},{80,64},{96,80},{112,96},{0,112}} | collective-permute-start | bytes 786440 | tf_op jit(solution)/shard_map/ppermute | solution.py:393
  11.1 7.8 %collective-permute-start.2 = (bf16[128,1024]{1,0:T(8,128)(2,1)}, bf16[128,1024]{1,0:T(8,128)(2,1)S(1)}, u32[]{:S(2)}, u32[]{:S(2)}) collective-permute-start(bf16[128,1024]{1,0:T(8,128)(2,1)} %get-tuple-element.45), channel_id=1, source_target_pairs={{16,8},{32,24},{48,40},{64,56},{80,72},{96,88},{112,104},{0,120}} | collective-permute-start | bytes 786440 | tf_op jit(solution)/shard_map/ppermute | solution.py:394
  13.9 5.5 %collective-permute-start = (bf16[128,1024]{1,0:T(8,128)(2,1)}, bf16[128,1024]{1,0:T(8,128)(2,1)S(1)}, u32[]{:S(2)}, u32[]{:S(2)}) collective-permute-start(bf16[128,1024]{1,0:T(8,128)(2,1)} %get-tuple-element.43), channel_id=1, source_target_pairs={{0,8},{16,24},{32,40},{48,56},{64,72},{80,88},{96,104},{112,120}} | collective-permute-start | bytes 786440 | tf_op jit(solution)/shard_map/ppermute | solution.py:347
  15.3 31.2 %all-to-all-start = ((bf16[16,2,2,16,512]{4,3,2,1,0:T(8,128)(2,1)}), bf16[16,2,2,16,512]{4,3,2,1,0:T(8,128)(2,1)S(1)}, u32[]{:S(2)}, u32[]{:S(2)}) async-start(bf16[16,2,2,16,512]{4,3,2,1,0:T(8,128)(2,1)} %get-tuple-element.46), calls=%async_computation | async-start | bytes 2097152 | tf_op jit(solution)/shard_map/all_to_all | solution.py:381
  18.9 9.4 %copy-start.6 = (s32[32,3]{0,1:T(4,128)S(1)}, s32[32,3]{0,1:T(4,128)}, u32[]{:S(2)}) copy-start(s32[32,3]{0,1:T(4,128)} %param.11) | copy-start | bytes 1156
  20.3 16.7 %collective-permute-start.5 = (bf16[2,128,1024]{2,1,0:T(8,128)(2,1)}, bf16[2,128,1024]{2,1,0:T(8,128)(2,1)S(1)}, u32[]{:S(2)}, u32[]{:S(2)}) collective-permute-start(bf16[2,128,1024]{2,1,0:T(8,128)(2,1)} %pad_maximum_fusion), channel_id=1, source_target_pairs={{0,6},{8,14},{16,22},{24,30},{32,38},{40,46},{48,54},{56,62},{64,7... | collective-permute-start | bytes 1572872 | tf_op jit(solution)/shard_map/ppermute | solution.py:347
  24.9 15.0 %collective-permute-start.4 = (bf16[2,128,1024]{2,1,0:T(8,128)(2,1)}, bf16[2,128,1024]{2,1,0:T(8,128)(2,1)S(1)}, u32[]{:S(2)}, u32[]{:S(2)}) collective-permute-start(bf16[2,128,1024]{2,1,0:T(8,128)(2,1)} %pad_maximum_fusion), channel_id=1, source_target_pairs={{0,4},{8,12},{16,20},{24,28},{32,36},{40,44},{48,52},{56,60},{64,6... | collective-permute-start | bytes 1572872 | tf_op jit(solution)/shard_map/ppermute | solution.py:347
  26.2 19.3 %collective-permute-start.3 = (bf16[2,128,1024]{2,1,0:T(8,128)(2,1)}, bf16[2,128,1024]{2,1,0:T(8,128)(2,1)S(1)}, u32[]{:S(2)}, u32[]{:S(2)}) collective-permute-start(bf16[2,128,1024]{2,1,0:T(8,128)(2,1)} %pad_maximum_fusion), channel_id=1, source_target_pairs={{0,2},{8,10},{16,18},{24,26},{32,34},{40,42},{48,50},{56,58},{64,6... | collective-permute-start | bytes 1572872 | tf_op jit(solution)/shard_map/ppermute | solution.py:347
  27.5 18.9 %collective-permute-start.6 = (bf16[2,256,512]{2,1,0:T(8,128)(2,1)}, bf16[2,256,512]{2,1,0:T(8,128)(2,1)}, u32[]{:S(2)}, u32[]{:S(2)}) collective-permute-start(bf16[2,256,512]{2,1,0:T(8,128)(2,1)} %get-tuple-element.47.own_ref), channel_id=1, source_target_pairs={{0,1},{1,0},{2,3},{3,2},{4,5},{5,4},{6,7},{7,6},{8,9},{9,8},{10,11... | collective-permute-start | bytes 1572872 | tf_op jit(solution)/shard_map/ppermute | solution.py:347
  27.6 18.8 %collective-permute-start.7 = (bf16[2,128,512]{2,1,0:T(8,128)(2,1)}, bf16[2,128,512]{2,1,0:T(8,128)(2,1)S(1)}, u32[]{:S(2)}, u32[]{:S(2)}) collective-permute-start(bf16[2,128,512]{2,1,0:T(8,128)(2,1)} %get-tuple-element.48), channel_id=1, source_target_pairs={{0,15},{1,2},{2,1},{3,4},{4,3},{5,6},{6,5},{7,8},{8,7},{9,10},{10,... | collective-permute-start | bytes 786440 | tf_op jit(solution)/shard_map/ppermute | solution.py:347
  46.4 2.2 %copy-start.7 = (bf16[2,128,512]{2,1,0:T(8,128)(2,1)}, bf16[2,128,512]{2,1,0:T(8,128)(2,1)S(1)}, u32[]{:S(2)}) copy-start(bf16[2,128,512]{2,1,0:T(8,128)(2,1)S(1)} %collective-permute-done.7.nb_ref) | copy-start | bytes 786436
  48.6 4.7 %copy-start.2 = (bf16[2,128,1024]{2,1,0:T(8,128)(2,1)S(1)}, bf16[2,128,1024]{2,1,0:T(8,128)(2,1)}, u32[]{:S(2)}) copy-start(bf16[2,128,1024]{2,1,0:T(8,128)(2,1)} %add_add_fusion) | copy-start | bytes 1572868
  48.6 28.4 %all-to-all-start.1 = ((bf16[8,2,7,16,512]{4,3,2,1,0:T(8,128)(2,1)}), bf16[8,2,7,16,512]{4,3,2,1,0:T(8,128)(2,1)S(1)}, u32[]{:S(2)}, u32[]{:S(2)}) async-start(bf16[8,2,7,16,512]{4,3,2,1,0:T(8,128)(2,1)} %select.6), calls=%async_computation.1 | async-start | bytes 3670016 | tf_op jit(solution)/shard_map/all_to_all | solution.py:384
  52.4 25.9 %collective-permute-start.8 = (bf16[256,2048]{1,0:T(8,128)(2,1)}, bf16[256,2048]{1,0:T(8,128)(2,1)}, u32[]{:S(2)}, u32[]{:S(2)}) collective-permute-start(bf16[256,2048]{1,0:T(8,128)(2,1)} %bitcast.19), channel_id=1, source_target_pairs={{16,0},{32,16},{48,32},{64,48},{80,64},{96,80},{112,96},{0,112},{1... | collective-permute-start | bytes 3145736 | tf_op jit(solution)/shard_map/ppermute | solution.py:404
  53.3 3.6 %collective-permute-start.9 = (bf16[2,128,1024]{2,1,0:T(8,128)(2,1)S(1)}, bf16[2,128,1024]{2,1,0:T(8,128)(2,1)S(1)}, u32[]{:S(2)}, u32[]{:S(2)}) collective-permute-start(bf16[2,128,1024]{2,1,0:T(8,128)(2,1)S(1)} %copy-done.2), channel_id=1, source_target_pairs={{0,1},{2,3},{4,5},{6,7},{8,9},{10,11},{12,13},{14,15},{16,17},{18,... | collective-permute-start | bytes 1572872 | tf_op jit(solution)/shard_map/ppermute | solution.py:347
  60.0 1.4 collective-permute-start.10
  62.2 13.3 %collective-permute-start.13 = (f32[2,8,128]{2,1,0:T(8,128)S(1)}, f32[2,8,128]{2,1,0:T(8,128)S(1)}, u32[]{:S(2)}, u32[]{:S(2)}) collective-permute-start(f32[2,8,128]{2,1,0:T(8,128)S(1)} %pad_maximum_fusion.1), channel_id=1, source_target_pairs={{0,6},{1,7},{2,0},{3,1},{4,2},{5,3},{6,4},{7,5},{8,14},{9,15},{10,... | collective-permute-start | bytes 24584 | tf_op jit(solution)/shard_map/ppermute | solution.py:347
  65.2 11.9 %collective-permute-start.12 = (f32[2,8,128]{2,1,0:T(8,128)S(1)}, f32[2,8,128]{2,1,0:T(8,128)S(1)}, u32[]{:S(2)}, u32[]{:S(2)}) collective-permute-start(f32[2,8,128]{2,1,0:T(8,128)S(1)} %pad_maximum_fusion.1), channel_id=1, source_target_pairs={{0,4},{1,5},{2,6},{3,7},{4,0},{5,1},{6,2},{7,3},{8,12},{9,13},{10,... | collective-permute-start | bytes 24584 | tf_op jit(solution)/shard_map/ppermute | solution.py:347
  66.0 11.0 %collective-permute-start.11 = (f32[2,8,128]{2,1,0:T(8,128)S(1)}, f32[2,8,128]{2,1,0:T(8,128)S(1)}, u32[]{:S(2)}, u32[]{:S(2)}) collective-permute-start(f32[2,8,128]{2,1,0:T(8,128)S(1)} %pad_maximum_fusion.1), channel_id=1, source_target_pairs={{0,2},{1,3},{2,4},{3,5},{4,6},{5,7},{6,0},{7,1},{8,10},{9,11},{10,... | collective-permute-start | bytes 24584 | tf_op jit(solution)/shard_map/ppermute | solution.py:347
  87.8 39.9 %all-to-all-start.2 = ((bf16[8,2,7,16,512]{4,3,2,1,0:T(8,128)(2,1)}), bf16[8,2,7,16,512]{4,3,2,1,0:T(8,128)(2,1)S(1)}, u32[]{:S(2)}, u32[]{:S(2)}) async-start(bf16[8,2,7,16,512]{4,3,2,1,0:T(8,128)(2,1)} %get-tuple-element.55), calls=%async_computation.2 | async-start | bytes 3670016 | tf_op jit(solution)/shard_map/all_to_all | solution.py:384
  101.2 3.6 %collective-permute-start.15 = (bf16[128,1024]{1,0:T(8,128)(2,1)}, bf16[128,1024]{1,0:T(8,128)(2,1)S(1)}, u32[]{:S(2)}, u32[]{:S(2)}) collective-permute-start(bf16[128,1024]{1,0:T(8,128)(2,1)} %get-tuple-element.65), channel_id=1, source_target_pairs={{1,0},{3,2},{5,4},{7,6},{9,8},{11,10},{13,12},{15,14},{17,16},{19,... | collective-permute-start | bytes 786440 | tf_op jit(solution)/shard_map/ppermute | solution.py:347
  102.5 7.3 %collective-permute-start.14 = (bf16[2,128,512]{2,1,0:T(8,128)(2,1)}, bf16[2,128,512]{2,1,0:T(8,128)(2,1)S(1)}, u32[]{:S(2)}, u32[]{:S(2)}) collective-permute-start(bf16[2,128,512]{2,1,0:T(8,128)(2,1)} %get-tuple-element.56), channel_id=1, source_target_pairs={{0,1},{1,0},{2,3},{3,2},{4,5},{5,4},{6,7},{7,6},{8,9},{9,8},{10,11... | collective-permute-start | bytes 786440 | tf_op jit(solution)/shard_map/ppermute | solution.py:347
  105.9 21.8 %collective-permute-start.18 = (bf16[128,1024]{1,0:T(8,128)(2,1)S(1)}, bf16[128,1024]{1,0:T(8,128)(2,1)S(1)}, u32[]{:S(2)}, u32[]{:S(2)}) collective-permute-start(bf16[128,1024]{1,0:T(8,128)(2,1)S(1)} %add_convert_fusion.1), channel_id=1, source_target_pairs={{6,0},{14,8},{22,16},{30,24},{38,32},{46,40},{54,48},{62,56},{70,6... | collective-permute-start | bytes 786440 | tf_op jit(solution)/shard_map/ppermute | solution.py:347
  107.2 20.5 %collective-permute-start.17 = (bf16[128,1024]{1,0:T(8,128)(2,1)S(1)}, bf16[128,1024]{1,0:T(8,128)(2,1)S(1)}, u32[]{:S(2)}, u32[]{:S(2)}) collective-permute-start(bf16[128,1024]{1,0:T(8,128)(2,1)S(1)} %add_convert_fusion.1), channel_id=1, source_target_pairs={{4,0},{12,8},{20,16},{28,24},{36,32},{44,40},{52,48},{60,56},{68,6... | collective-permute-start | bytes 786440 | tf_op jit(solution)/shard_map/ppermute | solution.py:347
  108.5 19.2 %collective-permute-start.16 = (bf16[128,1024]{1,0:T(8,128)(2,1)S(1)}, bf16[128,1024]{1,0:T(8,128)(2,1)S(1)}, u32[]{:S(2)}, u32[]{:S(2)}) collective-permute-start(bf16[128,1024]{1,0:T(8,128)(2,1)S(1)} %add_convert_fusion.1), channel_id=1, source_target_pairs={{2,0},{10,8},{18,16},{26,24},{34,32},{42,40},{50,48},{58,56},{66,6... | collective-permute-start | bytes 786440 | tf_op jit(solution)/shard_map/ppermute | solution.py:347
  127.7 3.8 %copy-start.3 = (bf16[128,1024]{1,0:T(8,128)(2,1)}, bf16[128,1024]{1,0:T(8,128)(2,1)S(1)}, u32[]{:S(2)}) copy-start(bf16[128,1024]{1,0:T(8,128)(2,1)S(1)} %collective-permute-done.17) | copy-start | bytes 786436
  127.7 3.8 %copy-start.4 = (bf16[128,1024]{1,0:T(8,128)(2,1)}, bf16[128,1024]{1,0:T(8,128)(2,1)S(1)}, u32[]{:S(2)}) copy-start(bf16[128,1024]{1,0:T(8,128)(2,1)S(1)} %collective-permute-done.16) | copy-start | bytes 786436
  127.7 1.4 copy-start.1
  131.4 7.1 %copy-start.8 = (bf16[2,128,512]{2,1,0:T(8,128)(2,1)S(1)}, bf16[2,128,512]{2,1,0:T(8,128)(2,1)}, u32[]{:S(2)}) copy-start(bf16[2,128,512]{2,1,0:T(8,128)(2,1)} %get-tuple-element.77) | copy-start | bytes 786436
  131.4 28.4 %all-to-all-start.3 = ((bf16[16,2,2,16,512]{4,3,2,1,0:T(8,128)(2,1)}), bf16[16,2,2,16,512]{4,3,2,1,0:T(8,128)(2,1)S(1)}, u32[]{:S(2)}, u32[]{:S(2)}) async-start(bf16[16,2,2,16,512]{4,3,2,1,0:T(8,128)(2,1)} %combine.1), calls=%async_computation.3 | async-start | bytes 2097152 | tf_op jit(solution)/shard_map/all_to_all | solution.py:381
  135.9 23.9 %copy-start = (f32[2,256,512]{2,1,0:T(8,128)S(1)}, f32[2,256,512]{2,1,0:T(8,128)}, u32[]{:S(2)}) copy-start(f32[2,256,512]{2,1,0:T(8,128)} %get-tuple-element.75.own_ref) | copy-start | bytes 3145732
  137.2 20.2 %collective-permute-start.19 = (bf16[128,1024]{1,0:T(8,128)(2,1)S(1)}, bf16[128,1024]{1,0:T(8,128)(2,1)S(1)}, u32[]{:S(2)}, u32[]{:S(2)}) collective-permute-start(bf16[128,1024]{1,0:T(8,128)(2,1)S(1)} %add_convert_fusion.refs_0_), channel_id=1, source_target_pairs={{8,0},{24,16},{40,32},{56,48},{72,64},{88,80},{104,96},{120,112}} | collective-permute-start | bytes 786440 | tf_op jit(solution)/shard_map/ppermute | solution.py:347
  138.5 21.3 %collective-permute-start.20 = (bf16[2,128,512]{2,1,0:T(8,128)(2,1)S(1)}, bf16[2,128,512]{2,1,0:T(8,128)(2,1)S(1)}, u32[]{:S(2)}, u32[]{:S(2)}) collective-permute-start(bf16[2,128,512]{2,1,0:T(8,128)(2,1)S(1)} %copy-done.8), channel_id=1, source_target_pairs={{0,15},{1,2},{2,1},{3,4},{4,3},{5,6},{6,5},{7,8},{8,7},{9,10},{10,... | collective-permute-start | bytes 786440 | tf_op jit(solution)/shard_map/ppermute | solution.py:347

commit v2 on v1

--- a/solution.py
+++ b/solution.py
@@ -153,7 +153,7 @@
         wk_ref[0] = part_ref[:, BLK:, :]
         wk_ref[1] = nb_ref[...]
 
-    def attend(n):
+    def operands(n):
         rows = slice(n * BLK, (n + 1) * BLK)
         q, do = heads_to_rows(q_ref[0, rows, :]), heads_to_rows(do_ref[rows, :])
 
@@ -162,19 +162,25 @@
             parts += [rv_ref[:, i, 1 + 3 * n + j].reshape(BLK, HD) for j in range(3)]
             return jnp.concatenate(parts, axis=0)
 
-        k, v = blocks(0), blocks(1)
+        return q, do, blocks(0), blocks(1)
+
+    def exp_scores(n, q, do, k, v):
         e = jnp.exp2(dot(k, q, NT) * EXP2_SCALE)
         if n == 1:
             twice = jnp.logical_or(rank == 0, rank == 15)
             keep = jnp.where(twice, 0.0, 1.0).astype(F32)
             e = jnp.concatenate([e[: 3 * BLK], e[3 * BLK : 4 * BLK] * keep, e[4 * BLK :]], axis=0)
+        return e
+
+    def weights(e, q, do, k, v):
         p = e * (1.0 / jnp.sum(e, axis=0, keepdims=True))
-        pb = p.astype(BF16)
         dp = dot(v, do, NT)
         delta = jnp.sum(p * dp, axis=0, keepdims=True)
-        ds = (p * (dp - delta)).astype(BF16)
+        return p.astype(BF16), (p * (dp - delta)).astype(BF16)
+
+    def grads(n, pb, ds, q, do, k, v):
         dqt = dot(k, ds, TN) * SCALE
-        dq_ref[rows, :] = jnp.concatenate(
+        dq_ref[n * BLK : (n + 1) * BLK, :] = jnp.concatenate(
             [dqt[:, h * HD : (h + 1) * HD].T for h in range(NH)], axis=1
         ).astype(BF16)
         return dot(ds, q) * SCALE, dot(pb, do)
@@ -193,16 +199,12 @@
                 got = grad[(4 + j) * BLK : (5 + j) * BLK].astype(BF16)
                 send_ref[:, i, 1 + 3 * n + j] = got.reshape(8, 16, HD)
 
-    @pl.when(rank != 0)
-    def _():
-        emit(0, attend(0))
-
-    @pl.when(rank == 0)
-    def _():
-        dq_ref[:BLK, :] = jnp.zeros((BLK, NH * HD), BF16)
-        emit(0, [jnp.zeros((7 * BLK, HD), F32)] * 2)
-
-    emit(1, attend(1))
+    given = [operands(n) for n in range(2)]
+    scores = [exp_scores(n, *given[n]) for n in range(2)]
+    shares = [weights(scores[n], *given[n]) for n in range(2)]
+    first, second = (grads(n, *shares[n], *given[n]) for n in range(2))
+    emit(0, [jnp.where(rank != 0, term, 0.0) for term in first])
+    emit(1, second)
 
     @pl.when(even)
     def _():
@@ -425,8 +427,9 @@
     )
     winp, winn = send(winp, swap), send(winn, ring)
     part = add(part, send(part, [(r + 1, r) for r in range(0, n_ctx, 2)]))
-    near = [send(part, [(r + 2 * y, r) for r in (0, 8)]) for y in (1, 2, 3)]
-    got3, winp, part, *near = lax.optimization_barrier((got3, winp, part, *near))
+    near = [send(part, [(2 * y, 0), (8 + 2 * y, 1)]) for y in (1, 2, 3)]
+    far = send(part, [(8, 1)])
+    got3, winp, part, far, *near = lax.optimization_barrier((got3, winp, part, far, *near))
 
     (send4,) = on_chip(
         combine_kernel,
@@ -436,8 +439,8 @@
         scratch=[pltpu.VMEM((16, 2, 2, 16, width), F32)],
     )
     got4 = exchange(send4)
-    part = after(add(part, *near), send4)
-    dq = place(info, [part, send(part, [(8, 0)])], dq)
+    part = after(add(jnp.where(rank == 1, far, part), *near), send4)
+    dq = place(info, [part, send(part, [(1, 0)])], dq)
     got4, dq = lax.optimization_barrier((got4, dq))
     dk, dv = on_chip(
         finish_kernel,

time: 162 us -> 159 us (0.981)
  Pallas kernels: 26.7 us -> 31.6 us
  starting transfers between devices: 60.8 us -> 56.3 us
  waiting for transfers between devices: 64.3 us -> 60.4 us
    ppermute x18 -> x19, waiting for transfers between devices: 63 us -> 50.7 us  [send(): return lax.ppermute(block, 'ctx', pairs)]
    all_to_all x2, waiting for transfers between devices: 0.01 us -> 8.46 us  [exchange(): return lax.all_to_all(x, 'ctx', 0, 0, tiled=True)]
    all_to_all x2, starting transfers between devices: 13.9 us -> 8.22 us  [exchange_half(): return lax.all_to_all(x, 'ctx', 0, 0, tiled=True, axis_index_groups=halves)]
    pallas_call x1, Pallas kernels: 9.54 us -> 14.4 us  [attend(): pl.pallas_call(attend_kernel, grid_spec=pltpu.PrefetchScalarGridSpec(num_...]
    ppermute x18 -> x19, starting transfers between devices: 28.8 us -> 29.5 us  [send(): return lax.ppermute(block, 'ctx', pairs)]
  transfers between devices with their start and end apart: 25 -> 26, of which waited for: 12 -> 13; matrix products, arithmetic and copies ran while one was open for 4% -> 4% of each run, Pallas kernels for 5% -> 5%
where the time goes in v2:
time: 159 us; the launch traced here: 158 us
  waiting for transfers between devices  60.4 us (38%)
  starting transfers between devices  56.3 us (35%)
  Pallas kernels  31.6 us (20%)
  other arithmetic  6.4 us (4%)
  local copies, waits for them, and re-layouts  1.83 us (1%)
  between operations  1.59 us (1%)
    ppermute x19, waiting for transfers between devices, send(): return lax.ppermute(block, 'ctx', pairs)  50.7 us
    ppermute x19, starting transfers between devices, send(): return lax.ppermute(block, 'ctx', pairs)  29.5 us
    pallas_call x1, Pallas kernels, attend(): pl.pallas_call(attend_kernel, grid_spec=pltpu.PrefetchScalarGridSpec(num_...  14.4 us
    pallas_call x5, Pallas kernels, on_chip(): pl.pallas_call(kernel, in_specs=[pl.BlockSpec(memory_space=pltpu.SMEM)] +...  11.2 us
    all_to_all x2, starting transfers between devices, exchange(): return lax.all_to_all(x, 'ctx', 0, 0, tiled=True)  8.62 us
    all_to_all x2, waiting for transfers between devices, exchange(): return lax.all_to_all(x, 'ctx', 0, 0, tiled=True)  8.46 us
    all_to_all x2, starting transfers between devices, exchange_half(): return lax.all_to_all(x, 'ctx', 0, 0, tiled=True, axis_index_groups=halves)  8.22 us
    ppermute x1, starting transfers between devices, per_device(): lax.ppermute(g0, both, [(flat(s + 1, 0), flat(s, 0)) for s in range(n_seg)])  6.22 us
  transfers between devices with their start and end apart: 26, of which 13 were waited for; matrix products, arithmetic and copies ran while one was open for 4% of the time, Pallas kernels for 5%

profile of v2, /device:TPU:0, one launch (start us, length us, event | category | flops | bytes accessed | tf_op | source)
XLA Modules:
  0.0 158.1 jit_solution(10288782548027595871)
XLA Ops:
  1.3 0.1 pad_add_fusion.1.info_ref
  1.4 3.6 %pack.1 = (bf16[2,256,512]{2,1,0:T(8,128)(2,1)}, bf16[16,2,2,16,512]{4,3,2,1,0:T(8,128)(2,1)}, bf16[2,128,512]{2,1,0:T(8,128)(2,1)}, bf16[128,1024]{1,0:T(8,128)...) custom-call(s32[2]{0:T(128)S(1)} %pad_add_fusion.1.info_ref, ...), custom_call_target="tpu_custom_call" | custom-call | tf_op jit(solution)/shard_map/pack/pallas_call | solution.py:81
  4.9 6.2 %collective-permute-start.1 = (bf16[128,1024]{1,0:T(8,128)(2,1)}, bf16[128,1024]{1,0:T(8,128)(2,1)S(1)}, u32[]{:S(2)}, u32[]{:S(2)}) collective-permute-start(bf16[128,1024]{1,0:T(8,128)(2,1)} %get-tuple-element.45), channel_id=1, source_target_pairs={{16,0},{32,16},{48,32},{64,48},{80,64},{96,80},{112,96},{0,112}} | collective-permute-start | bytes 786440 | tf_op jit(solution)/shard_map/ppermute | solution.py:395
  11.1 2.8 %collective-permute-start.2 = (bf16[128,1024]{1,0:T(8,128)(2,1)}, bf16[128,1024]{1,0:T(8,128)(2,1)S(1)}, u32[]{:S(2)}, u32[]{:S(2)}) collective-permute-start(bf16[128,1024]{1,0:T(8,128)(2,1)} %get-tuple-element.46), channel_id=1, source_target_pairs={{16,8},{32,24},{48,40},{64,56},{80,72},{96,88},{112,104},{0,120}} | collective-permute-start | bytes 786440 | tf_op jit(solution)/shard_map/ppermute | solution.py:396
  14.0 1.3 collective-permute-start
  15.3 3.7 %all-to-all-start = ((bf16[16,2,2,16,512]{4,3,2,1,0:T(8,128)(2,1)}), bf16[16,2,2,16,512]{4,3,2,1,0:T(8,128)(2,1)S(1)}, u32[]{:S(2)}, u32[]{:S(2)}) async-start(bf16[16,2,2,16,512]{4,3,2,1,0:T(8,128)(2,1)} %get-tuple-element.47), calls=%async_computation | async-start | bytes 2097152 | tf_op jit(solution)/shard_map/all_to_all | solution.py:383
  18.9 0.0 copy-start.7
  19.0 0.0 collective-permute-done.1
  19.0 0.0 collective-permute-done.2
  19.0 0.4 collective-permute-done
  19.5 0.8 pad_maximum_fusion
  20.3 4.6 %collective-permute-start.5 = (bf16[2,128,1024]{2,1,0:T(8,128)(2,1)}, bf16[2,128,1024]{2,1,0:T(8,128)(2,1)S(1)}, u32[]{:S(2)}, u32[]{:S(2)}) collective-permute-start(bf16[2,128,1024]{2,1,0:T(8,128)(2,1)} %pad_maximum_fusion), channel_id=1, source_target_pairs={{0,6},{8,14},{16,22},{24,30},{32,38},{40,46},{48,54},{56,62},{64,7... | collective-permute-start | bytes 1572872 | tf_op jit(solution)/shard_map/ppermute | solution.py:349
  24.9 1.3 collective-permute-start.4
  26.2 1.3 collective-permute-start.3
  27.6 0.1 collective-permute-start.6
  27.7 0.7 collective-permute-start.7
  28.3 0.1 copy.11
  28.4 0.1 reshape.12
  28.5 0.1 pad_dynamic-slice_fusion
  28.6 0.1 reshape.13
  28.6 0.1 pad_add_fusion.table_ref
  28.7 8.3 %collective-permute-done.5 = bf16[2,128,1024]{2,1,0:T(8,128)(2,1)S(1)} collective-permute-done((bf16[2,128,1024]{2,1,0:T(8,128)(2,1)}, bf16[2,128,1024]{2,1,0:T(8,128)(2,1)S(1)}, u32[]{:S(2)}, u32[]{:S(2)}) %collective-permute-start.5) | collective-permute-done | bytes 524320 | tf_op jit(solution)/shard_map/ppermute | solution.py:349
  37.0 2.9 %collective-permute-done.4 = bf16[2,128,1024]{2,1,0:T(8,128)(2,1)S(1)} collective-permute-done((bf16[2,128,1024]{2,1,0:T(8,128)(2,1)}, bf16[2,128,1024]{2,1,0:T(8,128)(2,1)S(1)}, u32[]{:S(2)}, u32[]{:S(2)}) %collective-permute-start.4) | collective-permute-done | bytes 524320 | tf_op jit(solution)/shard_map/ppermute | solution.py:349
  39.9 5.6 %collective-permute-done.3 = bf16[2,128,1024]{2,1,0:T(8,128)(2,1)S(1)} collective-permute-done((bf16[2,128,1024]{2,1,0:T(8,128)(2,1)}, bf16[2,128,1024]{2,1,0:T(8,128)(2,1)S(1)}, u32[]{:S(2)}, u32[]{:S(2)}) %collective-permute-start.3) | collective-permute-done | bytes 524320 | tf_op jit(solution)/shard_map/ppermute | solution.py:349
  45.5 0.9 add_add_fusion
  46.4 2.2 %select.6 = bf16[8,2,7,16,512]{4,3,2,1,0:T(8,128)(2,1)} custom-call(s32[57]{0:T(128)S(1)} %pad_add_fusion.table_ref, bf16[16,2,2,16,512]{4,3,2,1,0:T(8,128)(2,1)S(1)} %all-to-all-done.got_ref), custom_call_target="tpu_custom_call" | custom-call | tf_op jit(solution)/shard_map/select/pallas_call | solution.py:33
  48.6 3.8 %all-to-all-start.1 = ((bf16[8,2,7,16,512]{4,3,2,1,0:T(8,128)(2,1)}), bf16[8,2,7,16,512]{4,3,2,1,0:T(8,128)(2,1)S(1)}, u32[]{:S(2)}, u32[]{:S(2)}) async-start(bf16[8,2,7,16,512]{4,3,2,1,0:T(8,128)(2,1)} %select.6), calls=%async_computation.1 | async-start | bytes 3670016 | tf_op jit(solution)/shard_map/all_to_all | solution.py:386
  52.4 0.9 collective-permute-start.8
  53.3 2.1 %collective-permute-start.9 = (bf16[2,128,1024]{2,1,0:T(8,128)(2,1)S(1)}, bf16[2,128,1024]{2,1,0:T(8,128)(2,1)S(1)}, u32[]{:S(2)}, u32[]{:S(2)}) collective-permute-start(bf16[2,128,1024]{2,1,0:T(8,128)(2,1)S(1)} %copy-done.2), channel_id=1, source_target_pairs={{0,1},{2,3},{4,5},{6,7},{8,9},{10,11},{12,13},{14,15},{16,17},{18,... | collective-permute-start | bytes 1572872 | tf_op jit(solution)/shard_map/ppermute | solution.py:349
  55.4 1.5 collective-permute-done.9
  56.9 1.2 add.66.x_ref
  58.1 1.9 %row_stats.1 = f32[2,8,128]{2,1,0:T(8,128)} custom-call(s32[2]{0:T(128)S(1)} %pad_add_fusion.1.info_ref, bf16[2,128,1024]{2,1,0:T(8,128)(2,1)S(1)} %add.66.x_ref, bf16[16,2,2,16,512]{4,3,2,1,0:T(8,128)(2,1)S(1)} %all-to-all-done.got_ref), custom_call_target="tpu_custom_call" | custom-call | tf_op jit(solution)/shard_map/row_stats/pallas_call | solution.py:33
  60.0 0.4 collective-permute-start.10
  60.4 1.0 collective-permute-done.10
  61.4 0.8 fusion
  62.2 3.0 %collective-permute-start.13 = (f32[2,8,128]{2,1,0:T(8,128)S(1)}, f32[2,8,128]{2,1,0:T(8,128)S(1)}, u32[]{:S(2)}, u32[]{:S(2)}) collective-permute-start(f32[2,8,128]{2,1,0:T(8,128)S(1)} %pad_maximum_fusion.1), channel_id=1, source_target_pairs={{0,6},{1,7},{2,0},{3,1},{4,2},{5,3},{6,4},{7,5},{8,14},{9,15},{10,... | collective-permute-start | bytes 24584 | tf_op jit(solution)/shard_map/ppermute | solution.py:349
  65.2 0.9 collective-permute-start.12
  66.0 0.9 collective-permute-start.11
  66.9 8.7 %collective-permute-done.13 = f32[2,8,128]{2,1,0:T(8,128)S(1)} collective-permute-done((f32[2,8,128]{2,1,0:T(8,128)S(1)}, f32[2,8,128]{2,1,0:T(8,128)S(1)}, u32[]{:S(2)}, u32[]{:S(2)}) %collective-permute-start.13) | collective-permute-done | bytes 8224 | tf_op jit(solution)/shard_map/ppermute | solution.py:349
  75.6 1.5 collective-permute-done.12
  77.1 1.2 collective-permute-done.8.do_ref
  78.3 14.4 %attend.1 = (bf16[256,2048]{1,0:T(8,128)(2,1)}, f32[2,256,512]{2,1,0:T(8,128)}, bf16[2,128,512]{2,1,0:T(8,128)(2,1)}, bf16[2,128,512]{2,1,0:T(8,128)(2,1)}, bf16[8,2,7,16,512]{4,3,2,1,0:T(8,128)(2,1)}) custom-call(s32[2]{0:T(128)S(1)} %pad_add_fusion.1.info_ref, bf16[8,256,2048]{2,1,0:T(8,128)(2,1)} %bitcast.14, ...), custom_call_target="tpu_custom_call" | custom-call | flops 4697620480 | bytes 10485760 | tf_op jit(solution)/shard_map/attend/pallas_call | solution.py:226
  92.7 4.4 %all-to-all-start.2 = ((bf16[8,2,7,16,512]{4,3,2,1,0:T(8,128)(2,1)}), bf16[8,2,7,16,512]{4,3,2,1,0:T(8,128)(2,1)S(1)}, u32[]{:S(2)}, u32[]{:S(2)}) async-start(bf16[8,2,7,16,512]{4,3,2,1,0:T(8,128)(2,1)} %get-tuple-element.56), calls=%async_computation.2 | async-start | bytes 3670016 | tf_op jit(solution)/shard_map/all_to_all | solution.py:386
  97.2 3.2 %row_grads.1 = (bf16[128,1024]{1,0:T(8,128)(2,1)}, f32[16,2,2,16,256]{4,3,2,1,0:T(8,128)}) custom-call(s32[2]{0:T(128)S(1)} %pad_add_fusion.1.info_ref, bf16[2,128,1024]{2,1,0:T(8,128)(2,1)S(1)} %add.66.x_ref, bf16[16,2,2,16,512]{4,3,2,1,0:T(8,128)(2,1)S(1)} %all-to-all-done.got_ref, f32[2,8,128]{2,1,0:T(8,128)S(1)} %pad_maximum_fusion.2.st_ref), custom_call_target="tpu_custom_call" | custom-call | tf_op jit(solution)/shard_map/row_grads/pallas_call | solution.py:33
  100.4 1.3 collective-permute-start.15
  101.7 1.2 collective-permute-start.14
  102.9 1.1 collective-permute-done.15
  104.1 1.0 add_convert_fusion.1
  105.1 1.3 collective-permute-start.19
  106.4 1.3 collective-permute-start.18
  107.7 1.3 collective-permute-start.17
  109.0 0.7 collective-permute-start.16
  109.7 17.2 %collective-permute-done.19 = bf16[128,1024]{1,0:T(8,128)(2,1)S(1)} collective-permute-done((bf16[128,1024]{1,0:T(8,128)(2,1)S(1)}, bf16[128,1024]{1,0:T(8,128)(2,1)S(1)}, u32[]{:S(2)}, u32[]{:S(2)}) %collective-permute-start.19) | collective-permute-done | bytes 262176 | tf_op jit(solution)/shard_map/ppermute | solution.py:349
  126.9 0.0 copy-start.4
  126.9 1.5 copy-done.1
  128.4 2.3 %combine.1 = bf16[16,2,2,16,512]{4,3,2,1,0:T(8,128)(2,1)} custom-call(s32[57]{0:T(128)S(1)} %pad_add_fusion.table_ref, bf16[8,2,7,16,512]{4,3,2,1,0:T(8,128)(2,1)S(1)} %all-to-all-done.2.got_ref, f32[16,2,2,16,256]{4,3,2,1,0:T(8,128)S(1)} %copy-done.1), custom_call_target="tpu_custom_call" | custom-call | tf_op jit(solution)/shard_map/combine/pallas_call | solution.py:33
  130.8 5.0 %all-to-all-start.3 = ((bf16[16,2,2,16,512]{4,3,2,1,0:T(8,128)(2,1)}), bf16[16,2,2,16,512]{4,3,2,1,0:T(8,128)(2,1)S(1)}, u32[]{:S(2)}, u32[]{:S(2)}) async-start(bf16[16,2,2,16,512]{4,3,2,1,0:T(8,128)(2,1)} %combine.1), calls=%async_computation.3 | async-start | bytes 2097152 | tf_op jit(solution)/shard_map/all_to_all | solution.py:383
  135.7 1.4 add_convert_fusion.refs_0_
  137.1 1.3 collective-permute-start.20
  138.4 4.8 %collective-permute-start.21 = (bf16[2,128,512]{2,1,0:T(8,128)(2,1)S(1)}, bf16[2,128,512]{2,1,0:T(8,128)(2,1)S(1)}, u32[]{:S(2)}, u32[]{:S(2)}) collective-permute-start(bf16[2,128,512]{2,1,0:T(8,128)(2,1)S(1)} %copy-done.9), channel_id=1, source_target_pairs={{0,15},{1,2},{2,1},{3,4},{4,3},{5,6},{6,5},{7,8},{8,7},{9,10},{10,... | collective-permute-start | bytes 786440 | tf_op jit(solution)/shard_map/ppermute | solution.py:349
  143.2 2.4 %place.1 = bf16[256,2048]{1,0:T(8,128)(2,1)} custom-call(s32[2]{0:T(128)S(1)} %pad_add_fusion.1.info_ref, bf16[128,1024]{1,0:T(8,128)(2,1)S(1)} %add_convert_fusion.refs_0_, bf16[128,1024]{1,0:T(8,128)(2,1)S(1)} %collective-permute-done.20.refs_1_, bf16[256,2048]{1,0:T(8,128)(2,1)} %get-tuple-element.75.refs_2_), custom_call_target="tpu_custom_call", output_to_operand_aliasing={{}: (3, {})} | custom-call | tf_op jit(solution)/shard_map/place/pallas_call | solution.py:315
  145.6 8.5 %all-to-all-done.3.got_ref = bf16[16,2,2,16,512]{4,3,2,1,0:T(8,128)(2,1)S(1)} async-done(((bf16[16,2,2,16,512]{4,3,2,1,0:T(8,128)(2,1)}), bf16[16,2,2,16,512]{4,3,2,1,0:T(8,128)(2,1)S(1)}, u32[]{:S(2)}, u32[]{:S(2)}) %all-to-all-start.3) | async-done | bytes 1048608 | tf_op jit(solution)/shard_map/all_to_all | solution.py:383
  154.0 2.5 %collective-permute-done.21.winn_ref = bf16[2,128,512]{2,1,0:T(8,128)(2,1)S(1)} collective-permute-done((bf16[2,128,512]{2,1,0:T(8,128)(2,1)S(1)}, bf16[2,128,512]{2,1,0:T(8,128)(2,1)S(1)}, u32[]{:S(2)}, u32[]{:S(2)}) %collective-permute-start.21) | collective-permute-done | bytes 262176 | tf_op jit(solution)/shard_map/ppermute | solution.py:349
  156.5 1.6 finish.1
  (33 shorter events, 0.2 us)
Async XLA Ops:
  4.9 14.5 %copy-start.6 = (bf16[128,1024]{1,0:T(8,128)(2,1)S(1)}, bf16[128,1024]{1,0:T(8,128)(2,1)}, u32[]{:S(2)}) copy-start(bf16[128,1024]{1,0:T(8,128)(2,1)} %get-tuple-element.43) | copy-start | bytes 786436
  4.9 14.1 %collective-permute-start.1 = (bf16[128,1024]{1,0:T(8,128)(2,1)}, bf16[128,1024]{1,0:T(8,128)(2,1)S(1)}, u32[]{:S(2)}, u32[]{:S(2)}) collective-permute-start(bf16[128,1024]{1,0:T(8,128)(2,1)} %get-tuple-element.45), channel_id=1, source_target_pairs={{16,0},{32,16},{48,32},{64,48},{80,64},{96,80},{112,96},{0,112}} | collective-permute-start | bytes 786440 | tf_op jit(solution)/shard_map/ppermute | solution.py:395
  11.1 7.8 %collective-permute-start.2 = (bf16[128,1024]{1,0:T(8,128)(2,1)}, bf16[128,1024]{1,0:T(8,128)(2,1)S(1)}, u32[]{:S(2)}, u32[]{:S(2)}) collective-permute-start(bf16[128,1024]{1,0:T(8,128)(2,1)} %get-tuple-element.46), channel_id=1, source_target_pairs={{16,8},{32,24},{48,40},{64,56},{80,72},{96,88},{112,104},{0,120}} | collective-permute-start | bytes 786440 | tf_op jit(solution)/shard_map/ppermute | solution.py:396
  14.0 5.5 %collective-permute-start = (bf16[128,1024]{1,0:T(8,128)(2,1)}, bf16[128,1024]{1,0:T(8,128)(2,1)S(1)}, u32[]{:S(2)}, u32[]{:S(2)}) collective-permute-start(bf16[128,1024]{1,0:T(8,128)(2,1)} %get-tuple-element.44), channel_id=1, source_target_pairs={{0,8},{16,24},{32,40},{48,56},{64,72},{80,88},{96,104},{112,120}} | collective-permute-start | bytes 786440 | tf_op jit(solution)/shard_map/ppermute | solution.py:349
  15.3 31.2 %all-to-all-start = ((bf16[16,2,2,16,512]{4,3,2,1,0:T(8,128)(2,1)}), bf16[16,2,2,16,512]{4,3,2,1,0:T(8,128)(2,1)S(1)}, u32[]{:S(2)}, u32[]{:S(2)}) async-start(bf16[16,2,2,16,512]{4,3,2,1,0:T(8,128)(2,1)} %get-tuple-element.47), calls=%async_computation | async-start | bytes 2097152 | tf_op jit(solution)/shard_map/all_to_all | solution.py:383
  18.9 9.4 %copy-start.7 = (s32[32,3]{0,1:T(4,128)S(1)}, s32[32,3]{0,1:T(4,128)}, u32[]{:S(2)}) copy-start(s32[32,3]{0,1:T(4,128)} %param.11) | copy-start | bytes 1156
  20.3 16.7 %collective-permute-start.5 = (bf16[2,128,1024]{2,1,0:T(8,128)(2,1)}, bf16[2,128,1024]{2,1,0:T(8,128)(2,1)S(1)}, u32[]{:S(2)}, u32[]{:S(2)}) collective-permute-start(bf16[2,128,1024]{2,1,0:T(8,128)(2,1)} %pad_maximum_fusion), channel_id=1, source_target_pairs={{0,6},{8,14},{16,22},{24,30},{32,38},{40,46},{48,54},{56,62},{64,7... | collective-permute-start | bytes 1572872 | tf_op jit(solution)/shard_map/ppermute | solution.py:349
  24.9 15.0 %collective-permute-start.4 = (bf16[2,128,1024]{2,1,0:T(8,128)(2,1)}, bf16[2,128,1024]{2,1,0:T(8,128)(2,1)S(1)}, u32[]{:S(2)}, u32[]{:S(2)}) collective-permute-start(bf16[2,128,1024]{2,1,0:T(8,128)(2,1)} %pad_maximum_fusion), channel_id=1, source_target_pairs={{0,4},{8,12},{16,20},{24,28},{32,36},{40,44},{48,52},{56,60},{64,6... | collective-permute-start | bytes 1572872 | tf_op jit(solution)/shard_map/ppermute | solution.py:349
  26.2 19.3 %collective-permute-start.3 = (bf16[2,128,1024]{2,1,0:T(8,128)(2,1)}, bf16[2,128,1024]{2,1,0:T(8,128)(2,1)S(1)}, u32[]{:S(2)}, u32[]{:S(2)}) collective-permute-start(bf16[2,128,1024]{2,1,0:T(8,128)(2,1)} %pad_maximum_fusion), channel_id=1, source_target_pairs={{0,2},{8,10},{16,18},{24,26},{32,34},{40,42},{48,50},{56,58},{64,6... | collective-permute-start | bytes 1572872 | tf_op jit(solution)/shard_map/ppermute | solution.py:349
  27.6 18.9 %collective-permute-start.6 = (bf16[2,256,512]{2,1,0:T(8,128)(2,1)}, bf16[2,256,512]{2,1,0:T(8,128)(2,1)}, u32[]{:S(2)}, u32[]{:S(2)}) collective-permute-start(bf16[2,256,512]{2,1,0:T(8,128)(2,1)} %get-tuple-element.48.own_ref), channel_id=1, source_target_pairs={{0,1},{1,0},{2,3},{3,2},{4,5},{5,4},{6,7},{7,6},{8,9},{9,8},{10,11... | collective-permute-start | bytes 1572872 | tf_op jit(solution)/shard_map/ppermute | solution.py:349
  27.7 18.8 %collective-permute-start.7 = (bf16[2,128,512]{2,1,0:T(8,128)(2,1)}, bf16[2,128,512]{2,1,0:T(8,128)(2,1)S(1)}, u32[]{:S(2)}, u32[]{:S(2)}) collective-permute-start(bf16[2,128,512]{2,1,0:T(8,128)(2,1)} %get-tuple-element.49), channel_id=1, source_target_pairs={{0,15},{1,2},{2,1},{3,4},{4,3},{5,6},{6,5},{7,8},{8,7},{9,10},{10,... | collective-permute-start | bytes 786440 | tf_op jit(solution)/shard_map/ppermute | solution.py:349
  46.4 2.2 %copy-start.8 = (bf16[2,128,512]{2,1,0:T(8,128)(2,1)}, bf16[2,128,512]{2,1,0:T(8,128)(2,1)S(1)}, u32[]{:S(2)}) copy-start(bf16[2,128,512]{2,1,0:T(8,128)(2,1)S(1)} %collective-permute-done.7.nb_ref) | copy-start | bytes 786436
  48.6 4.7 %copy-start.2 = (bf16[2,128,1024]{2,1,0:T(8,128)(2,1)S(1)}, bf16[2,128,1024]{2,1,0:T(8,128)(2,1)}, u32[]{:S(2)}) copy-start(bf16[2,128,1024]{2,1,0:T(8,128)(2,1)} %add_add_fusion) | copy-start | bytes 1572868
  48.6 28.4 %all-to-all-start.1 = ((bf16[8,2,7,16,512]{4,3,2,1,0:T(8,128)(2,1)}), bf16[8,2,7,16,512]{4,3,2,1,0:T(8,128)(2,1)S(1)}, u32[]{:S(2)}, u32[]{:S(2)}) async-start(bf16[8,2,7,16,512]{4,3,2,1,0:T(8,128)(2,1)} %select.6), calls=%async_computation.1 | async-start | bytes 3670016 | tf_op jit(solution)/shard_map/all_to_all | solution.py:386
  52.4 25.9 %collective-permute-start.8 = (bf16[256,2048]{1,0:T(8,128)(2,1)}, bf16[256,2048]{1,0:T(8,128)(2,1)}, u32[]{:S(2)}, u32[]{:S(2)}) collective-permute-start(bf16[256,2048]{1,0:T(8,128)(2,1)} %bitcast.19), channel_id=1, source_target_pairs={{16,0},{32,16},{48,32},{64,48},{80,64},{96,80},{112,96},{0,112},{1... | collective-permute-start | bytes 3145736 | tf_op jit(solution)/shard_map/ppermute | solution.py:406
  53.3 3.6 %collective-permute-start.9 = (bf16[2,128,1024]{2,1,0:T(8,128)(2,1)S(1)}, bf16[2,128,1024]{2,1,0:T(8,128)(2,1)S(1)}, u32[]{:S(2)}, u32[]{:S(2)}) collective-permute-start(bf16[2,128,1024]{2,1,0:T(8,128)(2,1)S(1)} %copy-done.2), channel_id=1, source_target_pairs={{0,1},{2,3},{4,5},{6,7},{8,9},{10,11},{12,13},{14,15},{16,17},{18,... | collective-permute-start | bytes 1572872 | tf_op jit(solution)/shard_map/ppermute | solution.py:349
  60.0 1.4 collective-permute-start.10
  62.2 13.3 %collective-permute-start.13 = (f32[2,8,128]{2,1,0:T(8,128)S(1)}, f32[2,8,128]{2,1,0:T(8,128)S(1)}, u32[]{:S(2)}, u32[]{:S(2)}) collective-permute-start(f32[2,8,128]{2,1,0:T(8,128)S(1)} %pad_maximum_fusion.1), channel_id=1, source_target_pairs={{0,6},{1,7},{2,0},{3,1},{4,2},{5,3},{6,4},{7,5},{8,14},{9,15},{10,... | collective-permute-start | bytes 24584 | tf_op jit(solution)/shard_map/ppermute | solution.py:349
  65.2 11.9 %collective-permute-start.12 = (f32[2,8,128]{2,1,0:T(8,128)S(1)}, f32[2,8,128]{2,1,0:T(8,128)S(1)}, u32[]{:S(2)}, u32[]{:S(2)}) collective-permute-start(f32[2,8,128]{2,1,0:T(8,128)S(1)} %pad_maximum_fusion.1), channel_id=1, source_target_pairs={{0,4},{1,5},{2,6},{3,7},{4,0},{5,1},{6,2},{7,3},{8,12},{9,13},{10,... | collective-permute-start | bytes 24584 | tf_op jit(solution)/shard_map/ppermute | solution.py:349
  66.0 11.0 %collective-permute-start.11 = (f32[2,8,128]{2,1,0:T(8,128)S(1)}, f32[2,8,128]{2,1,0:T(8,128)S(1)}, u32[]{:S(2)}, u32[]{:S(2)}) collective-permute-start(f32[2,8,128]{2,1,0:T(8,128)S(1)} %pad_maximum_fusion.1), channel_id=1, source_target_pairs={{0,2},{1,3},{2,4},{3,5},{4,6},{5,7},{6,0},{7,1},{8,10},{9,11},{10,... | collective-permute-start | bytes 24584 | tf_op jit(solution)/shard_map/ppermute | solution.py:349
  92.7 34.2 %all-to-all-start.2 = ((bf16[8,2,7,16,512]{4,3,2,1,0:T(8,128)(2,1)}), bf16[8,2,7,16,512]{4,3,2,1,0:T(8,128)(2,1)S(1)}, u32[]{:S(2)}, u32[]{:S(2)}) async-start(bf16[8,2,7,16,512]{4,3,2,1,0:T(8,128)(2,1)} %get-tuple-element.56), calls=%async_computation.2 | async-start | bytes 3670016 | tf_op jit(solution)/shard_map/all_to_all | solution.py:386
  100.4 3.6 %collective-permute-start.15 = (bf16[128,1024]{1,0:T(8,128)(2,1)}, bf16[128,1024]{1,0:T(8,128)(2,1)S(1)}, u32[]{:S(2)}, u32[]{:S(2)}) collective-permute-start(bf16[128,1024]{1,0:T(8,128)(2,1)} %get-tuple-element.66), channel_id=1, source_target_pairs={{1,0},{3,2},{5,4},{7,6},{9,8},{11,10},{13,12},{15,14},{17,16},{19,... | collective-permute-start | bytes 786440 | tf_op jit(solution)/shard_map/ppermute | solution.py:349
  101.7 8.0 %collective-permute-start.14 = (bf16[2,128,512]{2,1,0:T(8,128)(2,1)}, bf16[2,128,512]{2,1,0:T(8,128)(2,1)S(1)}, u32[]{:S(2)}, u32[]{:S(2)}) collective-permute-start(bf16[2,128,512]{2,1,0:T(8,128)(2,1)} %get-tuple-element.57), channel_id=1, source_target_pairs={{0,1},{1,0},{2,3},{3,2},{4,5},{5,4},{6,7},{7,6},{8,9},{9,8},{10,11... | collective-permute-start | bytes 786440 | tf_op jit(solution)/shard_map/ppermute | solution.py:349
  105.1 21.8 %collective-permute-start.19 = (bf16[128,1024]{1,0:T(8,128)(2,1)S(1)}, bf16[128,1024]{1,0:T(8,128)(2,1)S(1)}, u32[]{:S(2)}, u32[]{:S(2)}) collective-permute-start(bf16[128,1024]{1,0:T(8,128)(2,1)S(1)} %add_convert_fusion.1), channel_id=1, source_target_pairs={{6,0},{14,1},{22,16},{30,17},{38,32},{46,33},{54,48},{62,49},{70,6... | collective-permute-start | bytes 786440 | tf_op jit(solution)/shard_map/ppermute | solution.py:349
  106.4 20.5 %collective-permute-start.18 = (bf16[128,1024]{1,0:T(8,128)(2,1)S(1)}, bf16[128,1024]{1,0:T(8,128)(2,1)S(1)}, u32[]{:S(2)}, u32[]{:S(2)}) collective-permute-start(bf16[128,1024]{1,0:T(8,128)(2,1)S(1)} %add_convert_fusion.1), channel_id=1, source_target_pairs={{4,0},{12,1},{20,16},{28,17},{36,32},{44,33},{52,48},{60,49},{68,6... | collective-permute-start | bytes 786440 | tf_op jit(solution)/shard_map/ppermute | solution.py:349
  107.7 19.2 %collective-permute-start.17 = (bf16[128,1024]{1,0:T(8,128)(2,1)S(1)}, bf16[128,1024]{1,0:T(8,128)(2,1)S(1)}, u32[]{:S(2)}, u32[]{:S(2)}) collective-permute-start(bf16[128,1024]{1,0:T(8,128)(2,1)S(1)} %add_convert_fusion.1), channel_id=1, source_target_pairs={{2,0},{10,1},{18,16},{26,17},{34,32},{42,33},{50,48},{58,49},{66,6... | collective-permute-start | bytes 786440 | tf_op jit(solution)/shard_map/ppermute | solution.py:349
  109.0 17.9 %collective-permute-start.16 = (bf16[128,1024]{1,0:T(8,128)(2,1)S(1)}, bf16[128,1024]{1,0:T(8,128)(2,1)S(1)}, u32[]{:S(2)}, u32[]{:S(2)}) collective-permute-start(bf16[128,1024]{1,0:T(8,128)(2,1)S(1)} %add_convert_fusion.1), channel_id=1, source_target_pairs={{8,1},{24,17},{40,33},{56,49},{72,65},{88,81},{104,97},{120,113}} | collective-permute-start | bytes 786440 | tf_op jit(solution)/shard_map/ppermute | solution.py:349
  126.9 3.9 %copy-start.3 = (bf16[128,1024]{1,0:T(8,128)(2,1)}, bf16[128,1024]{1,0:T(8,128)(2,1)S(1)}, u32[]{:S(2)}) copy-start(bf16[128,1024]{1,0:T(8,128)(2,1)S(1)} %collective-permute-done.18) | copy-start | bytes 786436
  126.9 3.9 %copy-start.4 = (bf16[128,1024]{1,0:T(8,128)(2,1)}, bf16[128,1024]{1,0:T(8,128)(2,1)S(1)}, u32[]{:S(2)}) copy-start(bf16[128,1024]{1,0:T(8,128)(2,1)S(1)} %collective-permute-done.17) | copy-start | bytes 786436
  126.9 3.8 %copy-start.5 = (bf16[128,1024]{1,0:T(8,128)(2,1)}, bf16[128,1024]{1,0:T(8,128)(2,1)S(1)}, u32[]{:S(2)}) copy-start(bf16[128,1024]{1,0:T(8,128)(2,1)S(1)} %collective-permute-done.16) | copy-start | bytes 786436
  126.9 1.5 copy-start.1
  130.7 7.6 %copy-start.9 = (bf16[2,128,512]{2,1,0:T(8,128)(2,1)S(1)}, bf16[2,128,512]{2,1,0:T(8,128)(2,1)}, u32[]{:S(2)}) copy-start(bf16[2,128,512]{2,1,0:T(8,128)(2,1)} %get-tuple-element.79) | copy-start | bytes 786436
  130.8 23.3 %all-to-all-start.3 = ((bf16[16,2,2,16,512]{4,3,2,1,0:T(8,128)(2,1)}), bf16[16,2,2,16,512]{4,3,2,1,0:T(8,128)(2,1)S(1)}, u32[]{:S(2)}, u32[]{:S(2)}) async-start(bf16[16,2,2,16,512]{4,3,2,1,0:T(8,128)(2,1)} %combine.1), calls=%async_computation.3 | async-start | bytes 2097152 | tf_op jit(solution)/shard_map/all_to_all | solution.py:383
  135.7 20.8 %copy-start = (f32[2,256,512]{2,1,0:T(8,128)S(1)}, f32[2,256,512]{2,1,0:T(8,128)}, u32[]{:S(2)}) copy-start(f32[2,256,512]{2,1,0:T(8,128)} %get-tuple-element.77.own_ref) | copy-start | bytes 3145732
  137.1 6.1 %collective-permute-start.20 = (bf16[128,1024]{1,0:T(8,128)(2,1)S(1)}, bf16[128,1024]{1,0:T(8,128)(2,1)S(1)}, u32[]{:S(2)}, u32[]{:S(2)}) collective-permute-start(bf16[128,1024]{1,0:T(8,128)(2,1)S(1)} %add_convert_fusion.refs_0_), channel_id=1, source_target_pairs={{1,0},{17,16},{33,32},{49,48},{65,64},{81,80},{97,96},{113,112}} | collective-permute-start | bytes 786440 | tf_op jit(solution)/shard_map/ppermute | solution.py:349
  138.4 18.1 %collective-permute-start.21 = (bf16[2,128,512]{2,1,0:T(8,128)(2,1)S(1)}, bf16[2,128,512]{2,1,0:T(8,128)(2,1)S(1)}, u32[]{:S(2)}, u32[]{:S(2)}) collective-permute-start(bf16[2,128,512]{2,1,0:T(8,128)(2,1)S(1)} %copy-done.9), channel_id=1, source_target_pairs={{0,15},{1,2},{2,1},{3,4},{4,3},{5,6},{6,5},{7,8},{8,7},{9,10},{10,... | collective-permute-start | bytes 786440 | tf_op jit(solution)/shard_map/ppermute | solution.py:349

commit v3 on v2

--- a/solution.py
+++ b/solution.py
@@ -399,12 +399,13 @@
     swap = [(r, r ^ 1) for r in range(n_ctx)]
     ring = [(r, (r - 1 if r % 2 == 0 else r + 1) % n_ctx) for r in range(n_ctx)]
     partner, neighbour = send(own, swap), send(edge, ring)
-    x = x + sum(send(x, [(r, r + 2 * y) for r in (0, 8)]) for y in (1, 2, 3))
-    x, got1, grad, partner, neighbour = lax.optimization_barrier(
-        (x, got1, grad, partner, neighbour)
+    spread = [send(x, [(r, r + 2 * y) for r in (0, 8)]) for y in (1, 2, 3)]
+    (send2,) = on_chip(select_kernel, "select", [stored((8, 2, 7, 16, width), BF16)], table, got1)
+    x = after(x, send2) + sum(spread)
+    x, send2, got1, grad, partner, neighbour = lax.optimization_barrier(
+        (x, send2, got1, grad, partner, neighbour)
     )
     upstream = lax.ppermute(grad, "segment", [((s + 1) % n_seg, s) for s in range(n_seg)])
-    (send2,) = on_chip(select_kernel, "select", [stored((8, 2, 7, 16, width), BF16)], table, got1)
     got2 = exchange_half(send2)
     x = x + send(x, [(r, r + 1) for r in range(0, n_ctx, 2)])
     (stats,) = on_chip(stats_kernel, "row_stats", [stored((2, 8, BLK), F32)], info, x, got1)

time: 159 us -> 158 us (level)
  waiting for transfers between devices: 60.4 us -> 58.2 us
    ppermute x19, waiting for transfers between devices: 50.7 us -> 40 us  [send(): return lax.ppermute(block, 'ctx', pairs)]
    all_to_all x2, waiting for transfers between devices: 8.46 us -> 17 us  [exchange(): return lax.all_to_all(x, 'ctx', 0, 0, tiled=True)]
  transfers between devices with their start and end apart: 26 -> 26, of which waited for: 13 -> 13; matrix products, arithmetic and copies ran while one was open for 4% -> 4% of each run, Pallas kernels for 5% -> 6%
where the time goes in v3:
time: 158 us; the launch traced here: 157 us
  waiting for transfers between devices  58.2 us (37%)
  starting transfers between devices  57.1 us (36%)
  Pallas kernels  31.5 us (20%)
  other arithmetic  5.92 us (4%)
  local copies, waits for them, and re-layouts  2.57 us (2%)
  between operations  1.61 us (1%)
    ppermute x19, waiting for transfers between devices, send(): return lax.ppermute(block, 'ctx', pairs)  40 us
    ppermute x19, starting transfers between devices, send(): return lax.ppermute(block, 'ctx', pairs)  30.3 us
    all_to_all x2, waiting for transfers between devices, exchange(): return lax.all_to_all(x, 'ctx', 0, 0, tiled=True)  17 us
    pallas_call x1, Pallas kernels, attend(): pl.pallas_call(attend_kernel, grid_spec=pltpu.PrefetchScalarGridSpec(num_...  14.4 us
    pallas_call x5, Pallas kernels, on_chip(): pl.pallas_call(kernel, in_specs=[pl.BlockSpec(memory_space=pltpu.SMEM)] +...  11.2 us
    all_to_all x2, starting transfers between devices, exchange(): return lax.all_to_all(x, 'ctx', 0, 0, tiled=True)  8.61 us
    all_to_all x2, starting transfers between devices, exchange_half(): return lax.all_to_all(x, 'ctx', 0, 0, tiled=True, axis_index_groups=halves)  8.31 us
    ppermute x1, starting transfers between devices, per_device(): lax.ppermute(g0, both, [(flat(s + 1, 0), flat(s, 0)) for s in range(n_seg)])  6.22 us
  transfers between devices with their start and end apart: 26, of which 13 were waited for; matrix products, arithmetic and copies ran while one was open for 4% of the time, Pallas kernels for 6%

profile of v3, /device:TPU:0, one launch (start us, length us, event | category | flops | bytes accessed | tf_op | source)
XLA Modules:
  0.0 156.9 jit_solution(17209847605952345172)
XLA Ops:
  1.3 0.1 pad_add_fusion.1.info_ref
  1.4 3.6 %pack.1 = (bf16[2,256,512]{2,1,0:T(8,128)(2,1)}, bf16[16,2,2,16,512]{4,3,2,1,0:T(8,128)(2,1)}, bf16[2,128,512]{2,1,0:T(8,128)(2,1)}, bf16[128,1024]{1,0:T(8,128)...) custom-call(s32[2]{0:T(128)S(1)} %pad_add_fusion.1.info_ref, ...), custom_call_target="tpu_custom_call" | custom-call | tf_op jit(solution)/shard_map/pack/pallas_call | solution.py:81
  4.9 6.2 %collective-permute-start.1 = (bf16[128,1024]{1,0:T(8,128)(2,1)}, bf16[128,1024]{1,0:T(8,128)(2,1)S(1)}, u32[]{:S(2)}, u32[]{:S(2)}) collective-permute-start(bf16[128,1024]{1,0:T(8,128)(2,1)} %get-tuple-element.47), channel_id=1, source_target_pairs={{16,0},{32,16},{48,32},{64,48},{80,64},{96,80},{112,96},{0,112}} | collective-permute-start | bytes 786440 | tf_op jit(solution)/shard_map/ppermute | solution.py:395
  11.1 2.8 %collective-permute-start.2 = (bf16[128,1024]{1,0:T(8,128)(2,1)}, bf16[128,1024]{1,0:T(8,128)(2,1)S(1)}, u32[]{:S(2)}, u32[]{:S(2)}) collective-permute-start(bf16[128,1024]{1,0:T(8,128)(2,1)} %get-tuple-element.48), channel_id=1, source_target_pairs={{16,8},{32,24},{48,40},{64,56},{80,72},{96,88},{112,104},{0,120}} | collective-permute-start | bytes 786440 | tf_op jit(solution)/shard_map/ppermute | solution.py:396
  14.0 1.3 collective-permute-start
  15.3 3.7 %all-to-all-start = ((bf16[16,2,2,16,512]{4,3,2,1,0:T(8,128)(2,1)}), bf16[16,2,2,16,512]{4,3,2,1,0:T(8,128)(2,1)S(1)}, u32[]{:S(2)}, u32[]{:S(2)}) async-start(bf16[16,2,2,16,512]{4,3,2,1,0:T(8,128)(2,1)} %get-tuple-element.49), calls=%async_computation | async-start | bytes 2097152 | tf_op jit(solution)/shard_map/all_to_all | solution.py:383
  18.9 0.0 copy-start.7
  19.0 0.4 collective-permute-done
  19.5 0.1 pad_maximum_fusion
  19.5 4.6 %collective-permute-start.5 = (bf16[2,128,1024]{2,1,0:T(8,128)(2,1)S(1)}, bf16[2,128,1024]{2,1,0:T(8,128)(2,1)S(1)}, u32[]{:S(2)}, u32[]{:S(2)}) collective-permute-start(bf16[2,128,1024]{2,1,0:T(8,128)(2,1)S(1)} %pad_maximum_fusion), channel_id=1, source_target_pairs={{0,6},{8,14},{16,22},{24,30},{32,38},{40,46},{48,54},{56,62},{64,7... | collective-permute-start | bytes 1572872 | tf_op jit(solution)/shard_map/ppermute | solution.py:349
  24.1 1.3 collective-permute-start.4
  25.5 2.1 %collective-permute-start.3 = (bf16[2,128,1024]{2,1,0:T(8,128)(2,1)S(1)}, bf16[2,128,1024]{2,1,0:T(8,128)(2,1)}, u32[]{:S(2)}, u32[]{:S(2)}) collective-permute-start(bf16[2,128,1024]{2,1,0:T(8,128)(2,1)S(1)} %pad_maximum_fusion), channel_id=1, source_target_pairs={{0,2},{8,10},{16,18},{24,26},{32,34},{40,42},{48,50},{56,58},{64,6... | collective-permute-start | bytes 1572872 | tf_op jit(solution)/shard_map/ppermute | solution.py:349
  27.6 0.7 collective-permute-start.7
  28.2 0.1 copy.11
  28.3 0.1 reshape.12
  28.4 0.1 pad_dynamic-slice_fusion
  28.5 0.1 reshape.13
  28.6 0.1 pad_add_fusion.table_ref
  28.6 8.6 %all-to-all-done.got_ref = bf16[16,2,2,16,512]{4,3,2,1,0:T(8,128)(2,1)S(1)} async-done(((bf16[16,2,2,16,512]{4,3,2,1,0:T(8,128)(2,1)}), bf16[16,2,2,16,512]{4,3,2,1,0:T(8,128)(2,1)S(1)}, u32[]{:S(2)}, u32[]{:S(2)}) %all-to-all-start) | async-done | bytes 1048608 | tf_op jit(solution)/shard_map/all_to_all | solution.py:383
  37.2 2.2 %select.6 = bf16[8,2,7,16,512]{4,3,2,1,0:T(8,128)(2,1)} custom-call(s32[57]{0:T(128)S(1)} %pad_add_fusion.table_ref, bf16[16,2,2,16,512]{4,3,2,1,0:T(8,128)(2,1)S(1)} %all-to-all-done.got_ref), custom_call_target="tpu_custom_call" | custom-call | tf_op jit(solution)/shard_map/select/pallas_call | solution.py:33
  39.4 0.4 collective-permute-done.4
  39.8 5.6 %collective-permute-done.3 = bf16[2,128,1024]{2,1,0:T(8,128)(2,1)} collective-permute-done((bf16[2,128,1024]{2,1,0:T(8,128)(2,1)S(1)}, bf16[2,128,1024]{2,1,0:T(8,128)(2,1)}, u32[]{:S(2)}, u32[]{:S(2)}) %collective-permute-start.3) | collective-permute-done | bytes 524320 | tf_op jit(solution)/shard_map/ppermute | solution.py:349
  45.4 1.2 add_add_fusion
  46.6 0.0 copy-start.2
  46.6 0.0 copy-start.8
  46.7 0.7 copy-done.8
  47.4 3.9 %all-to-all-start.1 = ((bf16[8,2,7,16,512]{4,3,2,1,0:T(8,128)(2,1)}), bf16[8,2,7,16,512]{4,3,2,1,0:T(8,128)(2,1)S(1)}, u32[]{:S(2)}, u32[]{:S(2)}) async-start(bf16[8,2,7,16,512]{4,3,2,1,0:T(8,128)(2,1)} %select.6), calls=%async_computation.1 | async-start | bytes 3670016 | tf_op jit(solution)/shard_map/all_to_all | solution.py:386
  51.3 0.8 collective-permute-start.8
  52.1 2.1 %collective-permute-start.9 = (bf16[2,128,1024]{2,1,0:T(8,128)(2,1)S(1)}, bf16[2,128,1024]{2,1,0:T(8,128)(2,1)S(1)}, u32[]{:S(2)}, u32[]{:S(2)}) collective-permute-start(bf16[2,128,1024]{2,1,0:T(8,128)(2,1)S(1)} %add_add_fusion), channel_id=1, source_target_pairs={{0,1},{2,3},{4,5},{6,7},{8,9},{10,11},{12,13},{14,15},{16,17},{18,... | collective-permute-start | bytes 1572872 | tf_op jit(solution)/shard_map/ppermute | solution.py:349
  54.3 1.5 collective-permute-done.9
  55.8 1.2 add.66.x_ref
  57.0 1.9 %row_stats.1 = f32[2,8,128]{2,1,0:T(8,128)} custom-call(s32[2]{0:T(128)S(1)} %pad_add_fusion.1.info_ref, bf16[2,128,1024]{2,1,0:T(8,128)(2,1)S(1)} %add.66.x_ref, bf16[16,2,2,16,512]{4,3,2,1,0:T(8,128)(2,1)S(1)} %all-to-all-done.got_ref), custom_call_target="tpu_custom_call" | custom-call | tf_op jit(solution)/shard_map/row_stats/pallas_call | solution.py:33
  58.9 0.4 collective-permute-start.10
  59.2 1.0 collective-permute-done.10
  60.3 0.8 fusion
  61.1 2.9 %collective-permute-start.13 = (f32[2,8,128]{2,1,0:T(8,128)S(1)}, f32[2,8,128]{2,1,0:T(8,128)S(1)}, u32[]{:S(2)}, u32[]{:S(2)}) collective-permute-start(f32[2,8,128]{2,1,0:T(8,128)S(1)} %pad_maximum_fusion.1), channel_id=1, source_target_pairs={{0,6},{1,7},{2,0},{3,1},{4,2},{5,3},{6,4},{7,5},{8,14},{9,15},{10,... | collective-permute-start | bytes 24584 | tf_op jit(solution)/shard_map/ppermute | solution.py:349
  64.0 0.9 collective-permute-start.12
  64.9 0.9 collective-permute-start.11
  65.7 8.7 %collective-permute-done.13 = f32[2,8,128]{2,1,0:T(8,128)S(1)} collective-permute-done((f32[2,8,128]{2,1,0:T(8,128)S(1)}, f32[2,8,128]{2,1,0:T(8,128)S(1)}, u32[]{:S(2)}, u32[]{:S(2)}) %collective-permute-start.13) | collective-permute-done | bytes 8224 | tf_op jit(solution)/shard_map/ppermute | solution.py:349
  74.4 1.5 collective-permute-done.12
  75.9 1.2 collective-permute-done.8.do_ref
  77.1 14.4 %attend.1 = (bf16[256,2048]{1,0:T(8,128)(2,1)}, f32[2,256,512]{2,1,0:T(8,128)}, bf16[2,128,512]{2,1,0:T(8,128)(2,1)}, bf16[2,128,512]{2,1,0:T(8,128)(2,1)}, bf16[8,2,7,16,512]{4,3,2,1,0:T(8,128)(2,1)}) custom-call(s32[2]{0:T(128)S(1)} %pad_add_fusion.1.info_ref, bf16[8,256,2048]{2,1,0:T(8,128)(2,1)} %bitcast.14, ...), custom_call_target="tpu_custom_call" | custom-call | flops 4697620480 | bytes 10485760 | tf_op jit(solution)/shard_map/attend/pallas_call | solution.py:226
  91.6 4.4 %all-to-all-start.2 = ((bf16[8,2,7,16,512]{4,3,2,1,0:T(8,128)(2,1)}), bf16[8,2,7,16,512]{4,3,2,1,0:T(8,128)(2,1)S(1)}, u32[]{:S(2)}, u32[]{:S(2)}) async-start(bf16[8,2,7,16,512]{4,3,2,1,0:T(8,128)(2,1)} %get-tuple-element.60), calls=%async_computation.2 | async-start | bytes 3670016 | tf_op jit(solution)/shard_map/all_to_all | solution.py:386
  96.0 3.2 %row_grads.1 = (bf16[128,1024]{1,0:T(8,128)(2,1)}, f32[16,2,2,16,256]{4,3,2,1,0:T(8,128)}) custom-call(s32[2]{0:T(128)S(1)} %pad_add_fusion.1.info_ref, bf16[2,128,1024]{2,1,0:T(8,128)(2,1)S(1)} %add.66.x_ref, bf16[16,2,2,16,512]{4,3,2,1,0:T(8,128)(2,1)S(1)} %all-to-all-done.got_ref, f32[2,8,128]{2,1,0:T(8,128)S(1)} %pad_maximum_fusion.2.st_ref), custom_call_target="tpu_custom_call" | custom-call | tf_op jit(solution)/shard_map/row_grads/pallas_call | solution.py:33
  99.3 1.3 collective-permute-start.15
  100.6 1.2 collective-permute-start.14
  101.8 1.1 collective-permute-done.15
  102.9 1.0 add_convert_fusion.1
  104.0 1.3 collective-permute-start.19
  105.3 1.3 collective-permute-start.18
  106.6 1.3 collective-permute-start.17
  107.9 0.7 collective-permute-start.16
  108.5 17.2 %collective-permute-done.19 = bf16[128,1024]{1,0:T(8,128)(2,1)S(1)} collective-permute-done((bf16[128,1024]{1,0:T(8,128)(2,1)S(1)}, bf16[128,1024]{1,0:T(8,128)(2,1)S(1)}, u32[]{:S(2)}, u32[]{:S(2)}) %collective-permute-start.19) | collective-permute-done | bytes 262176 | tf_op jit(solution)/shard_map/ppermute | solution.py:349
  125.7 0.0 copy-start.4
  125.8 1.5 copy-done.1
  127.3 2.3 %combine.1 = bf16[16,2,2,16,512]{4,3,2,1,0:T(8,128)(2,1)} custom-call(s32[57]{0:T(128)S(1)} %pad_add_fusion.table_ref, bf16[8,2,7,16,512]{4,3,2,1,0:T(8,128)(2,1)S(1)} %all-to-all-done.2.got_ref, f32[16,2,2,16,256]{4,3,2,1,0:T(8,128)S(1)} %copy-done.1), custom_call_target="tpu_custom_call" | custom-call | tf_op jit(solution)/shard_map/combine/pallas_call | solution.py:33
  129.6 4.9 %all-to-all-start.3 = ((bf16[16,2,2,16,512]{4,3,2,1,0:T(8,128)(2,1)}), bf16[16,2,2,16,512]{4,3,2,1,0:T(8,128)(2,1)S(1)}, u32[]{:S(2)}, u32[]{:S(2)}) async-start(bf16[16,2,2,16,512]{4,3,2,1,0:T(8,128)(2,1)} %combine.1), calls=%async_computation.3 | async-start | bytes 2097152 | tf_op jit(solution)/shard_map/all_to_all | solution.py:383
  134.6 1.4 add_convert_fusion.refs_0_
  135.9 1.3 collective-permute-start.20
  137.2 4.8 %collective-permute-start.21 = (bf16[2,128,512]{2,1,0:T(8,128)(2,1)S(1)}, bf16[2,128,512]{2,1,0:T(8,128)(2,1)S(1)}, u32[]{:S(2)}, u32[]{:S(2)}) collective-permute-start(bf16[2,128,512]{2,1,0:T(8,128)(2,1)S(1)} %copy-done.9), channel_id=1, source_target_pairs={{0,15},{1,2},{2,1},{3,4},{4,3},{5,6},{6,5},{7,8},{8,7},{9,10},{10,... | collective-permute-start | bytes 786440 | tf_op jit(solution)/shard_map/ppermute | solution.py:349
  142.0 2.4 %place.1 = bf16[256,2048]{1,0:T(8,128)(2,1)} custom-call(s32[2]{0:T(128)S(1)} %pad_add_fusion.1.info_ref, bf16[128,1024]{1,0:T(8,128)(2,1)S(1)} %add_convert_fusion.refs_0_, bf16[128,1024]{1,0:T(8,128)(2,1)S(1)} %collective-permute-done.20.refs_1_, bf16[256,2048]{1,0:T(8,128)(2,1)} %get-tuple-element.79.refs_2_), custom_call_target="tpu_custom_call", output_to_operand_aliasing={{}: (3, {})} | custom-call | tf_op jit(solution)/shard_map/place/pallas_call | solution.py:315
  144.4 8.5 %all-to-all-done.3.got_ref = bf16[16,2,2,16,512]{4,3,2,1,0:T(8,128)(2,1)S(1)} async-done(((bf16[16,2,2,16,512]{4,3,2,1,0:T(8,128)(2,1)}), bf16[16,2,2,16,512]{4,3,2,1,0:T(8,128)(2,1)S(1)}, u32[]{:S(2)}, u32[]{:S(2)}) %all-to-all-start.3) | async-done | bytes 1048608 | tf_op jit(solution)/shard_map/all_to_all | solution.py:383
  152.9 2.5 %collective-permute-done.21.winn_ref = bf16[2,128,512]{2,1,0:T(8,128)(2,1)S(1)} collective-permute-done((bf16[2,128,512]{2,1,0:T(8,128)(2,1)S(1)}, bf16[2,128,512]{2,1,0:T(8,128)(2,1)S(1)}, u32[]{:S(2)}, u32[]{:S(2)}) %collective-permute-start.21) | collective-permute-done | bytes 262176 | tf_op jit(solution)/shard_map/ppermute | solution.py:349
  155.3 1.6 finish.1
  (33 shorter events, 0.2 us)
Async XLA Ops:
  4.9 14.5 %copy-start.6 = (bf16[128,1024]{1,0:T(8,128)(2,1)S(1)}, bf16[128,1024]{1,0:T(8,128)(2,1)}, u32[]{:S(2)}) copy-start(bf16[128,1024]{1,0:T(8,128)(2,1)} %get-tuple-element.45) | copy-start | bytes 786436
  4.9 14.1 %collective-permute-start.1 = (bf16[128,1024]{1,0:T(8,128)(2,1)}, bf16[128,1024]{1,0:T(8,128)(2,1)S(1)}, u32[]{:S(2)}, u32[]{:S(2)}) collective-permute-start(bf16[128,1024]{1,0:T(8,128)(2,1)} %get-tuple-element.47), channel_id=1, source_target_pairs={{16,0},{32,16},{48,32},{64,48},{80,64},{96,80},{112,96},{0,112}} | collective-permute-start | bytes 786440 | tf_op jit(solution)/shard_map/ppermute | solution.py:395
  11.1 7.8 %collective-permute-start.2 = (bf16[128,1024]{1,0:T(8,128)(2,1)}, bf16[128,1024]{1,0:T(8,128)(2,1)S(1)}, u32[]{:S(2)}, u32[]{:S(2)}) collective-permute-start(bf16[128,1024]{1,0:T(8,128)(2,1)} %get-tuple-element.48), channel_id=1, source_target_pairs={{16,8},{32,24},{48,40},{64,56},{80,72},{96,88},{112,104},{0,120}} | collective-permute-start | bytes 786440 | tf_op jit(solution)/shard_map/ppermute | solution.py:396
  14.0 5.5 %collective-permute-start = (bf16[128,1024]{1,0:T(8,128)(2,1)}, bf16[128,1024]{1,0:T(8,128)(2,1)S(1)}, u32[]{:S(2)}, u32[]{:S(2)}) collective-permute-start(bf16[128,1024]{1,0:T(8,128)(2,1)} %get-tuple-element.46), channel_id=1, source_target_pairs={{0,8},{16,24},{32,40},{48,56},{64,72},{80,88},{96,104},{112,120}} | collective-permute-start | bytes 786440 | tf_op jit(solution)/shard_map/ppermute | solution.py:349
  15.3 21.9 %all-to-all-start = ((bf16[16,2,2,16,512]{4,3,2,1,0:T(8,128)(2,1)}), bf16[16,2,2,16,512]{4,3,2,1,0:T(8,128)(2,1)S(1)}, u32[]{:S(2)}, u32[]{:S(2)}) async-start(bf16[16,2,2,16,512]{4,3,2,1,0:T(8,128)(2,1)} %get-tuple-element.49), calls=%async_computation | async-start | bytes 2097152 | tf_op jit(solution)/shard_map/all_to_all | solution.py:383
  18.9 9.3 %copy-start.7 = (s32[32,3]{0,1:T(4,128)S(1)}, s32[32,3]{0,1:T(4,128)}, u32[]{:S(2)}) copy-start(s32[32,3]{0,1:T(4,128)} %param.11) | copy-start | bytes 1156
  19.5 19.8 %collective-permute-start.5 = (bf16[2,128,1024]{2,1,0:T(8,128)(2,1)S(1)}, bf16[2,128,1024]{2,1,0:T(8,128)(2,1)S(1)}, u32[]{:S(2)}, u32[]{:S(2)}) collective-permute-start(bf16[2,128,1024]{2,1,0:T(8,128)(2,1)S(1)} %pad_maximum_fusion), channel_id=1, source_target_pairs={{0,6},{8,14},{16,22},{24,30},{32,38},{40,46},{48,54},{56,62},{64,7... | collective-permute-start | bytes 1572872 | tf_op jit(solution)/shard_map/ppermute | solution.py:349
  24.1 15.7 %collective-permute-start.4 = (bf16[2,128,1024]{2,1,0:T(8,128)(2,1)S(1)}, bf16[2,128,1024]{2,1,0:T(8,128)(2,1)S(1)}, u32[]{:S(2)}, u32[]{:S(2)}) collective-permute-start(bf16[2,128,1024]{2,1,0:T(8,128)(2,1)S(1)} %pad_maximum_fusion), channel_id=1, source_target_pairs={{0,4},{8,12},{16,20},{24,28},{32,36},{40,44},{48,52},{56,60},{64,6... | collective-permute-start | bytes 1572872 | tf_op jit(solution)/shard_map/ppermute | solution.py:349
  25.5 20.0 %collective-permute-start.3 = (bf16[2,128,1024]{2,1,0:T(8,128)(2,1)S(1)}, bf16[2,128,1024]{2,1,0:T(8,128)(2,1)}, u32[]{:S(2)}, u32[]{:S(2)}) collective-permute-start(bf16[2,128,1024]{2,1,0:T(8,128)(2,1)S(1)} %pad_maximum_fusion), channel_id=1, source_target_pairs={{0,2},{8,10},{16,18},{24,26},{32,34},{40,42},{48,50},{56,58},{64,6... | collective-permute-start | bytes 1572872 | tf_op jit(solution)/shard_map/ppermute | solution.py:349
  27.6 19.1 %collective-permute-start.6 = (bf16[2,256,512]{2,1,0:T(8,128)(2,1)}, bf16[2,256,512]{2,1,0:T(8,128)(2,1)}, u32[]{:S(2)}, u32[]{:S(2)}) collective-permute-start(bf16[2,256,512]{2,1,0:T(8,128)(2,1)} %get-tuple-element.51.own_ref), channel_id=1, source_target_pairs={{0,1},{1,0},{2,3},{3,2},{4,5},{5,4},{6,7},{7,6},{8,9},{9,8},{10,11... | collective-permute-start | bytes 1572872 | tf_op jit(solution)/shard_map/ppermute | solution.py:349
  27.6 19.1 %collective-permute-start.7 = (bf16[2,128,512]{2,1,0:T(8,128)(2,1)}, bf16[2,128,512]{2,1,0:T(8,128)(2,1)S(1)}, u32[]{:S(2)}, u32[]{:S(2)}) collective-permute-start(bf16[2,128,512]{2,1,0:T(8,128)(2,1)} %get-tuple-element.52), channel_id=1, source_target_pairs={{0,15},{1,2},{2,1},{3,4},{4,3},{5,6},{6,5},{7,8},{8,7},{9,10},{10,... | collective-permute-start | bytes 786440 | tf_op jit(solution)/shard_map/ppermute | solution.py:349
  46.6 7.7 %copy-start.2 = (bf16[2,128,1024]{2,1,0:T(8,128)(2,1)}, bf16[2,128,1024]{2,1,0:T(8,128)(2,1)S(1)}, u32[]{:S(2)}) copy-start(bf16[2,128,1024]{2,1,0:T(8,128)(2,1)S(1)} %add_add_fusion) | copy-start | bytes 1572868
  46.6 0.8 copy-start.8
  47.4 28.5 %all-to-all-start.1 = ((bf16[8,2,7,16,512]{4,3,2,1,0:T(8,128)(2,1)}), bf16[8,2,7,16,512]{4,3,2,1,0:T(8,128)(2,1)S(1)}, u32[]{:S(2)}, u32[]{:S(2)}) async-start(bf16[8,2,7,16,512]{4,3,2,1,0:T(8,128)(2,1)} %select.6), calls=%async_computation.1 | async-start | bytes 3670016 | tf_op jit(solution)/shard_map/all_to_all | solution.py:386
  51.3 25.9 %collective-permute-start.8 = (bf16[256,2048]{1,0:T(8,128)(2,1)}, bf16[256,2048]{1,0:T(8,128)(2,1)}, u32[]{:S(2)}, u32[]{:S(2)}) collective-permute-start(bf16[256,2048]{1,0:T(8,128)(2,1)} %bitcast.19), channel_id=1, source_target_pairs={{16,0},{32,16},{48,32},{64,48},{80,64},{96,80},{112,96},{0,112},{1... | collective-permute-start | bytes 3145736 | tf_op jit(solution)/shard_map/ppermute | solution.py:408
  52.1 3.6 %collective-permute-start.9 = (bf16[2,128,1024]{2,1,0:T(8,128)(2,1)S(1)}, bf16[2,128,1024]{2,1,0:T(8,128)(2,1)S(1)}, u32[]{:S(2)}, u32[]{:S(2)}) collective-permute-start(bf16[2,128,1024]{2,1,0:T(8,128)(2,1)S(1)} %add_add_fusion), channel_id=1, source_target_pairs={{0,1},{2,3},{4,5},{6,7},{8,9},{10,11},{12,13},{14,15},{16,17},{18,... | collective-permute-start | bytes 1572872 | tf_op jit(solution)/shard_map/ppermute | solution.py:349
  58.9 1.4 collective-permute-start.10
  61.1 13.3 %collective-permute-start.13 = (f32[2,8,128]{2,1,0:T(8,128)S(1)}, f32[2,8,128]{2,1,0:T(8,128)S(1)}, u32[]{:S(2)}, u32[]{:S(2)}) collective-permute-start(f32[2,8,128]{2,1,0:T(8,128)S(1)} %pad_maximum_fusion.1), channel_id=1, source_target_pairs={{0,6},{1,7},{2,0},{3,1},{4,2},{5,3},{6,4},{7,5},{8,14},{9,15},{10,... | collective-permute-start | bytes 24584 | tf_op jit(solution)/shard_map/ppermute | solution.py:349
  64.0 11.9 %collective-permute-start.12 = (f32[2,8,128]{2,1,0:T(8,128)S(1)}, f32[2,8,128]{2,1,0:T(8,128)S(1)}, u32[]{:S(2)}, u32[]{:S(2)}) collective-permute-start(f32[2,8,128]{2,1,0:T(8,128)S(1)} %pad_maximum_fusion.1), channel_id=1, source_target_pairs={{0,4},{1,5},{2,6},{3,7},{4,0},{5,1},{6,2},{7,3},{8,12},{9,13},{10,... | collective-permute-start | bytes 24584 | tf_op jit(solution)/shard_map/ppermute | solution.py:349
  64.9 11.0 %collective-permute-start.11 = (f32[2,8,128]{2,1,0:T(8,128)S(1)}, f32[2,8,128]{2,1,0:T(8,128)S(1)}, u32[]{:S(2)}, u32[]{:S(2)}) collective-permute-start(f32[2,8,128]{2,1,0:T(8,128)S(1)} %pad_maximum_fusion.1), channel_id=1, source_target_pairs={{0,2},{1,3},{2,4},{3,5},{4,6},{5,7},{6,0},{7,1},{8,10},{9,11},{10,... | collective-permute-start | bytes 24584 | tf_op jit(solution)/shard_map/ppermute | solution.py:349
  91.6 34.2 %all-to-all-start.2 = ((bf16[8,2,7,16,512]{4,3,2,1,0:T(8,128)(2,1)}), bf16[8,2,7,16,512]{4,3,2,1,0:T(8,128)(2,1)S(1)}, u32[]{:S(2)}, u32[]{:S(2)}) async-start(bf16[8,2,7,16,512]{4,3,2,1,0:T(8,128)(2,1)} %get-tuple-element.60), calls=%async_computation.2 | async-start | bytes 3670016 | tf_op jit(solution)/shard_map/all_to_all | solution.py:386
  99.3 3.6 %collective-permute-start.15 = (bf16[128,1024]{1,0:T(8,128)(2,1)}, bf16[128,1024]{1,0:T(8,128)(2,1)S(1)}, u32[]{:S(2)}, u32[]{:S(2)}) collective-permute-start(bf16[128,1024]{1,0:T(8,128)(2,1)} %get-tuple-element.70), channel_id=1, source_target_pairs={{1,0},{3,2},{5,4},{7,6},{9,8},{11,10},{13,12},{15,14},{17,16},{19,... | collective-permute-start | bytes 786440 | tf_op jit(solution)/shard_map/ppermute | solution.py:349
  100.6 8.0 %collective-permute-start.14 = (bf16[2,128,512]{2,1,0:T(8,128)(2,1)}, bf16[2,128,512]{2,1,0:T(8,128)(2,1)S(1)}, u32[]{:S(2)}, u32[]{:S(2)}) collective-permute-start(bf16[2,128,512]{2,1,0:T(8,128)(2,1)} %get-tuple-element.61), channel_id=1, source_target_pairs={{0,1},{1,0},{2,3},{3,2},{4,5},{5,4},{6,7},{7,6},{8,9},{9,8},{10,11... | collective-permute-start | bytes 786440 | tf_op jit(solution)/shard_map/ppermute | solution.py:349
  104.0 21.8 %collective-permute-start.19 = (bf16[128,1024]{1,0:T(8,128)(2,1)S(1)}, bf16[128,1024]{1,0:T(8,128)(2,1)S(1)}, u32[]{:S(2)}, u32[]{:S(2)}) collective-permute-start(bf16[128,1024]{1,0:T(8,128)(2,1)S(1)} %add_convert_fusion.1), channel_id=1, source_target_pairs={{6,0},{14,1},{22,16},{30,17},{38,32},{46,33},{54,48},{62,49},{70,6... | collective-permute-start | bytes 786440 | tf_op jit(solution)/shard_map/ppermute | solution.py:349
  105.3 20.5 %collective-permute-start.18 = (bf16[128,1024]{1,0:T(8,128)(2,1)S(1)}, bf16[128,1024]{1,0:T(8,128)(2,1)S(1)}, u32[]{:S(2)}, u32[]{:S(2)}) collective-permute-start(bf16[128,1024]{1,0:T(8,128)(2,1)S(1)} %add_convert_fusion.1), channel_id=1, source_target_pairs={{4,0},{12,1},{20,16},{28,17},{36,32},{44,33},{52,48},{60,49},{68,6... | collective-permute-start | bytes 786440 | tf_op jit(solution)/shard_map/ppermute | solution.py:349
  106.6 19.2 %collective-permute-start.17 = (bf16[128,1024]{1,0:T(8,128)(2,1)S(1)}, bf16[128,1024]{1,0:T(8,128)(2,1)S(1)}, u32[]{:S(2)}, u32[]{:S(2)}) collective-permute-start(bf16[128,1024]{1,0:T(8,128)(2,1)S(1)} %add_convert_fusion.1), channel_id=1, source_target_pairs={{2,0},{10,1},{18,16},{26,17},{34,32},{42,33},{50,48},{58,49},{66,6... | collective-permute-start | bytes 786440 | tf_op jit(solution)/shard_map/ppermute | solution.py:349
  107.9 17.9 %collective-permute-start.16 = (bf16[128,1024]{1,0:T(8,128)(2,1)S(1)}, bf16[128,1024]{1,0:T(8,128)(2,1)S(1)}, u32[]{:S(2)}, u32[]{:S(2)}) collective-permute-start(bf16[128,1024]{1,0:T(8,128)(2,1)S(1)} %add_convert_fusion.1), channel_id=1, source_target_pairs={{8,1},{24,17},{40,33},{56,49},{72,65},{88,81},{104,97},{120,113}} | collective-permute-start | bytes 786440 | tf_op jit(solution)/shard_map/ppermute | solution.py:349
  125.7 3.9 %copy-start.3 = (bf16[128,1024]{1,0:T(8,128)(2,1)}, bf16[128,1024]{1,0:T(8,128)(2,1)S(1)}, u32[]{:S(2)}) copy-start(bf16[128,1024]{1,0:T(8,128)(2,1)S(1)} %collective-permute-done.18) | copy-start | bytes 786436
  125.7 3.9 %copy-start.4 = (bf16[128,1024]{1,0:T(8,128)(2,1)}, bf16[128,1024]{1,0:T(8,128)(2,1)S(1)}, u32[]{:S(2)}) copy-start(bf16[128,1024]{1,0:T(8,128)(2,1)S(1)} %collective-permute-done.17) | copy-start | bytes 786436
  125.8 3.8 %copy-start.5 = (bf16[128,1024]{1,0:T(8,128)(2,1)}, bf16[128,1024]{1,0:T(8,128)(2,1)S(1)}, u32[]{:S(2)}) copy-start(bf16[128,1024]{1,0:T(8,128)(2,1)S(1)} %collective-permute-done.16) | copy-start | bytes 786436
  125.8 1.5 copy-start.1
  129.6 7.6 %copy-start.9 = (bf16[2,128,512]{2,1,0:T(8,128)(2,1)S(1)}, bf16[2,128,512]{2,1,0:T(8,128)(2,1)}, u32[]{:S(2)}) copy-start(bf16[2,128,512]{2,1,0:T(8,128)(2,1)} %get-tuple-element.83) | copy-start | bytes 786436
  129.6 23.3 %all-to-all-start.3 = ((bf16[16,2,2,16,512]{4,3,2,1,0:T(8,128)(2,1)}), bf16[16,2,2,16,512]{4,3,2,1,0:T(8,128)(2,1)S(1)}, u32[]{:S(2)}, u32[]{:S(2)}) async-start(bf16[16,2,2,16,512]{4,3,2,1,0:T(8,128)(2,1)} %combine.1), calls=%async_computation.3 | async-start | bytes 2097152 | tf_op jit(solution)/shard_map/all_to_all | solution.py:383
  134.6 20.8 %copy-start = (f32[2,256,512]{2,1,0:T(8,128)S(1)}, f32[2,256,512]{2,1,0:T(8,128)}, u32[]{:S(2)}) copy-start(f32[2,256,512]{2,1,0:T(8,128)} %get-tuple-element.81.own_ref) | copy-start | bytes 3145732
  135.9 6.1 %collective-permute-start.20 = (bf16[128,1024]{1,0:T(8,128)(2,1)S(1)}, bf16[128,1024]{1,0:T(8,128)(2,1)S(1)}, u32[]{:S(2)}, u32[]{:S(2)}) collective-permute-start(bf16[128,1024]{1,0:T(8,128)(2,1)S(1)} %add_convert_fusion.refs_0_), channel_id=1, source_target_pairs={{1,0},{17,16},{33,32},{49,48},{65,64},{81,80},{97,96},{113,112}} | collective-permute-start | bytes 786440 | tf_op jit(solution)/shard_map/ppermute | solution.py:349
  137.2 18.1 %collective-permute-start.21 = (bf16[2,128,512]{2,1,0:T(8,128)(2,1)S(1)}, bf16[2,128,512]{2,1,0:T(8,128)(2,1)S(1)}, u32[]{:S(2)}, u32[]{:S(2)}) collective-permute-start(bf16[2,128,512]{2,1,0:T(8,128)(2,1)S(1)} %copy-done.9), channel_id=1, source_target_pairs={{0,15},{1,2},{2,1},{3,4},{4,3},{5,6},{6,5},{7,8},{8,7},{9,10},{10,... | collective-permute-start | bytes 786440 | tf_op jit(solution)/shard_map/ppermute | solution.py:349

commit v4 on v3

--- a/solution.py
+++ b/solution.py
@@ -423,7 +423,7 @@
     part, row = on_chip(
         row_kernel,
         "row_grads",
-        [stored((BLK, half), BF16), stored((16, 2, 2, 16, 2 * HD), F32)],
+        [stored((BLK, half), BF16), shape((16, 2, 2, 16, 2 * HD), F32)],
         info, x, got1, stats,
     )
     winp, winn = send(winp, swap), send(winn, ring)

time: 158 us -> 158 us (level)
    unnamed x21 -> x23, local copies, waits for them, and re-layouts: 2.33 us -> 3.3 us
where the time goes in v4:
time: 158 us; the launch traced here: 157 us
  waiting for transfers between devices  57.6 us (36%)
  starting transfers between devices  57.1 us (36%)
  Pallas kernels  31.3 us (20%)
  other arithmetic  5.92 us (4%)
  local copies, waits for them, and re-layouts  3.53 us (2%)
  between operations  1.61 us (1%)
    ppermute x19, waiting for transfers between devices, send(): return lax.ppermute(block, 'ctx', pairs)  39.3 us
    ppermute x19, starting transfers between devices, send(): return lax.ppermute(block, 'ctx', pairs)  30.3 us
    all_to_all x2, waiting for transfers between devices, exchange(): return lax.all_to_all(x, 'ctx', 0, 0, tiled=True)  17 us
    pallas_call x1, Pallas kernels, attend(): pl.pallas_call(attend_kernel, grid_spec=pltpu.PrefetchScalarGridSpec(num_...  14.4 us
    pallas_call x5, Pallas kernels, on_chip(): pl.pallas_call(kernel, in_specs=[pl.BlockSpec(memory_space=pltpu.SMEM)] +...  10.9 us
    all_to_all x2, starting transfers between devices, exchange(): return lax.all_to_all(x, 'ctx', 0, 0, tiled=True)  8.62 us
    all_to_all x2, starting transfers between devices, exchange_half(): return lax.all_to_all(x, 'ctx', 0, 0, tiled=True, axis_index_groups=halves)  8.3 us
    ppermute x1, starting transfers between devices, per_device(): lax.ppermute(g0, both, [(flat(s + 1, 0), flat(s, 0)) for s in range(n_seg)])  6.22 us
  transfers between devices with their start and end apart: 26, of which 13 were waited for; matrix products, arithmetic and copies ran while one was open for 4% of the time, Pallas kernels for 6%

profile of v4, /device:TPU:0, one launch (start us, length us, event | category | flops | bytes accessed | tf_op | source)
XLA Modules:
  0.0 157.0 jit_solution(15663977070034894867)
XLA Ops:
  1.3 0.1 pad_add_fusion.1.info_ref
  1.4 3.6 %pack.1 = (bf16[2,256,512]{2,1,0:T(8,128)(2,1)}, bf16[16,2,2,16,512]{4,3,2,1,0:T(8,128)(2,1)}, bf16[2,128,512]{2,1,0:T(8,128)(2,1)}, bf16[128,1024]{1,0:T(8,128)...) custom-call(s32[2]{0:T(128)S(1)} %pad_add_fusion.1.info_ref, ...), custom_call_target="tpu_custom_call" | custom-call | tf_op jit(solution)/shard_map/pack/pallas_call | solution.py:81
  4.9 6.2 %collective-permute-start.1 = (bf16[128,1024]{1,0:T(8,128)(2,1)}, bf16[128,1024]{1,0:T(8,128)(2,1)S(1)}, u32[]{:S(2)}, u32[]{:S(2)}) collective-permute-start(bf16[128,1024]{1,0:T(8,128)(2,1)} %get-tuple-element.47), channel_id=1, source_target_pairs={{16,0},{32,16},{48,32},{64,48},{80,64},{96,80},{112,96},{0,112}} | collective-permute-start | bytes 786440 | tf_op jit(solution)/shard_map/ppermute | solution.py:395
  11.1 2.8 %collective-permute-start.2 = (bf16[128,1024]{1,0:T(8,128)(2,1)}, bf16[128,1024]{1,0:T(8,128)(2,1)S(1)}, u32[]{:S(2)}, u32[]{:S(2)}) collective-permute-start(bf16[128,1024]{1,0:T(8,128)(2,1)} %get-tuple-element.48), channel_id=1, source_target_pairs={{16,8},{32,24},{48,40},{64,56},{80,72},{96,88},{112,104},{0,120}} | collective-permute-start | bytes 786440 | tf_op jit(solution)/shard_map/ppermute | solution.py:396
  14.0 1.3 collective-permute-start
  15.3 3.7 %all-to-all-start = ((bf16[16,2,2,16,512]{4,3,2,1,0:T(8,128)(2,1)}), bf16[16,2,2,16,512]{4,3,2,1,0:T(8,128)(2,1)S(1)}, u32[]{:S(2)}, u32[]{:S(2)}) async-start(bf16[16,2,2,16,512]{4,3,2,1,0:T(8,128)(2,1)} %get-tuple-element.49), calls=%async_computation | async-start | bytes 2097152 | tf_op jit(solution)/shard_map/all_to_all | solution.py:383
  18.9 0.0 copy-start.8
  19.0 0.4 collective-permute-done
  19.5 0.1 pad_maximum_fusion
  19.5 4.6 %collective-permute-start.5 = (bf16[2,128,1024]{2,1,0:T(8,128)(2,1)S(1)}, bf16[2,128,1024]{2,1,0:T(8,128)(2,1)S(1)}, u32[]{:S(2)}, u32[]{:S(2)}) collective-permute-start(bf16[2,128,1024]{2,1,0:T(8,128)(2,1)S(1)} %pad_maximum_fusion), channel_id=1, source_target_pairs={{0,6},{8,14},{16,22},{24,30},{32,38},{40,46},{48,54},{56,62},{64,7... | collective-permute-start | bytes 1572872 | tf_op jit(solution)/shard_map/ppermute | solution.py:349
  24.1 1.3 collective-permute-start.4
  25.5 2.1 %collective-permute-start.3 = (bf16[2,128,1024]{2,1,0:T(8,128)(2,1)S(1)}, bf16[2,128,1024]{2,1,0:T(8,128)(2,1)}, u32[]{:S(2)}, u32[]{:S(2)}) collective-permute-start(bf16[2,128,1024]{2,1,0:T(8,128)(2,1)S(1)} %pad_maximum_fusion), channel_id=1, source_target_pairs={{0,2},{8,10},{16,18},{24,26},{32,34},{40,42},{48,50},{56,58},{64,6... | collective-permute-start | bytes 1572872 | tf_op jit(solution)/shard_map/ppermute | solution.py:349
  27.6 0.7 collective-permute-start.7
  28.3 0.1 copy.11
  28.3 0.1 reshape.12
  28.4 0.1 pad_dynamic-slice_fusion
  28.5 0.1 reshape.13
  28.6 0.1 pad_add_fusion.table_ref
  28.7 8.6 %all-to-all-done.got_ref = bf16[16,2,2,16,512]{4,3,2,1,0:T(8,128)(2,1)S(1)} async-done(((bf16[16,2,2,16,512]{4,3,2,1,0:T(8,128)(2,1)}), bf16[16,2,2,16,512]{4,3,2,1,0:T(8,128)(2,1)S(1)}, u32[]{:S(2)}, u32[]{:S(2)}) %all-to-all-start) | async-done | bytes 1048608 | tf_op jit(solution)/shard_map/all_to_all | solution.py:383
  37.2 2.2 %select.6 = bf16[8,2,7,16,512]{4,3,2,1,0:T(8,128)(2,1)} custom-call(s32[57]{0:T(128)S(1)} %pad_add_fusion.table_ref, bf16[16,2,2,16,512]{4,3,2,1,0:T(8,128)(2,1)S(1)} %all-to-all-done.got_ref), custom_call_target="tpu_custom_call" | custom-call | tf_op jit(solution)/shard_map/select/pallas_call | solution.py:33
  39.4 0.4 collective-permute-done.4
  39.8 5.6 %collective-permute-done.3 = bf16[2,128,1024]{2,1,0:T(8,128)(2,1)} collective-permute-done((bf16[2,128,1024]{2,1,0:T(8,128)(2,1)S(1)}, bf16[2,128,1024]{2,1,0:T(8,128)(2,1)}, u32[]{:S(2)}, u32[]{:S(2)}) %collective-permute-start.3) | collective-permute-done | bytes 524320 | tf_op jit(solution)/shard_map/ppermute | solution.py:349
  45.4 1.2 add_add_fusion
  46.6 0.0 copy-start.9
  46.7 0.7 copy-done.9
  47.4 3.9 %all-to-all-start.1 = ((bf16[8,2,7,16,512]{4,3,2,1,0:T(8,128)(2,1)}), bf16[8,2,7,16,512]{4,3,2,1,0:T(8,128)(2,1)S(1)}, u32[]{:S(2)}, u32[]{:S(2)}) async-start(bf16[8,2,7,16,512]{4,3,2,1,0:T(8,128)(2,1)} %select.6), calls=%async_computation.1 | async-start | bytes 3670016 | tf_op jit(solution)/shard_map/all_to_all | solution.py:386
  51.3 0.8 collective-permute-start.8
  52.1 2.1 %collective-permute-start.9 = (bf16[2,128,1024]{2,1,0:T(8,128)(2,1)S(1)}, bf16[2,128,1024]{2,1,0:T(8,128)(2,1)S(1)}, u32[]{:S(2)}, u32[]{:S(2)}) collective-permute-start(bf16[2,128,1024]{2,1,0:T(8,128)(2,1)S(1)} %add_add_fusion), channel_id=1, source_target_pairs={{0,1},{2,3},{4,5},{6,7},{8,9},{10,11},{12,13},{14,15},{16,17},{18,... | collective-permute-start | bytes 1572872 | tf_op jit(solution)/shard_map/ppermute | solution.py:349
  54.3 1.5 collective-permute-done.9
  55.8 1.2 add.66.x_ref
  57.0 1.9 %row_stats.1 = f32[2,8,128]{2,1,0:T(8,128)} custom-call(s32[2]{0:T(128)S(1)} %pad_add_fusion.1.info_ref, bf16[2,128,1024]{2,1,0:T(8,128)(2,1)S(1)} %add.66.x_ref, bf16[16,2,2,16,512]{4,3,2,1,0:T(8,128)(2,1)S(1)} %all-to-all-done.got_ref), custom_call_target="tpu_custom_call" | custom-call | tf_op jit(solution)/shard_map/row_stats/pallas_call | solution.py:33
  58.9 0.4 collective-permute-start.10
  59.2 1.0 collective-permute-done.10
  60.3 0.8 fusion
  61.1 2.9 %collective-permute-start.13 = (f32[2,8,128]{2,1,0:T(8,128)S(1)}, f32[2,8,128]{2,1,0:T(8,128)S(1)}, u32[]{:S(2)}, u32[]{:S(2)}) collective-permute-start(f32[2,8,128]{2,1,0:T(8,128)S(1)} %pad_maximum_fusion.1), channel_id=1, source_target_pairs={{0,6},{1,7},{2,0},{3,1},{4,2},{5,3},{6,4},{7,5},{8,14},{9,15},{10,... | collective-permute-start | bytes 24584 | tf_op jit(solution)/shard_map/ppermute | solution.py:349
  64.0 0.9 collective-permute-start.12
  64.9 0.9 collective-permute-start.11
  65.7 8.7 %collective-permute-done.13 = f32[2,8,128]{2,1,0:T(8,128)S(1)} collective-permute-done((f32[2,8,128]{2,1,0:T(8,128)S(1)}, f32[2,8,128]{2,1,0:T(8,128)S(1)}, u32[]{:S(2)}, u32[]{:S(2)}) %collective-permute-start.13) | collective-permute-done | bytes 8224 | tf_op jit(solution)/shard_map/ppermute | solution.py:349
  74.4 1.5 collective-permute-done.12
  75.9 1.2 collective-permute-done.8.do_ref
  77.2 14.4 %attend.1 = (bf16[256,2048]{1,0:T(8,128)(2,1)}, f32[2,256,512]{2,1,0:T(8,128)}, bf16[2,128,512]{2,1,0:T(8,128)(2,1)}, bf16[2,128,512]{2,1,0:T(8,128)(2,1)}, bf16[8,2,7,16,512]{4,3,2,1,0:T(8,128)(2,1)}) custom-call(s32[2]{0:T(128)S(1)} %pad_add_fusion.1.info_ref, bf16[8,256,2048]{2,1,0:T(8,128)(2,1)} %bitcast.14, ...), custom_call_target="tpu_custom_call" | custom-call | flops 4697620480 | bytes 10485760 | tf_op jit(solution)/shard_map/attend/pallas_call | solution.py:226
  91.6 4.4 %all-to-all-start.2 = ((bf16[8,2,7,16,512]{4,3,2,1,0:T(8,128)(2,1)}), bf16[8,2,7,16,512]{4,3,2,1,0:T(8,128)(2,1)S(1)}, u32[]{:S(2)}, u32[]{:S(2)}) async-start(bf16[8,2,7,16,512]{4,3,2,1,0:T(8,128)(2,1)} %get-tuple-element.60), calls=%async_computation.2 | async-start | bytes 3670016 | tf_op jit(solution)/shard_map/all_to_all | solution.py:386
  96.1 2.9 %row_grads.1 = (bf16[128,1024]{1,0:T(8,128)(2,1)}, f32[16,2,2,16,256]{4,3,2,1,0:T(8,128)S(1)}) custom-call(s32[2]{0:T(128)S(1)} %pad_add_fusion.1.info_ref, bf16[2,128,1024]{2,1,0:T(8,128)(2,1)S(1)} %add.66.x_ref, bf16[16,2,2,16,512]{4,3,2,1,0:T(8,128)(2,1)S(1)} %all-to-all-done.got_ref, f32[2,8,128]{2,1,0:T(8,128)S(1)} %pad_maximum_fusion.2.st_ref), custom_call_target="tpu_custom_call" | custom-call | tf_op jit(solution)/shard_map/row_grads/pallas_call | solution.py:33
  99.0 1.0 copy-done.1
  99.9 1.3 collective-permute-start.15
  101.2 1.2 collective-permute-start.14
  102.4 1.1 collective-permute-done.15
  103.5 1.0 add_convert_fusion.1
  104.6 1.3 collective-permute-start.19
  105.9 1.3 collective-permute-start.18
  107.2 1.3 collective-permute-start.17
  108.5 0.7 collective-permute-start.16
  109.2 16.6 %collective-permute-done.19 = bf16[128,1024]{1,0:T(8,128)(2,1)S(1)} collective-permute-done((bf16[128,1024]{1,0:T(8,128)(2,1)S(1)}, bf16[128,1024]{1,0:T(8,128)(2,1)S(1)}, u32[]{:S(2)}, u32[]{:S(2)}) %collective-permute-start.19) | collective-permute-done | bytes 262176 | tf_op jit(solution)/shard_map/ppermute | solution.py:349
  125.8 0.0 copy-start.5
  125.8 1.5 copy-done.2
  127.3 2.3 %combine.1 = bf16[16,2,2,16,512]{4,3,2,1,0:T(8,128)(2,1)} custom-call(s32[57]{0:T(128)S(1)} %pad_add_fusion.table_ref, bf16[8,2,7,16,512]{4,3,2,1,0:T(8,128)(2,1)S(1)} %all-to-all-done.2.got_ref, f32[16,2,2,16,256]{4,3,2,1,0:T(8,128)S(1)} %copy-done.2), custom_call_target="tpu_custom_call" | custom-call | tf_op jit(solution)/shard_map/combine/pallas_call | solution.py:33
  129.6 5.0 %all-to-all-start.3 = ((bf16[16,2,2,16,512]{4,3,2,1,0:T(8,128)(2,1)}), bf16[16,2,2,16,512]{4,3,2,1,0:T(8,128)(2,1)S(1)}, u32[]{:S(2)}, u32[]{:S(2)}) async-start(bf16[16,2,2,16,512]{4,3,2,1,0:T(8,128)(2,1)} %combine.1), calls=%async_computation.3 | async-start | bytes 2097152 | tf_op jit(solution)/shard_map/all_to_all | solution.py:383
  134.6 1.4 add_convert_fusion.refs_0_
  136.0 1.3 collective-permute-start.20
  137.3 4.8 %collective-permute-start.21 = (bf16[2,128,512]{2,1,0:T(8,128)(2,1)S(1)}, bf16[2,128,512]{2,1,0:T(8,128)(2,1)S(1)}, u32[]{:S(2)}, u32[]{:S(2)}) collective-permute-start(bf16[2,128,512]{2,1,0:T(8,128)(2,1)S(1)} %copy-done.10), channel_id=1, source_target_pairs={{0,15},{1,2},{2,1},{3,4},{4,3},{5,6},{6,5},{7,8},{8,7},{9,10},{10,... | collective-permute-start | bytes 786440 | tf_op jit(solution)/shard_map/ppermute | solution.py:349
  142.0 2.4 %place.1 = bf16[256,2048]{1,0:T(8,128)(2,1)} custom-call(s32[2]{0:T(128)S(1)} %pad_add_fusion.1.info_ref, bf16[128,1024]{1,0:T(8,128)(2,1)S(1)} %add_convert_fusion.refs_0_, bf16[128,1024]{1,0:T(8,128)(2,1)S(1)} %collective-permute-done.20.refs_1_, bf16[256,2048]{1,0:T(8,128)(2,1)} %get-tuple-element.79.refs_2_), custom_call_target="tpu_custom_call", output_to_operand_aliasing={{}: (3, {})} | custom-call | tf_op jit(solution)/shard_map/place/pallas_call | solution.py:315
  144.4 8.5 %all-to-all-done.3.got_ref = bf16[16,2,2,16,512]{4,3,2,1,0:T(8,128)(2,1)S(1)} async-done(((bf16[16,2,2,16,512]{4,3,2,1,0:T(8,128)(2,1)}), bf16[16,2,2,16,512]{4,3,2,1,0:T(8,128)(2,1)S(1)}, u32[]{:S(2)}, u32[]{:S(2)}) %all-to-all-start.3) | async-done | bytes 1048608 | tf_op jit(solution)/shard_map/all_to_all | solution.py:383
  152.9 2.5 %collective-permute-done.21.winn_ref = bf16[2,128,512]{2,1,0:T(8,128)(2,1)S(1)} collective-permute-done((bf16[2,128,512]{2,1,0:T(8,128)(2,1)S(1)}, bf16[2,128,512]{2,1,0:T(8,128)(2,1)S(1)}, u32[]{:S(2)}, u32[]{:S(2)}) %collective-permute-start.21) | collective-permute-done | bytes 262176 | tf_op jit(solution)/shard_map/ppermute | solution.py:349
  155.4 1.6 finish.1
  (35 shorter events, 0.2 us)
Async XLA Ops:
  4.9 14.5 %copy-start.7 = (bf16[128,1024]{1,0:T(8,128)(2,1)S(1)}, bf16[128,1024]{1,0:T(8,128)(2,1)}, u32[]{:S(2)}) copy-start(bf16[128,1024]{1,0:T(8,128)(2,1)} %get-tuple-element.45) | copy-start | bytes 786436
  4.9 14.1 %collective-permute-start.1 = (bf16[128,1024]{1,0:T(8,128)(2,1)}, bf16[128,1024]{1,0:T(8,128)(2,1)S(1)}, u32[]{:S(2)}, u32[]{:S(2)}) collective-permute-start(bf16[128,1024]{1,0:T(8,128)(2,1)} %get-tuple-element.47), channel_id=1, source_target_pairs={{16,0},{32,16},{48,32},{64,48},{80,64},{96,80},{112,96},{0,112}} | collective-permute-start | bytes 786440 | tf_op jit(solution)/shard_map/ppermute | solution.py:395
  11.1 7.8 %collective-permute-start.2 = (bf16[128,1024]{1,0:T(8,128)(2,1)}, bf16[128,1024]{1,0:T(8,128)(2,1)S(1)}, u32[]{:S(2)}, u32[]{:S(2)}) collective-permute-start(bf16[128,1024]{1,0:T(8,128)(2,1)} %get-tuple-element.48), channel_id=1, source_target_pairs={{16,8},{32,24},{48,40},{64,56},{80,72},{96,88},{112,104},{0,120}} | collective-permute-start | bytes 786440 | tf_op jit(solution)/shard_map/ppermute | solution.py:396
  14.0 5.5 %collective-permute-start = (bf16[128,1024]{1,0:T(8,128)(2,1)}, bf16[128,1024]{1,0:T(8,128)(2,1)S(1)}, u32[]{:S(2)}, u32[]{:S(2)}) collective-permute-start(bf16[128,1024]{1,0:T(8,128)(2,1)} %get-tuple-element.46), channel_id=1, source_target_pairs={{0,8},{16,24},{32,40},{48,56},{64,72},{80,88},{96,104},{112,120}} | collective-permute-start | bytes 786440 | tf_op jit(solution)/shard_map/ppermute | solution.py:349
  15.3 21.9 %all-to-all-start = ((bf16[16,2,2,16,512]{4,3,2,1,0:T(8,128)(2,1)}), bf16[16,2,2,16,512]{4,3,2,1,0:T(8,128)(2,1)S(1)}, u32[]{:S(2)}, u32[]{:S(2)}) async-start(bf16[16,2,2,16,512]{4,3,2,1,0:T(8,128)(2,1)} %get-tuple-element.49), calls=%async_computation | async-start | bytes 2097152 | tf_op jit(solution)/shard_map/all_to_all | solution.py:383
  18.9 9.3 %copy-start.8 = (s32[32,3]{0,1:T(4,128)S(1)}, s32[32,3]{0,1:T(4,128)}, u32[]{:S(2)}) copy-start(s32[32,3]{0,1:T(4,128)} %param.11) | copy-start | bytes 1156
  19.5 19.9 %collective-permute-start.5 = (bf16[2,128,1024]{2,1,0:T(8,128)(2,1)S(1)}, bf16[2,128,1024]{2,1,0:T(8,128)(2,1)S(1)}, u32[]{:S(2)}, u32[]{:S(2)}) collective-permute-start(bf16[2,128,1024]{2,1,0:T(8,128)(2,1)S(1)} %pad_maximum_fusion), channel_id=1, source_target_pairs={{0,6},{8,14},{16,22},{24,30},{32,38},{40,46},{48,54},{56,62},{64,7... | collective-permute-start | bytes 1572872 | tf_op jit(solution)/shard_map/ppermute | solution.py:349
  24.1 15.7 %collective-permute-start.4 = (bf16[2,128,1024]{2,1,0:T(8,128)(2,1)S(1)}, bf16[2,128,1024]{2,1,0:T(8,128)(2,1)S(1)}, u32[]{:S(2)}, u32[]{:S(2)}) collective-permute-start(bf16[2,128,1024]{2,1,0:T(8,128)(2,1)S(1)} %pad_maximum_fusion), channel_id=1, source_target_pairs={{0,4},{8,12},{16,20},{24,28},{32,36},{40,44},{48,52},{56,60},{64,6... | collective-permute-start | bytes 1572872 | tf_op jit(solution)/shard_map/ppermute | solution.py:349
  25.5 20.0 %collective-permute-start.3 = (bf16[2,128,1024]{2,1,0:T(8,128)(2,1)S(1)}, bf16[2,128,1024]{2,1,0:T(8,128)(2,1)}, u32[]{:S(2)}, u32[]{:S(2)}) collective-permute-start(bf16[2,128,1024]{2,1,0:T(8,128)(2,1)S(1)} %pad_maximum_fusion), channel_id=1, source_target_pairs={{0,2},{8,10},{16,18},{24,26},{32,34},{40,42},{48,50},{56,58},{64,6... | collective-permute-start | bytes 1572872 | tf_op jit(solution)/shard_map/ppermute | solution.py:349
  27.6 19.1 %collective-permute-start.6 = (bf16[2,256,512]{2,1,0:T(8,128)(2,1)}, bf16[2,256,512]{2,1,0:T(8,128)(2,1)}, u32[]{:S(2)}, u32[]{:S(2)}) collective-permute-start(bf16[2,256,512]{2,1,0:T(8,128)(2,1)} %get-tuple-element.51.own_ref), channel_id=1, source_target_pairs={{0,1},{1,0},{2,3},{3,2},{4,5},{5,4},{6,7},{7,6},{8,9},{9,8},{10,11... | collective-permute-start | bytes 1572872 | tf_op jit(solution)/shard_map/ppermute | solution.py:349
  27.6 19.1 %collective-permute-start.7 = (bf16[2,128,512]{2,1,0:T(8,128)(2,1)}, bf16[2,128,512]{2,1,0:T(8,128)(2,1)S(1)}, u32[]{:S(2)}, u32[]{:S(2)}) collective-permute-start(bf16[2,128,512]{2,1,0:T(8,128)(2,1)} %get-tuple-element.52), channel_id=1, source_target_pairs={{0,15},{1,2},{2,1},{3,4},{4,3},{5,6},{6,5},{7,8},{8,7},{9,10},{10,... | collective-permute-start | bytes 786440 | tf_op jit(solution)/shard_map/ppermute | solution.py:349
  46.6 7.7 %copy-start.3 = (bf16[2,128,1024]{2,1,0:T(8,128)(2,1)}, bf16[2,128,1024]{2,1,0:T(8,128)(2,1)S(1)}, u32[]{:S(2)}) copy-start(bf16[2,128,1024]{2,1,0:T(8,128)(2,1)S(1)} %add_add_fusion) | copy-start | bytes 1572868
  46.6 0.8 copy-start.9
  47.4 28.5 %all-to-all-start.1 = ((bf16[8,2,7,16,512]{4,3,2,1,0:T(8,128)(2,1)}), bf16[8,2,7,16,512]{4,3,2,1,0:T(8,128)(2,1)S(1)}, u32[]{:S(2)}, u32[]{:S(2)}) async-start(bf16[8,2,7,16,512]{4,3,2,1,0:T(8,128)(2,1)} %select.6), calls=%async_computation.1 | async-start | bytes 3670016 | tf_op jit(solution)/shard_map/all_to_all | solution.py:386
  51.3 25.9 %collective-permute-start.8 = (bf16[256,2048]{1,0:T(8,128)(2,1)}, bf16[256,2048]{1,0:T(8,128)(2,1)}, u32[]{:S(2)}, u32[]{:S(2)}) collective-permute-start(bf16[256,2048]{1,0:T(8,128)(2,1)} %bitcast.19), channel_id=1, source_target_pairs={{16,0},{32,16},{48,32},{64,48},{80,64},{96,80},{112,96},{0,112},{1... | collective-permute-start | bytes 3145736 | tf_op jit(solution)/shard_map/ppermute | solution.py:408
  52.1 3.6 %collective-permute-start.9 = (bf16[2,128,1024]{2,1,0:T(8,128)(2,1)S(1)}, bf16[2,128,1024]{2,1,0:T(8,128)(2,1)S(1)}, u32[]{:S(2)}, u32[]{:S(2)}) collective-permute-start(bf16[2,128,1024]{2,1,0:T(8,128)(2,1)S(1)} %add_add_fusion), channel_id=1, source_target_pairs={{0,1},{2,3},{4,5},{6,7},{8,9},{10,11},{12,13},{14,15},{16,17},{18,... | collective-permute-start | bytes 1572872 | tf_op jit(solution)/shard_map/ppermute | solution.py:349
  58.9 1.4 collective-permute-start.10
  61.1 13.3 %collective-permute-start.13 = (f32[2,8,128]{2,1,0:T(8,128)S(1)}, f32[2,8,128]{2,1,0:T(8,128)S(1)}, u32[]{:S(2)}, u32[]{:S(2)}) collective-permute-start(f32[2,8,128]{2,1,0:T(8,128)S(1)} %pad_maximum_fusion.1), channel_id=1, source_target_pairs={{0,6},{1,7},{2,0},{3,1},{4,2},{5,3},{6,4},{7,5},{8,14},{9,15},{10,... | collective-permute-start | bytes 24584 | tf_op jit(solution)/shard_map/ppermute | solution.py:349
  64.0 11.9 %collective-permute-start.12 = (f32[2,8,128]{2,1,0:T(8,128)S(1)}, f32[2,8,128]{2,1,0:T(8,128)S(1)}, u32[]{:S(2)}, u32[]{:S(2)}) collective-permute-start(f32[2,8,128]{2,1,0:T(8,128)S(1)} %pad_maximum_fusion.1), channel_id=1, source_target_pairs={{0,4},{1,5},{2,6},{3,7},{4,0},{5,1},{6,2},{7,3},{8,12},{9,13},{10,... | collective-permute-start | bytes 24584 | tf_op jit(solution)/shard_map/ppermute | solution.py:349
  64.9 11.0 %collective-permute-start.11 = (f32[2,8,128]{2,1,0:T(8,128)S(1)}, f32[2,8,128]{2,1,0:T(8,128)S(1)}, u32[]{:S(2)}, u32[]{:S(2)}) collective-permute-start(f32[2,8,128]{2,1,0:T(8,128)S(1)} %pad_maximum_fusion.1), channel_id=1, source_target_pairs={{0,2},{1,3},{2,4},{3,5},{4,6},{5,7},{6,0},{7,1},{8,10},{9,11},{10,... | collective-permute-start | bytes 24584 | tf_op jit(solution)/shard_map/ppermute | solution.py:349
  91.6 34.2 %all-to-all-start.2 = ((bf16[8,2,7,16,512]{4,3,2,1,0:T(8,128)(2,1)}), bf16[8,2,7,16,512]{4,3,2,1,0:T(8,128)(2,1)S(1)}, u32[]{:S(2)}, u32[]{:S(2)}) async-start(bf16[8,2,7,16,512]{4,3,2,1,0:T(8,128)(2,1)} %get-tuple-element.60), calls=%async_computation.2 | async-start | bytes 3670016 | tf_op jit(solution)/shard_map/all_to_all | solution.py:386
  99.0 1.0 copy-start.1
  99.9 3.6 %collective-permute-start.15 = (bf16[128,1024]{1,0:T(8,128)(2,1)}, bf16[128,1024]{1,0:T(8,128)(2,1)S(1)}, u32[]{:S(2)}, u32[]{:S(2)}) collective-permute-start(bf16[128,1024]{1,0:T(8,128)(2,1)} %get-tuple-element.70), channel_id=1, source_target_pairs={{1,0},{3,2},{5,4},{7,6},{9,8},{11,10},{13,12},{15,14},{17,16},{19,... | collective-permute-start | bytes 786440 | tf_op jit(solution)/shard_map/ppermute | solution.py:349
  101.2 8.0 %collective-permute-start.14 = (bf16[2,128,512]{2,1,0:T(8,128)(2,1)}, bf16[2,128,512]{2,1,0:T(8,128)(2,1)S(1)}, u32[]{:S(2)}, u32[]{:S(2)}) collective-permute-start(bf16[2,128,512]{2,1,0:T(8,128)(2,1)} %get-tuple-element.61), channel_id=1, source_target_pairs={{0,1},{1,0},{2,3},{3,2},{4,5},{5,4},{6,7},{7,6},{8,9},{9,8},{10,11... | collective-permute-start | bytes 786440 | tf_op jit(solution)/shard_map/ppermute | solution.py:349
  104.6 21.2 %collective-permute-start.19 = (bf16[128,1024]{1,0:T(8,128)(2,1)S(1)}, bf16[128,1024]{1,0:T(8,128)(2,1)S(1)}, u32[]{:S(2)}, u32[]{:S(2)}) collective-permute-start(bf16[128,1024]{1,0:T(8,128)(2,1)S(1)} %add_convert_fusion.1), channel_id=1, source_target_pairs={{6,0},{14,1},{22,16},{30,17},{38,32},{46,33},{54,48},{62,49},{70,6... | collective-permute-start | bytes 786440 | tf_op jit(solution)/shard_map/ppermute | solution.py:349
  105.9 19.9 %collective-permute-start.18 = (bf16[128,1024]{1,0:T(8,128)(2,1)S(1)}, bf16[128,1024]{1,0:T(8,128)(2,1)S(1)}, u32[]{:S(2)}, u32[]{:S(2)}) collective-permute-start(bf16[128,1024]{1,0:T(8,128)(2,1)S(1)} %add_convert_fusion.1), channel_id=1, source_target_pairs={{4,0},{12,1},{20,16},{28,17},{36,32},{44,33},{52,48},{60,49},{68,6... | collective-permute-start | bytes 786440 | tf_op jit(solution)/shard_map/ppermute | solution.py:349
  107.2 18.6 %collective-permute-start.17 = (bf16[128,1024]{1,0:T(8,128)(2,1)S(1)}, bf16[128,1024]{1,0:T(8,128)(2,1)S(1)}, u32[]{:S(2)}, u32[]{:S(2)}) collective-permute-start(bf16[128,1024]{1,0:T(8,128)(2,1)S(1)} %add_convert_fusion.1), channel_id=1, source_target_pairs={{2,0},{10,1},{18,16},{26,17},{34,32},{42,33},{50,48},{58,49},{66,6... | collective-permute-start | bytes 786440 | tf_op jit(solution)/shard_map/ppermute | solution.py:349
  108.5 17.3 %collective-permute-start.16 = (bf16[128,1024]{1,0:T(8,128)(2,1)S(1)}, bf16[128,1024]{1,0:T(8,128)(2,1)S(1)}, u32[]{:S(2)}, u32[]{:S(2)}) collective-permute-start(bf16[128,1024]{1,0:T(8,128)(2,1)S(1)} %add_convert_fusion.1), channel_id=1, source_target_pairs={{8,1},{24,17},{40,33},{56,49},{72,65},{88,81},{104,97},{120,113}} | collective-permute-start | bytes 786440 | tf_op jit(solution)/shard_map/ppermute | solution.py:349
  125.7 3.9 %copy-start.4 = (bf16[128,1024]{1,0:T(8,128)(2,1)}, bf16[128,1024]{1,0:T(8,128)(2,1)S(1)}, u32[]{:S(2)}) copy-start(bf16[128,1024]{1,0:T(8,128)(2,1)S(1)} %collective-permute-done.18) | copy-start | bytes 786436
  125.8 3.9 %copy-start.5 = (bf16[128,1024]{1,0:T(8,128)(2,1)}, bf16[128,1024]{1,0:T(8,128)(2,1)S(1)}, u32[]{:S(2)}) copy-start(bf16[128,1024]{1,0:T(8,128)(2,1)S(1)} %collective-permute-done.17) | copy-start | bytes 786436
  125.8 3.8 %copy-start.6 = (bf16[128,1024]{1,0:T(8,128)(2,1)}, bf16[128,1024]{1,0:T(8,128)(2,1)S(1)}, u32[]{:S(2)}) copy-start(bf16[128,1024]{1,0:T(8,128)(2,1)S(1)} %collective-permute-done.16) | copy-start | bytes 786436
  125.8 1.5 copy-start.2
  129.6 7.6 %copy-start.10 = (bf16[2,128,512]{2,1,0:T(8,128)(2,1)S(1)}, bf16[2,128,512]{2,1,0:T(8,128)(2,1)}, u32[]{:S(2)}) copy-start(bf16[2,128,512]{2,1,0:T(8,128)(2,1)} %get-tuple-element.83) | copy-start | bytes 786436
  129.6 23.3 %all-to-all-start.3 = ((bf16[16,2,2,16,512]{4,3,2,1,0:T(8,128)(2,1)}), bf16[16,2,2,16,512]{4,3,2,1,0:T(8,128)(2,1)S(1)}, u32[]{:S(2)}, u32[]{:S(2)}) async-start(bf16[16,2,2,16,512]{4,3,2,1,0:T(8,128)(2,1)} %combine.1), calls=%async_computation.3 | async-start | bytes 2097152 | tf_op jit(solution)/shard_map/all_to_all | solution.py:383
  134.6 20.8 %copy-start = (f32[2,256,512]{2,1,0:T(8,128)S(1)}, f32[2,256,512]{2,1,0:T(8,128)}, u32[]{:S(2)}) copy-start(f32[2,256,512]{2,1,0:T(8,128)} %get-tuple-element.81.own_ref) | copy-start | bytes 3145732
  136.0 6.1 %collective-permute-start.20 = (bf16[128,1024]{1,0:T(8,128)(2,1)S(1)}, bf16[128,1024]{1,0:T(8,128)(2,1)S(1)}, u32[]{:S(2)}, u32[]{:S(2)}) collective-permute-start(bf16[128,1024]{1,0:T(8,128)(2,1)S(1)} %add_convert_fusion.refs_0_), channel_id=1, source_target_pairs={{1,0},{17,16},{33,32},{49,48},{65,64},{81,80},{97,96},{113,112}} | collective-permute-start | bytes 786440 | tf_op jit(solution)/shard_map/ppermute | solution.py:349
  137.3 18.1 %collective-permute-start.21 = (bf16[2,128,512]{2,1,0:T(8,128)(2,1)S(1)}, bf16[2,128,512]{2,1,0:T(8,128)(2,1)S(1)}, u32[]{:S(2)}, u32[]{:S(2)}) collective-permute-start(bf16[2,128,512]{2,1,0:T(8,128)(2,1)S(1)} %copy-done.10), channel_id=1, source_target_pairs={{0,15},{1,2},{2,1},{3,4},{4,3},{5,6},{6,5},{7,8},{8,7},{9,10},{10,... | collective-permute-start | bytes 786440 | tf_op jit(solution)/shard_map/ppermute | solution.py:349

commit v5 on v4

--- a/solution.py
+++ b/solution.py
@@ -118,7 +118,7 @@
 
 def combine_kernel(table_ref, got_ref, row_ref, send_ref, acc_ref):
     acc_ref[...] = jnp.zeros_like(acc_ref)
-    acc_ref[:, :, :, :, columns(table_ref[56], 2 * HD)] = row_ref[...]
+    acc_ref[:, :, :, :, columns(table_ref[56], 2 * HD)] = row_ref[...].astype(F32)
     for d in range(8):
         for s in range(7):
             block = table_ref[d * 7 + s]
@@ -292,7 +292,7 @@
         ).astype(BF16)
         kc = slice(g * HD, (g + 1) * HD)
         for i, grad in enumerate((dot(ds, q) * SCALE, dot(pb, do))):
-            down_ref[:, i, :, :, kc] = grad.reshape(16, 2, 16, HD)
+            down_ref[:, i, :, :, kc] = grad.astype(BF16).reshape(16, 2, 16, HD)
 
 
 def place_kernel(info_ref, *refs):
@@ -423,7 +423,7 @@
     part, row = on_chip(
         row_kernel,
         "row_grads",
-        [stored((BLK, half), BF16), shape((16, 2, 2, 16, 2 * HD), F32)],
+        [stored((BLK, half), BF16), shape((16, 2, 2, 16, 2 * HD), BF16)],
         info, x, got1, stats,
     )
     winp, winn = send(winp, swap), send(winn, ring)

time: 158 us -> 158 us (level)
  no operation moved by 1% of the time
where the time goes in v5:
time: 158 us; the launch traced here: 157 us
  waiting for transfers between devices  57.8 us (37%)
  starting transfers between devices  57.1 us (36%)
  Pallas kernels  31.3 us (20%)
  other arithmetic  5.84 us (4%)
  local copies, waits for them, and re-layouts  3.72 us (2%)
  between operations  1.6 us (1%)
    ppermute x19, waiting for transfers between devices, send(): return lax.ppermute(block, 'ctx', pairs)  39.5 us
    ppermute x19, starting transfers between devices, send(): return lax.ppermute(block, 'ctx', pairs)  30.3 us
    all_to_all x2, waiting for transfers between devices, exchange(): return lax.all_to_all(x, 'ctx', 0, 0, tiled=True)  17.1 us
    pallas_call x1, Pallas kernels, attend(): pl.pallas_call(attend_kernel, grid_spec=pltpu.PrefetchScalarGridSpec(num_...  14.4 us
    pallas_call x5, Pallas kernels, on_chip(): pl.pallas_call(kernel, in_specs=[pl.BlockSpec(memory_space=pltpu.SMEM)] +...  10.9 us
    all_to_all x2, starting transfers between devices, exchange(): return lax.all_to_all(x, 'ctx', 0, 0, tiled=True)  8.61 us
    all_to_all x2, starting transfers between devices, exchange_half(): return lax.all_to_all(x, 'ctx', 0, 0, tiled=True, axis_index_groups=halves)  8.3 us
    ppermute x1, starting transfers between devices, per_device(): lax.ppermute(g0, both, [(flat(s + 1, 0), flat(s, 0)) for s in range(n_seg)])  6.22 us
  transfers between devices with their start and end apart: 26, of which 13 were waited for; matrix products, arithmetic and copies ran while one was open for 4% of the time, Pallas kernels for 6%

profile of v5, /device:TPU:0, one launch (start us, length us, event | category | flops | bytes accessed | tf_op | source)
XLA Modules:
  0.0 157.3 jit_solution(5130592508376149266)
XLA Ops:
  1.3 0.1 pad_add_fusion.1.info_ref
  1.4 3.6 %pack.1 = (bf16[2,256,512]{2,1,0:T(8,128)(2,1)}, bf16[16,2,2,16,512]{4,3,2,1,0:T(8,128)(2,1)}, bf16[2,128,512]{2,1,0:T(8,128)(2,1)}, bf16[128,1024]{1,0:T(8,128)...) custom-call(s32[2]{0:T(128)S(1)} %pad_add_fusion.1.info_ref, ...), custom_call_target="tpu_custom_call" | custom-call | tf_op jit(solution)/shard_map/pack/pallas_call | solution.py:81
  4.9 6.2 %collective-permute-start.1 = (bf16[128,1024]{1,0:T(8,128)(2,1)}, bf16[128,1024]{1,0:T(8,128)(2,1)S(1)}, u32[]{:S(2)}, u32[]{:S(2)}) collective-permute-start(bf16[128,1024]{1,0:T(8,128)(2,1)} %get-tuple-element.47), channel_id=1, source_target_pairs={{16,0},{32,16},{48,32},{64,48},{80,64},{96,80},{112,96},{0,112}} | collective-permute-start | bytes 786440 | tf_op jit(solution)/shard_map/ppermute | solution.py:395
  11.1 2.8 %collective-permute-start.2 = (bf16[128,1024]{1,0:T(8,128)(2,1)}, bf16[128,1024]{1,0:T(8,128)(2,1)S(1)}, u32[]{:S(2)}, u32[]{:S(2)}) collective-permute-start(bf16[128,1024]{1,0:T(8,128)(2,1)} %get-tuple-element.48), channel_id=1, source_target_pairs={{16,8},{32,24},{48,40},{64,56},{80,72},{96,88},{112,104},{0,120}} | collective-permute-start | bytes 786440 | tf_op jit(solution)/shard_map/ppermute | solution.py:396
  14.0 1.3 collective-permute-start
  15.3 3.7 %all-to-all-start = ((bf16[16,2,2,16,512]{4,3,2,1,0:T(8,128)(2,1)}), bf16[16,2,2,16,512]{4,3,2,1,0:T(8,128)(2,1)S(1)}, u32[]{:S(2)}, u32[]{:S(2)}) async-start(bf16[16,2,2,16,512]{4,3,2,1,0:T(8,128)(2,1)} %get-tuple-element.49), calls=%async_computation | async-start | bytes 2097152 | tf_op jit(solution)/shard_map/all_to_all | solution.py:383
  18.9 0.0 copy-start.9
  19.0 0.4 collective-permute-done
  19.5 0.1 pad_maximum_fusion
  19.5 4.6 %collective-permute-start.5 = (bf16[2,128,1024]{2,1,0:T(8,128)(2,1)S(1)}, bf16[2,128,1024]{2,1,0:T(8,128)(2,1)S(1)}, u32[]{:S(2)}, u32[]{:S(2)}) collective-permute-start(bf16[2,128,1024]{2,1,0:T(8,128)(2,1)S(1)} %pad_maximum_fusion), channel_id=1, source_target_pairs={{0,6},{8,14},{16,22},{24,30},{32,38},{40,46},{48,54},{56,62},{64,7... | collective-permute-start | bytes 1572872 | tf_op jit(solution)/shard_map/ppermute | solution.py:349
  24.1 1.3 collective-permute-start.4
  25.5 2.1 %collective-permute-start.3 = (bf16[2,128,1024]{2,1,0:T(8,128)(2,1)S(1)}, bf16[2,128,1024]{2,1,0:T(8,128)(2,1)}, u32[]{:S(2)}, u32[]{:S(2)}) collective-permute-start(bf16[2,128,1024]{2,1,0:T(8,128)(2,1)S(1)} %pad_maximum_fusion), channel_id=1, source_target_pairs={{0,2},{8,10},{16,18},{24,26},{32,34},{40,42},{48,50},{56,58},{64,6... | collective-permute-start | bytes 1572872 | tf_op jit(solution)/shard_map/ppermute | solution.py:349
  27.6 0.7 collective-permute-start.7
  28.3 0.1 copy.11
  28.3 0.1 reshape.12
  28.4 0.1 pad_dynamic-slice_fusion
  28.5 0.1 reshape.13
  28.6 0.1 pad_add_fusion.table_ref
  28.7 8.6 %all-to-all-done.got_ref = bf16[16,2,2,16,512]{4,3,2,1,0:T(8,128)(2,1)S(1)} async-done(((bf16[16,2,2,16,512]{4,3,2,1,0:T(8,128)(2,1)}), bf16[16,2,2,16,512]{4,3,2,1,0:T(8,128)(2,1)S(1)}, u32[]{:S(2)}, u32[]{:S(2)}) %all-to-all-start) | async-done | bytes 1048608 | tf_op jit(solution)/shard_map/all_to_all | solution.py:383
  37.2 2.2 %select.6 = bf16[8,2,7,16,512]{4,3,2,1,0:T(8,128)(2,1)} custom-call(s32[57]{0:T(128)S(1)} %pad_add_fusion.table_ref, bf16[16,2,2,16,512]{4,3,2,1,0:T(8,128)(2,1)S(1)} %all-to-all-done.got_ref), custom_call_target="tpu_custom_call" | custom-call | tf_op jit(solution)/shard_map/select/pallas_call | solution.py:33
  39.4 0.4 collective-permute-done.4
  39.8 5.6 %collective-permute-done.3 = bf16[2,128,1024]{2,1,0:T(8,128)(2,1)} collective-permute-done((bf16[2,128,1024]{2,1,0:T(8,128)(2,1)S(1)}, bf16[2,128,1024]{2,1,0:T(8,128)(2,1)}, u32[]{:S(2)}, u32[]{:S(2)}) %collective-permute-start.3) | collective-permute-done | bytes 524320 | tf_op jit(solution)/shard_map/ppermute | solution.py:349
  45.4 1.2 add_add_fusion
  46.7 0.7 copy-done.10
  47.4 3.9 %all-to-all-start.1 = ((bf16[8,2,7,16,512]{4,3,2,1,0:T(8,128)(2,1)}), bf16[8,2,7,16,512]{4,3,2,1,0:T(8,128)(2,1)S(1)}, u32[]{:S(2)}, u32[]{:S(2)}) async-start(bf16[8,2,7,16,512]{4,3,2,1,0:T(8,128)(2,1)} %select.6), calls=%async_computation.1 | async-start | bytes 3670016 | tf_op jit(solution)/shard_map/all_to_all | solution.py:386
  51.3 0.8 collective-permute-start.8
  52.1 2.1 %collective-permute-start.9 = (bf16[2,128,1024]{2,1,0:T(8,128)(2,1)S(1)}, bf16[2,128,1024]{2,1,0:T(8,128)(2,1)S(1)}, u32[]{:S(2)}, u32[]{:S(2)}) collective-permute-start(bf16[2,128,1024]{2,1,0:T(8,128)(2,1)S(1)} %add_add_fusion), channel_id=1, source_target_pairs={{0,1},{2,3},{4,5},{6,7},{8,9},{10,11},{12,13},{14,15},{16,17},{18,... | collective-permute-start | bytes 1572872 | tf_op jit(solution)/shard_map/ppermute | solution.py:349
  54.3 1.5 collective-permute-done.9
  55.8 1.2 add.66.x_ref
  57.0 1.9 %row_stats.1 = f32[2,8,128]{2,1,0:T(8,128)} custom-call(s32[2]{0:T(128)S(1)} %pad_add_fusion.1.info_ref, bf16[2,128,1024]{2,1,0:T(8,128)(2,1)S(1)} %add.66.x_ref, bf16[16,2,2,16,512]{4,3,2,1,0:T(8,128)(2,1)S(1)} %all-to-all-done.got_ref), custom_call_target="tpu_custom_call" | custom-call | tf_op jit(solution)/shard_map/row_stats/pallas_call | solution.py:33
  58.9 0.4 collective-permute-start.10
  59.2 1.0 collective-permute-done.10
  60.3 0.8 fusion
  61.1 2.9 %collective-permute-start.13 = (f32[2,8,128]{2,1,0:T(8,128)S(1)}, f32[2,8,128]{2,1,0:T(8,128)S(1)}, u32[]{:S(2)}, u32[]{:S(2)}) collective-permute-start(f32[2,8,128]{2,1,0:T(8,128)S(1)} %pad_maximum_fusion.1), channel_id=1, source_target_pairs={{0,6},{1,7},{2,0},{3,1},{4,2},{5,3},{6,4},{7,5},{8,14},{9,15},{10,... | collective-permute-start | bytes 24584 | tf_op jit(solution)/shard_map/ppermute | solution.py:349
  64.0 0.9 collective-permute-start.12
  64.9 0.9 collective-permute-start.11
  65.7 8.7 %collective-permute-done.13 = f32[2,8,128]{2,1,0:T(8,128)S(1)} collective-permute-done((f32[2,8,128]{2,1,0:T(8,128)S(1)}, f32[2,8,128]{2,1,0:T(8,128)S(1)}, u32[]{:S(2)}, u32[]{:S(2)}) %collective-permute-start.13) | collective-permute-done | bytes 8224 | tf_op jit(solution)/shard_map/ppermute | solution.py:349
  74.4 1.5 collective-permute-done.12
  75.9 1.2 collective-permute-done.8.do_ref
  77.2 14.4 %attend.1 = (bf16[256,2048]{1,0:T(8,128)(2,1)}, f32[2,256,512]{2,1,0:T(8,128)}, bf16[2,128,512]{2,1,0:T(8,128)(2,1)}, bf16[2,128,512]{2,1,0:T(8,128)(2,1)}, bf16[8,2,7,16,512]{4,3,2,1,0:T(8,128)(2,1)}) custom-call(s32[2]{0:T(128)S(1)} %pad_add_fusion.1.info_ref, bf16[8,256,2048]{2,1,0:T(8,128)(2,1)} %bitcast.14, ...), custom_call_target="tpu_custom_call" | custom-call | flops 4697620480 | bytes 10485760 | tf_op jit(solution)/shard_map/attend/pallas_call | solution.py:226
  91.6 4.4 %all-to-all-start.2 = ((bf16[8,2,7,16,512]{4,3,2,1,0:T(8,128)(2,1)}), bf16[8,2,7,16,512]{4,3,2,1,0:T(8,128)(2,1)S(1)}, u32[]{:S(2)}, u32[]{:S(2)}) async-start(bf16[8,2,7,16,512]{4,3,2,1,0:T(8,128)(2,1)} %get-tuple-element.60), calls=%async_computation.2 | async-start | bytes 3670016 | tf_op jit(solution)/shard_map/all_to_all | solution.py:386
  96.1 2.9 %row_grads.1 = (bf16[128,1024]{1,0:T(8,128)(2,1)}, bf16[16,2,2,16,256]{4,3,2,1,0:T(8,128)(2,1)S(1)}) custom-call(s32[2]{0:T(128)S(1)} %pad_add_fusion.1.info_ref, bf16[2,128,1024]{2,1,0:T(8,128)(2,1)S(1)} %add.66.x_ref, bf16[16,2,2,16,512]{4,3,2,1,0:T(8,128)(2,1)S(1)} %all-to-all-done.got_ref, f32[2,8,128]{2,1,0:T(8,128)S(1)} %pad_maximum_fusion.2.st_ref), custom_call_target="tpu_custom_call" | custom-call | tf_op jit(solution)/shard_map/row_grads/pallas_call | solution.py:33
  99.0 0.8 copy-done.1
  99.8 1.3 collective-permute-start.15
  101.1 1.2 collective-permute-start.14
  102.3 1.1 collective-permute-done.15
  103.4 1.0 add_convert_fusion.1
  104.4 1.3 collective-permute-start.19
  105.7 1.3 collective-permute-start.18
  107.0 1.3 collective-permute-start.17
  108.3 0.7 collective-permute-start.16
  109.0 16.7 %collective-permute-done.19 = bf16[128,1024]{1,0:T(8,128)(2,1)S(1)} collective-permute-done((bf16[128,1024]{1,0:T(8,128)(2,1)S(1)}, bf16[128,1024]{1,0:T(8,128)(2,1)S(1)}, u32[]{:S(2)}, u32[]{:S(2)}) %collective-permute-start.19) | collective-permute-done | bytes 262176 | tf_op jit(solution)/shard_map/ppermute | solution.py:349
  125.8 0.7 copy-done.5
  126.5 0.1 copy-done.7
  126.6 1.0 copy-done.2
  127.6 2.3 %combine.1 = bf16[16,2,2,16,512]{4,3,2,1,0:T(8,128)(2,1)} custom-call(s32[57]{0:T(128)S(1)} %pad_add_fusion.table_ref, bf16[8,2,7,16,512]{4,3,2,1,0:T(8,128)(2,1)S(1)} %all-to-all-done.2.got_ref, bf16[16,2,2,16,256]{4,3,2,1,0:T(8,128)(2,1)S(1)} %copy-done.2), custom_call_target="tpu_custom_call" | custom-call | tf_op jit(solution)/shard_map/combine/pallas_call | solution.py:33
  130.0 4.9 %all-to-all-start.3 = ((bf16[16,2,2,16,512]{4,3,2,1,0:T(8,128)(2,1)}), bf16[16,2,2,16,512]{4,3,2,1,0:T(8,128)(2,1)S(1)}, u32[]{:S(2)}, u32[]{:S(2)}) async-start(bf16[16,2,2,16,512]{4,3,2,1,0:T(8,128)(2,1)} %combine.1), calls=%async_computation.3 | async-start | bytes 2097152 | tf_op jit(solution)/shard_map/all_to_all | solution.py:383
  134.9 1.3 add_convert_fusion.refs_0_
  136.2 1.3 collective-permute-start.20
  137.5 4.8 %collective-permute-start.21 = (bf16[2,128,512]{2,1,0:T(8,128)(2,1)}, bf16[2,128,512]{2,1,0:T(8,128)(2,1)S(1)}, u32[]{:S(2)}, u32[]{:S(2)}) collective-permute-start(bf16[2,128,512]{2,1,0:T(8,128)(2,1)} %get-tuple-element.83), channel_id=1, source_target_pairs={{0,15},{1,2},{2,1},{3,4},{4,3},{5,6},{6,5},{7,8},{8,7},{9,10},{10,... | collective-permute-start | bytes 786440 | tf_op jit(solution)/shard_map/ppermute | solution.py:349
  142.3 2.4 %place.1 = bf16[256,2048]{1,0:T(8,128)(2,1)} custom-call(s32[2]{0:T(128)S(1)} %pad_add_fusion.1.info_ref, bf16[128,1024]{1,0:T(8,128)(2,1)S(1)} %add_convert_fusion.refs_0_, bf16[128,1024]{1,0:T(8,128)(2,1)S(1)} %collective-permute-done.20.refs_1_, bf16[256,2048]{1,0:T(8,128)(2,1)} %get-tuple-element.79.refs_2_), custom_call_target="tpu_custom_call", output_to_operand_aliasing={{}: (3, {})} | custom-call | tf_op jit(solution)/shard_map/place/pallas_call | solution.py:315
  144.7 8.5 %all-to-all-done.3.got_ref = bf16[16,2,2,16,512]{4,3,2,1,0:T(8,128)(2,1)S(1)} async-done(((bf16[16,2,2,16,512]{4,3,2,1,0:T(8,128)(2,1)}), bf16[16,2,2,16,512]{4,3,2,1,0:T(8,128)(2,1)S(1)}, u32[]{:S(2)}, u32[]{:S(2)}) %all-to-all-start.3) | async-done | bytes 1048608 | tf_op jit(solution)/shard_map/all_to_all | solution.py:383
  153.2 2.5 %collective-permute-done.21.winn_ref = bf16[2,128,512]{2,1,0:T(8,128)(2,1)S(1)} collective-permute-done((bf16[2,128,512]{2,1,0:T(8,128)(2,1)}, bf16[2,128,512]{2,1,0:T(8,128)(2,1)S(1)}, u32[]{:S(2)}, u32[]{:S(2)}) %collective-permute-start.21) | collective-permute-done | bytes 262176 | tf_op jit(solution)/shard_map/ppermute | solution.py:349
  155.7 1.6 finish.1
  (35 shorter events, 0.2 us)
Async XLA Ops:
  4.9 14.5 %copy-start.8 = (bf16[128,1024]{1,0:T(8,128)(2,1)S(1)}, bf16[128,1024]{1,0:T(8,128)(2,1)}, u32[]{:S(2)}) copy-start(bf16[128,1024]{1,0:T(8,128)(2,1)} %get-tuple-element.45) | copy-start | bytes 786436
  4.9 14.1 %collective-permute-start.1 = (bf16[128,1024]{1,0:T(8,128)(2,1)}, bf16[128,1024]{1,0:T(8,128)(2,1)S(1)}, u32[]{:S(2)}, u32[]{:S(2)}) collective-permute-start(bf16[128,1024]{1,0:T(8,128)(2,1)} %get-tuple-element.47), channel_id=1, source_target_pairs={{16,0},{32,16},{48,32},{64,48},{80,64},{96,80},{112,96},{0,112}} | collective-permute-start | bytes 786440 | tf_op jit(solution)/shard_map/ppermute | solution.py:395
  11.1 7.8 %collective-permute-start.2 = (bf16[128,1024]{1,0:T(8,128)(2,1)}, bf16[128,1024]{1,0:T(8,128)(2,1)S(1)}, u32[]{:S(2)}, u32[]{:S(2)}) collective-permute-start(bf16[128,1024]{1,0:T(8,128)(2,1)} %get-tuple-element.48), channel_id=1, source_target_pairs={{16,8},{32,24},{48,40},{64,56},{80,72},{96,88},{112,104},{0,120}} | collective-permute-start | bytes 786440 | tf_op jit(solution)/shard_map/ppermute | solution.py:396
  14.0 5.5 %collective-permute-start = (bf16[128,1024]{1,0:T(8,128)(2,1)}, bf16[128,1024]{1,0:T(8,128)(2,1)S(1)}, u32[]{:S(2)}, u32[]{:S(2)}) collective-permute-start(bf16[128,1024]{1,0:T(8,128)(2,1)} %get-tuple-element.46), channel_id=1, source_target_pairs={{0,8},{16,24},{32,40},{48,56},{64,72},{80,88},{96,104},{112,120}} | collective-permute-start | bytes 786440 | tf_op jit(solution)/shard_map/ppermute | solution.py:349
  15.3 21.9 %all-to-all-start = ((bf16[16,2,2,16,512]{4,3,2,1,0:T(8,128)(2,1)}), bf16[16,2,2,16,512]{4,3,2,1,0:T(8,128)(2,1)S(1)}, u32[]{:S(2)}, u32[]{:S(2)}) async-start(bf16[16,2,2,16,512]{4,3,2,1,0:T(8,128)(2,1)} %get-tuple-element.49), calls=%async_computation | async-start | bytes 2097152 | tf_op jit(solution)/shard_map/all_to_all | solution.py:383
  18.9 9.3 %copy-start.9 = (s32[32,3]{0,1:T(4,128)S(1)}, s32[32,3]{0,1:T(4,128)}, u32[]{:S(2)}) copy-start(s32[32,3]{0,1:T(4,128)} %param.11) | copy-start | bytes 1156
  19.5 19.9 %collective-permute-start.5 = (bf16[2,128,1024]{2,1,0:T(8,128)(2,1)S(1)}, bf16[2,128,1024]{2,1,0:T(8,128)(2,1)S(1)}, u32[]{:S(2)}, u32[]{:S(2)}) collective-permute-start(bf16[2,128,1024]{2,1,0:T(8,128)(2,1)S(1)} %pad_maximum_fusion), channel_id=1, source_target_pairs={{0,6},{8,14},{16,22},{24,30},{32,38},{40,46},{48,54},{56,62},{64,7... | collective-permute-start | bytes 1572872 | tf_op jit(solution)/shard_map/ppermute | solution.py:349
  24.1 15.7 %collective-permute-start.4 = (bf16[2,128,1024]{2,1,0:T(8,128)(2,1)S(1)}, bf16[2,128,1024]{2,1,0:T(8,128)(2,1)S(1)}, u32[]{:S(2)}, u32[]{:S(2)}) collective-permute-start(bf16[2,128,1024]{2,1,0:T(8,128)(2,1)S(1)} %pad_maximum_fusion), channel_id=1, source_target_pairs={{0,4},{8,12},{16,20},{24,28},{32,36},{40,44},{48,52},{56,60},{64,6... | collective-permute-start | bytes 1572872 | tf_op jit(solution)/shard_map/ppermute | solution.py:349
  25.5 20.0 %collective-permute-start.3 = (bf16[2,128,1024]{2,1,0:T(8,128)(2,1)S(1)}, bf16[2,128,1024]{2,1,0:T(8,128)(2,1)}, u32[]{:S(2)}, u32[]{:S(2)}) collective-permute-start(bf16[2,128,1024]{2,1,0:T(8,128)(2,1)S(1)} %pad_maximum_fusion), channel_id=1, source_target_pairs={{0,2},{8,10},{16,18},{24,26},{32,34},{40,42},{48,50},{56,58},{64,6... | collective-permute-start | bytes 1572872 | tf_op jit(solution)/shard_map/ppermute | solution.py:349
  27.6 19.1 %collective-permute-start.6 = (bf16[2,256,512]{2,1,0:T(8,128)(2,1)}, bf16[2,256,512]{2,1,0:T(8,128)(2,1)}, u32[]{:S(2)}, u32[]{:S(2)}) collective-permute-start(bf16[2,256,512]{2,1,0:T(8,128)(2,1)} %get-tuple-element.51.own_ref), channel_id=1, source_target_pairs={{0,1},{1,0},{2,3},{3,2},{4,5},{5,4},{6,7},{7,6},{8,9},{9,8},{10,11... | collective-permute-start | bytes 1572872 | tf_op jit(solution)/shard_map/ppermute | solution.py:349
  27.6 19.1 %collective-permute-start.7 = (bf16[2,128,512]{2,1,0:T(8,128)(2,1)}, bf16[2,128,512]{2,1,0:T(8,128)(2,1)S(1)}, u32[]{:S(2)}, u32[]{:S(2)}) collective-permute-start(bf16[2,128,512]{2,1,0:T(8,128)(2,1)} %get-tuple-element.52), channel_id=1, source_target_pairs={{0,15},{1,2},{2,1},{3,4},{4,3},{5,6},{6,5},{7,8},{8,7},{9,10},{10,... | collective-permute-start | bytes 786440 | tf_op jit(solution)/shard_map/ppermute | solution.py:349
  46.6 7.7 %copy-start.3 = (bf16[2,128,1024]{2,1,0:T(8,128)(2,1)}, bf16[2,128,1024]{2,1,0:T(8,128)(2,1)S(1)}, u32[]{:S(2)}) copy-start(bf16[2,128,1024]{2,1,0:T(8,128)(2,1)S(1)} %add_add_fusion) | copy-start | bytes 1572868
  46.6 0.8 copy-start.10
  47.4 28.5 %all-to-all-start.1 = ((bf16[8,2,7,16,512]{4,3,2,1,0:T(8,128)(2,1)}), bf16[8,2,7,16,512]{4,3,2,1,0:T(8,128)(2,1)S(1)}, u32[]{:S(2)}, u32[]{:S(2)}) async-start(bf16[8,2,7,16,512]{4,3,2,1,0:T(8,128)(2,1)} %select.6), calls=%async_computation.1 | async-start | bytes 3670016 | tf_op jit(solution)/shard_map/all_to_all | solution.py:386
  51.3 25.9 %collective-permute-start.8 = (bf16[256,2048]{1,0:T(8,128)(2,1)}, bf16[256,2048]{1,0:T(8,128)(2,1)}, u32[]{:S(2)}, u32[]{:S(2)}) collective-permute-start(bf16[256,2048]{1,0:T(8,128)(2,1)} %bitcast.19), channel_id=1, source_target_pairs={{16,0},{32,16},{48,32},{64,48},{80,64},{96,80},{112,96},{0,112},{1... | collective-permute-start | bytes 3145736 | tf_op jit(solution)/shard_map/ppermute | solution.py:408
  52.1 3.6 %collective-permute-start.9 = (bf16[2,128,1024]{2,1,0:T(8,128)(2,1)S(1)}, bf16[2,128,1024]{2,1,0:T(8,128)(2,1)S(1)}, u32[]{:S(2)}, u32[]{:S(2)}) collective-permute-start(bf16[2,128,1024]{2,1,0:T(8,128)(2,1)S(1)} %add_add_fusion), channel_id=1, source_target_pairs={{0,1},{2,3},{4,5},{6,7},{8,9},{10,11},{12,13},{14,15},{16,17},{18,... | collective-permute-start | bytes 1572872 | tf_op jit(solution)/shard_map/ppermute | solution.py:349
  58.9 1.4 collective-permute-start.10
  61.1 13.3 %collective-permute-start.13 = (f32[2,8,128]{2,1,0:T(8,128)S(1)}, f32[2,8,128]{2,1,0:T(8,128)S(1)}, u32[]{:S(2)}, u32[]{:S(2)}) collective-permute-start(f32[2,8,128]{2,1,0:T(8,128)S(1)} %pad_maximum_fusion.1), channel_id=1, source_target_pairs={{0,6},{1,7},{2,0},{3,1},{4,2},{5,3},{6,4},{7,5},{8,14},{9,15},{10,... | collective-permute-start | bytes 24584 | tf_op jit(solution)/shard_map/ppermute | solution.py:349
  64.0 11.9 %collective-permute-start.12 = (f32[2,8,128]{2,1,0:T(8,128)S(1)}, f32[2,8,128]{2,1,0:T(8,128)S(1)}, u32[]{:S(2)}, u32[]{:S(2)}) collective-permute-start(f32[2,8,128]{2,1,0:T(8,128)S(1)} %pad_maximum_fusion.1), channel_id=1, source_target_pairs={{0,4},{1,5},{2,6},{3,7},{4,0},{5,1},{6,2},{7,3},{8,12},{9,13},{10,... | collective-permute-start | bytes 24584 | tf_op jit(solution)/shard_map/ppermute | solution.py:349
  64.9 11.0 %collective-permute-start.11 = (f32[2,8,128]{2,1,0:T(8,128)S(1)}, f32[2,8,128]{2,1,0:T(8,128)S(1)}, u32[]{:S(2)}, u32[]{:S(2)}) collective-permute-start(f32[2,8,128]{2,1,0:T(8,128)S(1)} %pad_maximum_fusion.1), channel_id=1, source_target_pairs={{0,2},{1,3},{2,4},{3,5},{4,6},{5,7},{6,0},{7,1},{8,10},{9,11},{10,... | collective-permute-start | bytes 24584 | tf_op jit(solution)/shard_map/ppermute | solution.py:349
  91.6 34.2 %all-to-all-start.2 = ((bf16[8,2,7,16,512]{4,3,2,1,0:T(8,128)(2,1)}), bf16[8,2,7,16,512]{4,3,2,1,0:T(8,128)(2,1)S(1)}, u32[]{:S(2)}, u32[]{:S(2)}) async-start(bf16[8,2,7,16,512]{4,3,2,1,0:T(8,128)(2,1)} %get-tuple-element.60), calls=%async_computation.2 | async-start | bytes 3670016 | tf_op jit(solution)/shard_map/all_to_all | solution.py:386
  99.0 0.8 copy-start.1
  99.8 3.6 %collective-permute-start.15 = (bf16[128,1024]{1,0:T(8,128)(2,1)}, bf16[128,1024]{1,0:T(8,128)(2,1)S(1)}, u32[]{:S(2)}, u32[]{:S(2)}) collective-permute-start(bf16[128,1024]{1,0:T(8,128)(2,1)} %get-tuple-element.70), channel_id=1, source_target_pairs={{1,0},{3,2},{5,4},{7,6},{9,8},{11,10},{13,12},{15,14},{17,16},{19,... | collective-permute-start | bytes 786440 | tf_op jit(solution)/shard_map/ppermute | solution.py:349
  101.1 8.0 %collective-permute-start.14 = (bf16[2,128,512]{2,1,0:T(8,128)(2,1)}, bf16[2,128,512]{2,1,0:T(8,128)(2,1)S(1)}, u32[]{:S(2)}, u32[]{:S(2)}) collective-permute-start(bf16[2,128,512]{2,1,0:T(8,128)(2,1)} %get-tuple-element.61), channel_id=1, source_target_pairs={{0,1},{1,0},{2,3},{3,2},{4,5},{5,4},{6,7},{7,6},{8,9},{9,8},{10,11... | collective-permute-start | bytes 786440 | tf_op jit(solution)/shard_map/ppermute | solution.py:349
  104.4 21.3 %collective-permute-start.19 = (bf16[128,1024]{1,0:T(8,128)(2,1)S(1)}, bf16[128,1024]{1,0:T(8,128)(2,1)S(1)}, u32[]{:S(2)}, u32[]{:S(2)}) collective-permute-start(bf16[128,1024]{1,0:T(8,128)(2,1)S(1)} %add_convert_fusion.1), channel_id=1, source_target_pairs={{6,0},{14,1},{22,16},{30,17},{38,32},{46,33},{54,48},{62,49},{70,6... | collective-permute-start | bytes 786440 | tf_op jit(solution)/shard_map/ppermute | solution.py:349
  105.7 20.0 %collective-permute-start.18 = (bf16[128,1024]{1,0:T(8,128)(2,1)S(1)}, bf16[128,1024]{1,0:T(8,128)(2,1)S(1)}, u32[]{:S(2)}, u32[]{:S(2)}) collective-permute-start(bf16[128,1024]{1,0:T(8,128)(2,1)S(1)} %add_convert_fusion.1), channel_id=1, source_target_pairs={{4,0},{12,1},{20,16},{28,17},{36,32},{44,33},{52,48},{60,49},{68,6... | collective-permute-start | bytes 786440 | tf_op jit(solution)/shard_map/ppermute | solution.py:349
  107.0 18.7 %collective-permute-start.17 = (bf16[128,1024]{1,0:T(8,128)(2,1)S(1)}, bf16[128,1024]{1,0:T(8,128)(2,1)S(1)}, u32[]{:S(2)}, u32[]{:S(2)}) collective-permute-start(bf16[128,1024]{1,0:T(8,128)(2,1)S(1)} %add_convert_fusion.1), channel_id=1, source_target_pairs={{2,0},{10,1},{18,16},{26,17},{34,32},{42,33},{50,48},{58,49},{66,6... | collective-permute-start | bytes 786440 | tf_op jit(solution)/shard_map/ppermute | solution.py:349
  108.3 17.4 %collective-permute-start.16 = (bf16[128,1024]{1,0:T(8,128)(2,1)S(1)}, bf16[128,1024]{1,0:T(8,128)(2,1)S(1)}, u32[]{:S(2)}, u32[]{:S(2)}) collective-permute-start(bf16[128,1024]{1,0:T(8,128)(2,1)S(1)} %add_convert_fusion.1), channel_id=1, source_target_pairs={{8,1},{24,17},{40,33},{56,49},{72,65},{88,81},{104,97},{120,113}} | collective-permute-start | bytes 786440 | tf_op jit(solution)/shard_map/ppermute | solution.py:349
  125.7 4.2 %copy-start.4 = (bf16[128,1024]{1,0:T(8,128)(2,1)}, bf16[128,1024]{1,0:T(8,128)(2,1)S(1)}, u32[]{:S(2)}) copy-start(bf16[128,1024]{1,0:T(8,128)(2,1)S(1)} %collective-permute-done.18) | copy-start | bytes 786436
  125.8 0.7 copy-start.5
  125.8 0.8 copy-start.7
  126.6 1.0 copy-start.2
  130.0 5.0 %copy-start.6 = (bf16[128,1024]{1,0:T(8,128)(2,1)S(1)}, bf16[128,1024]{1,0:T(8,128)(2,1)}, u32[]{:S(2)}) copy-start(bf16[128,1024]{1,0:T(8,128)(2,1)} %copy-done.5) | copy-start | bytes 786436
  130.0 23.3 %all-to-all-start.3 = ((bf16[16,2,2,16,512]{4,3,2,1,0:T(8,128)(2,1)}), bf16[16,2,2,16,512]{4,3,2,1,0:T(8,128)(2,1)S(1)}, u32[]{:S(2)}, u32[]{:S(2)}) async-start(bf16[16,2,2,16,512]{4,3,2,1,0:T(8,128)(2,1)} %combine.1), calls=%async_computation.3 | async-start | bytes 2097152 | tf_op jit(solution)/shard_map/all_to_all | solution.py:383
  134.9 20.8 %copy-start = (f32[2,256,512]{2,1,0:T(8,128)S(1)}, f32[2,256,512]{2,1,0:T(8,128)}, u32[]{:S(2)}) copy-start(f32[2,256,512]{2,1,0:T(8,128)} %get-tuple-element.81.own_ref) | copy-start | bytes 3145732
  136.2 6.1 %collective-permute-start.20 = (bf16[128,1024]{1,0:T(8,128)(2,1)S(1)}, bf16[128,1024]{1,0:T(8,128)(2,1)S(1)}, u32[]{:S(2)}, u32[]{:S(2)}) collective-permute-start(bf16[128,1024]{1,0:T(8,128)(2,1)S(1)} %add_convert_fusion.refs_0_), channel_id=1, source_target_pairs={{1,0},{17,16},{33,32},{49,48},{65,64},{81,80},{97,96},{113,112}} | collective-permute-start | bytes 786440 | tf_op jit(solution)/shard_map/ppermute | solution.py:349
  137.5 18.2 %collective-permute-start.21 = (bf16[2,128,512]{2,1,0:T(8,128)(2,1)}, bf16[2,128,512]{2,1,0:T(8,128)(2,1)S(1)}, u32[]{:S(2)}, u32[]{:S(2)}) collective-permute-start(bf16[2,128,512]{2,1,0:T(8,128)(2,1)} %get-tuple-element.83), channel_id=1, source_target_pairs={{0,15},{1,2},{2,1},{3,4},{4,3},{5,6},{6,5},{7,8},{8,7},{9,10},{10,... | collective-permute-start | bytes 786440 | tf_op jit(solution)/shard_map/ppermute | solution.py:349
